TPU v7x, 32 devices: a whole 2x2x4 slice. The times are simulated.
32 devices in a mesh: dp: 16 (over z, y, core), seq: 2 (over x).
Axes of the slice: x: 2, y: 2, z: 4, core: 2. Of those that a mesh axis runs over, the one named last changes fastest.
Arguments:
- hidden_in: bfloat16 [16, 1024, 768], P('dp', 'seq'), may hold values from -18 to 18
- segment_ids: int32 [16, 1024], P('dp'), may hold values from 0 to 7, as said below
- piece_lengths: int32 [16, 8], P('dp'), may hold values from 0 to 1024, as said below
- time_index: int32 [16, 8], P('dp'), may hold values from 0 to 999
- first_gain: float32 [768], replicated, may hold values from 0.5 to 1.5
- modulation_weight: bfloat16 [128, 4608], replicated, may hold values from -0.5 to 0.5
- modulation_bias: float32 [4608], replicated, may hold values from -4 to 4
- query_key_value_weight: bfloat16 [768, 2304], replicated, may hold values from -0.21875 to 0.21875
- attention_output_matrix: bfloat16 [768, 768], replicated, may hold values from -0.875 to 0.875
- second_gain: float32 [768], replicated, may hold values from 0.5 to 1.5
- widen_weight: bfloat16 [768, 3072], replicated, may hold values from -0.21875 to 0.21875
- expand_bias: float32 [3072], replicated, may hold values from -6 to 6
- narrow_weight: bfloat16 [3072, 768], replicated, may hold values from -0.109375 to 0.109375
- reduce_bias: float32 [768], replicated, may hold values from -6 to 6
- cotangent: bfloat16 [16, 1024, 768], P('dp', 'seq'), may hold values from -6 to 6
Outputs:
- block_out: bfloat16 [16, 1024, 768], P('dp', 'seq')
- input_grad: bfloat16 [16, 1024, 768], P('dp', 'seq')
- first_gain_grad: float32 [768], replicated
- modulation_weight_grad: float32 [128, 4608], P('seq', 'dp')
- modulation_bias_grad: float32 [4608], replicated
- triple_weight_grad: float32 [768, 2304], P('seq', 'dp')
- output_weight_grad: float32 [768, 768], P('seq', 'dp')
- second_gain_grad: float32 [768], replicated
- expand_weight_grad: float32 [768, 3072], P('seq', 'dp')
- expand_bias_grad: float32 [3072], replicated
- reduce_weight_grad: float32 [3072, 768], P('seq', 'dp')
- reduce_bias_grad: float32 [768], replicated
- masked_rms: float32 [3], replicated
Inputs may be any that keep to these rules, and one draw needn't show every extreme that they name: `segment_ids`: each slot is cut into equal pieces of 128, 512 or 1024 tokens, the kind drawn for each slot, and a token's segment id is the number of its piece, so ids start at 0 and never fall; the first slot has pieces of 128 and the last one a single piece. piece_lengths[slot, s] counts the valid leading tokens of piece s: more than half of the piece and at most all of it, the first piece of every slot all valid; 0 for numbers beyond the slot's pieces.
All inputs are finite; a program needn't handle non-finite values.
Results may differ from a plain program's by a relative error of at most 0.014.
Values may be sent and summed in bfloat16 or wider, within the bound.
A program may use at most 192 MiB of HBM per device.

v0:
```python
import math

import jax
import jax.numpy as jnp
from jax import lax
from jax.sharding import PartitionSpec as P

HEADS = 12


highest = lax.Precision.HIGHEST
negative = -1000000000.0


def layer_norm(values, scaling):
    centered = values - jnp.mean(values, axis=-1, keepdims=True)
    spread = jnp.mean(centered * centered, axis=-1, keepdims=True)
    return centered * lax.rsqrt(spread + 1e-05) * scaling


def norm_modulate(values, scaling, offset, stretch):
    return layer_norm(values, scaling) * (1.0 + stretch) + offset


def gelu_tanh(values):
    argument = 0.7978845608028654 * (values + 0.044715 * values * values * values)
    return 0.5 * values * (1.0 + jnp.tanh(argument))


def rotate(values, cosine, sine_part):
    halfway = values.shape[-1] // 2
    turned = jnp.concatenate([-values[..., halfway:], values[..., :halfway]], axis=-1)
    return values * cosine + turned * sine_part


def rotary_tables(positions, head_dim):
    freq_index = jnp.arange(head_dim // 2).astype(jnp.float32)
    frequencies = jnp.exp(freq_index * (-2.0 * math.log(10000.0) / head_dim))
    angles = positions[..., None] * frequencies
    angles = jnp.concatenate([angles, angles], axis=-1)
    return (jnp.cos(angles)[..., None, :], jnp.sin(angles)[..., None, :])


def time_embed(time_values, feature_count):
    halfway = feature_count // 2
    freq_index = jnp.arange(halfway).astype(jnp.float32)
    frequencies = jnp.exp(freq_index * (-math.log(10000.0) / halfway))
    angles = time_values.astype(jnp.float32)[..., None] * frequencies
    return jnp.concatenate([jnp.cos(angles), jnp.sin(angles)], axis=-1)


def slot_layout(segments, lengths):
    seg_range = jnp.arange(lengths.shape[-1], dtype=jnp.int32)
    membership = (segments[..., :, None] == seg_range).astype(jnp.float32)
    piece_sizes = jnp.sum(membership, axis=-2)
    piece_starts = jnp.cumsum(piece_sizes, axis=-1) - piece_sizes
    token_start = jnp.sum(membership * piece_starts[..., None, :], axis=-1)
    positions = jnp.arange(segments.shape[-1]).astype(jnp.float32) - token_start
    valid_limit = jnp.sum(membership * lengths.astype(jnp.float32)[..., None, :], axis=-1)
    validity = (positions < valid_limit).astype(jnp.float32)
    return (membership, positions, validity)


def block_order(matrix, seq_count, data_count):
    rows, cols = matrix.shape
    arranged = matrix.reshape(seq_count, rows // seq_count, data_count, cols // data_count)
    arranged = arranged.transpose(2, 0, 1, 3)
    return arranged.reshape(data_count * rows, cols // data_count)


def local(
    hidden_in,
    segment_ids,
    piece_lengths,
    time_index,
    first_gain,
    modulation_weight,
    modulation_bias,
    query_key_value_weight,
    attention_output_matrix,
    second_gain,
    widen_weight,
    expand_bias,
    narrow_weight,
    reduce_bias,
    cotangent,
):
    slot_count, own_rows, width = hidden_in.shape
    slot_rows = segment_ids.shape[1]
    head_count = HEADS
    head_dim = width // head_count
    score_scale = head_dim ** (-0.5)
    first_row = lax.axis_index("seq") * own_rows
    membership, positions, validity = slot_layout(segment_ids, piece_lengths)
    own_member = lax.dynamic_slice_in_dim(membership, first_row, own_rows, 1)
    own_pos = lax.dynamic_slice_in_dim(positions, first_row, own_rows, 1)
    own_valid = lax.dynamic_slice_in_dim(validity, first_row, own_rows, 1)
    own_segments = lax.dynamic_slice_in_dim(segment_ids, first_row, own_rows, 1)
    allowed = (own_segments[:, :, None] == segment_ids[:, None, :]) & (validity[:, None, :] > 0.5)
    condition = time_embed(time_index, modulation_weight.shape[0]).astype(jnp.bfloat16)
    modulation = (
        jnp.einsum("smc,cf->smf", condition, modulation_weight, preferred_element_type=jnp.float32)
        + modulation_bias
    )
    per_token = jnp.zeros((slot_count, own_rows, modulation.shape[-1]), jnp.float32)
    for segment in range(membership.shape[-1]):
        per_token = (
            per_token
            + own_member[:, :, segment : segment + 1] * modulation[:, segment : segment + 1, :]
        )
    shift_attn, scale_attn, gate_attn, shift_mlp, scale_mlp, gate_mlp = jnp.split(
        per_token, 6, axis=-1
    )
    residual = hidden_in.astype(jnp.float32)
    first_normed_tokens = norm_modulate(residual, first_gain, shift_attn, scale_attn).astype(
        jnp.bfloat16
    )
    triple = jnp.einsum(
        "map,pr->mar",
        first_normed_tokens,
        query_key_value_weight,
        preferred_element_type=jnp.float32,
    )
    query, key_raw, value_raw = jnp.split(triple, 3, axis=-1)
    four_dims = (slot_count, own_rows, head_count, head_dim)
    cosine, sine_part = rotary_tables(own_pos, head_dim)

    def turn(raw_values):
        return rotate(raw_values, cosine, sine_part)

    query_turned, turn_back = jax.vjp(turn, query.reshape(four_dims))
    query_rot = query_turned.astype(jnp.bfloat16)
    key_rot = (
        turn(key_raw.reshape(four_dims)).astype(jnp.bfloat16).reshape(slot_count, own_rows, width)
    )
    value_low = value_raw.astype(jnp.bfloat16)
    all_keys, all_values = (
        lax.all_gather(key_rot, "seq", axis=1, tiled=True),
        lax.all_gather(value_low, "seq", axis=1, tiled=True),
    )
    all_keys = all_keys.reshape(slot_count, slot_rows, head_count, head_dim)
    all_values = all_values.reshape(slot_count, slot_rows, head_count, head_dim)

    def attend(inputs):
        queries, keys, values, key_mask = inputs
        scores = (
            jnp.einsum("qhd,khd->hqk", queries, keys, preferred_element_type=jnp.float32)
            * score_scale
        )
        scores = jnp.where(key_mask[None], scores, negative)
        row_peak = jnp.max(scores, axis=-1, keepdims=True)
        exponent = jnp.exp(scores - row_peak)
        row_total = jnp.sum(exponent, axis=-1, keepdims=True)
        probability = exponent / row_total
        weighted = jnp.einsum(
            "hqk,khd->qhd",
            probability.astype(jnp.bfloat16),
            values,
            preferred_element_type=jnp.float32,
        )
        return (weighted, (row_peak + jnp.log(row_total))[..., 0])

    attended, log_total = lax.map(attend, (query_rot, all_keys, all_values, allowed))
    attention_result_narrow = attended.reshape(slot_count, own_rows, width).astype(jnp.bfloat16)
    projected = jnp.einsum(
        "rkn,nh->rkh",
        attention_result_narrow,
        attention_output_matrix,
        preferred_element_type=jnp.float32,
    )
    attn_branch = gate_attn * projected
    middle = residual + attn_branch
    second_normed_tokens = norm_modulate(middle, second_gain, shift_mlp, scale_mlp).astype(
        jnp.bfloat16
    )
    expanded = (
        jnp.einsum(
            "map,pr->mar", second_normed_tokens, widen_weight, preferred_element_type=jnp.float32
        )
        + expand_bias
    )
    gelu_activations = gelu_tanh(expanded).astype(jnp.bfloat16)
    reduced = (
        jnp.einsum(
            "jpb,bc->jpc", gelu_activations, narrow_weight, preferred_element_type=jnp.float32
        )
        + reduce_bias
    )
    mlp_branch = gate_mlp * reduced
    block_value = middle + mlp_branch
    block_out = block_value.astype(jnp.bfloat16)
    masked = own_valid[..., None]
    stat_terms = jnp.stack(
        [
            jnp.sum(masked * block_value * block_value),
            jnp.sum(masked * attn_branch * attn_branch),
            jnp.sum(masked * mlp_branch * mlp_branch),
            jnp.sum(own_valid),
        ]
    )
    grad_out = cotangent.astype(jnp.float32) * masked
    grad_gate_mlp = grad_out * reduced
    gradient_narrowed = (gate_mlp * grad_out).astype(jnp.bfloat16)
    reduce_weight_grad = jnp.einsum(
        "mhg,mhn->gn", gelu_activations, gradient_narrowed, preferred_element_type=jnp.float32
    )
    reduce_bias_grad = jnp.sum(gradient_narrowed.astype(jnp.float32), axis=(0, 1))
    grad_activated = jnp.einsum(
        "kav,cv->kac", gradient_narrowed, narrow_weight, preferred_element_type=jnp.float32
    )
    gradient_widened = jax.vjp(gelu_tanh, expanded)[1](grad_activated)[0].astype(jnp.bfloat16)
    expand_weight_grad = jnp.einsum(
        "cqe,cqr->er", second_normed_tokens, gradient_widened, preferred_element_type=jnp.float32
    )
    expand_bias_grad = jnp.sum(gradient_widened.astype(jnp.float32), axis=(0, 1))
    grad_normed_two = jnp.einsum(
        "yma,ja->ymj", gradient_widened, widen_weight, preferred_element_type=jnp.float32
    )
    second_back = jax.vjp(norm_modulate, middle, second_gain, shift_mlp, scale_mlp)[1]
    grad_middle_norm, second_gain_grad, grad_shift_mlp, grad_scale_mlp = second_back(
        grad_normed_two
    )
    grad_middle = grad_out + grad_middle_norm
    grad_gate_attn = grad_middle * projected
    gradient_attention_projected = (gate_attn * grad_middle).astype(jnp.bfloat16)
    output_weight_grad = jnp.einsum(
        "grm,gra->ma",
        attention_result_narrow,
        gradient_attention_projected,
        preferred_element_type=jnp.float32,
    )
    grad_attended = (
        jnp.einsum(
            "yzq,rq->yzr",
            gradient_attention_projected,
            attention_output_matrix,
            preferred_element_type=jnp.float32,
        )
        .astype(jnp.bfloat16)
        .reshape(four_dims)
    )

    def attend_back(inputs):
        queries, keys, values, key_mask, log_rows, grad_rows = inputs
        scores = (
            jnp.einsum("qhd,khd->hqk", queries, keys, preferred_element_type=jnp.float32)
            * score_scale
        )
        scores = jnp.where(key_mask[None], scores, negative)
        probability = jnp.exp(scores - log_rows[..., None])
        grad_values = jnp.einsum(
            "hqk,qhd->khd",
            probability.astype(jnp.bfloat16),
            grad_rows,
            preferred_element_type=jnp.float32,
        )
        grad_prob = jnp.einsum(
            "qhd,khd->hqk", grad_rows, values, preferred_element_type=jnp.float32
        )
        row_delta = jnp.sum(grad_prob * probability, axis=-1, keepdims=True)
        grad_scores = (probability * (grad_prob - row_delta)).astype(jnp.bfloat16)
        grad_queries = (
            jnp.einsum("hqk,khd->qhd", grad_scores, keys, preferred_element_type=jnp.float32)
            * score_scale
        )
        grad_keys = (
            jnp.einsum("hqk,qhd->khd", grad_scores, queries, preferred_element_type=jnp.float32)
            * score_scale
        )
        return (
            grad_queries,
            grad_keys.reshape(slot_rows, width),
            grad_values.reshape(slot_rows, width),
        )

    grad_query_rot, grad_key_part, grad_value_part = lax.map(
        attend_back, (query_rot, all_keys, all_values, allowed, log_total, grad_attended)
    )
    grad_key_rot, grad_value = (
        lax.psum_scatter(
            grad_key_part.astype(jnp.bfloat16), "seq", scatter_dimension=1, tiled=True
        ).astype(jnp.float32),
        lax.psum_scatter(
            grad_value_part.astype(jnp.bfloat16), "seq", scatter_dimension=1, tiled=True
        ).astype(jnp.float32),
    )
    grad_query = turn_back(grad_query_rot)[0].reshape(slot_count, own_rows, width)
    grad_key = turn_back(grad_key_rot.reshape(four_dims))[0].reshape(slot_count, own_rows, width)
    gradient_query_key_value = jnp.concatenate([grad_query, grad_key, grad_value], axis=-1).astype(
        jnp.bfloat16
    )
    triple_weight_grad = jnp.einsum(
        "cqe,cqr->er",
        first_normed_tokens,
        gradient_query_key_value,
        preferred_element_type=jnp.float32,
    )
    grad_normed_one = jnp.einsum(
        "yma,ja->ymj",
        gradient_query_key_value,
        query_key_value_weight,
        preferred_element_type=jnp.float32,
    )
    first_back = jax.vjp(norm_modulate, residual, first_gain, shift_attn, scale_attn)[1]
    grad_residual, first_gain_grad, grad_shift_attn, grad_scale_attn = first_back(grad_normed_one)
    input_grad = (grad_middle + grad_residual).astype(jnp.bfloat16)
    grad_tokens = jnp.concatenate(
        [
            grad_shift_attn,
            grad_scale_attn,
            grad_gate_attn,
            grad_shift_mlp,
            grad_scale_mlp,
            grad_gate_mlp,
        ],
        axis=-1,
    )
    grad_modulation = jnp.einsum(
        "slm,slf->smf",
        own_member,
        grad_tokens,
        precision=highest,
        preferred_element_type=jnp.float32,
    )
    modulation_weight_grad = jnp.einsum(
        "smc,smf->cf",
        condition.astype(jnp.float32),
        grad_modulation,
        precision=highest,
        preferred_element_type=jnp.float32,
    )
    modulation_bias_grad = jnp.sum(grad_modulation, axis=(0, 1))
    vectors = [
        first_gain_grad,
        modulation_bias_grad,
        second_gain_grad,
        expand_bias_grad,
        reduce_bias_grad,
        stat_terms,
    ]
    flat_small = jnp.concatenate(vectors)
    summed_small = lax.psum(flat_small, ("dp", "seq"))
    small_results = []
    cursor = 0
    for vector in vectors:
        small_results.append(summed_small[cursor : cursor + vector.shape[0]])
        cursor = cursor + vector.shape[0]
    seq_count = lax.axis_size("seq")
    data_count = lax.axis_size("dp")
    matrix_parts = (
        lax.psum_scatter(
            block_order(modulation_weight_grad, seq_count, data_count),
            ("dp", "seq"),
            scatter_dimension=0,
            tiled=True,
        ),
        lax.psum_scatter(
            block_order(triple_weight_grad, seq_count, data_count),
            ("dp", "seq"),
            scatter_dimension=0,
            tiled=True,
        ),
        lax.psum_scatter(
            block_order(output_weight_grad, seq_count, data_count),
            ("dp", "seq"),
            scatter_dimension=0,
            tiled=True,
        ),
        lax.psum_scatter(
            block_order(expand_weight_grad, seq_count, data_count),
            ("dp", "seq"),
            scatter_dimension=0,
            tiled=True,
        ),
        lax.psum_scatter(
            block_order(reduce_weight_grad, seq_count, data_count),
            ("dp", "seq"),
            scatter_dimension=0,
            tiled=True,
        ),
    )
    totals = small_results[5]
    masked_rms = jnp.sqrt(totals[:3] / (totals[3] * width))
    return (
        block_out,
        input_grad,
        small_results[0],
        matrix_parts[0],
        small_results[1],
        matrix_parts[1],
        matrix_parts[2],
        small_results[2],
        matrix_parts[3],
        small_results[3],
        matrix_parts[4],
        small_results[4],
        masked_rms,
    )


def solution(mesh):
    in_specs = (
        P("dp", "seq", None),
        P("dp", None),
        P("dp", None),
        P("dp", None),
        P(),
        P(),
        P(),
        P(),
        P(),
        P(),
        P(),
        P(),
        P(),
        P(),
        P("dp", "seq", None),
    )
    out_specs = (
        P("dp", "seq", None),
        P("dp", "seq", None),
        P(),
        P("seq", "dp"),
        P(),
        P("seq", "dp"),
        P("seq", "dp"),
        P(),
        P("seq", "dp"),
        P(),
        P("seq", "dp"),
        P(),
        P(),
    )
    return jax.shard_map(local, mesh=mesh, in_specs=in_specs, out_specs=out_specs, check_vma=False)
```

profile of v0, /device:TPU:0, one launch (start us, length us, event | category | flops | bytes accessed | tf_op | source)
XLA Modules:
  0.0 905.2 jit_solution(2485126166303341673)
XLA Ops:
  26.8 3.1 copy.74
  32.1 3.0 copy.71
  36.2 6.6 multiply_add_fusion.2
  50.2 3.0 copy.72
  56.2 3.0 copy.73
  59.2 5.1 add_convert_fusion.1
  64.3 2.4 split.98
  68.5 3.1 copy.69
  75.8 18.5 %all-gather.5.cloned.1.call-done = bf16[1,1024,768]{2,1,0:T(8,128)(2,1)} async-done(((bf16[1,512,768]{2,1,0:T(8,128)(2,1)}), bf16[1,1024,768]{2,1,0:T(8,128)(2,1)}) %all-gather.5.cloned.1.call-update) | async-done | bytes 1572880 | tf_op jit(solution)/shard_map/all_gather | solution.py:138
  94.4 2.7 copy.75
  97.0 14.8 %fusion.8 = (f32[12,512]{1,0:T(8,128)S(1)}, f32[12,512,1024]{2,1,0:T(8,128)}) fusion(pred[512,1024]{1,0:T(8,128)(4,1)} %compare_and_fusion, bf16[512,12,64]{0,2,1:T(8,128)(2,1)} %fusion.57, bf16[1024,12,64]{0,2,1:T(8,128)(2,1)} %bitcast.275), kind=kOutput, calls=%fused_computation.20 | convolution fusion | flops 824174592 | bytes 28073984 | tf_op jit(solution)/shard_map/while/body/eval_jaxpr/qhd,khd->hqk/dot_general | solution.py:147
  111.8 11.8 %fusion = f32[12,512]{1,0:T(8,128)S(1)} fusion(f32[12,512]{1,0:T(8,128)S(1)} %get-tuple-element.132, f32[12,512,1024]{2,1,0:T(8,128)} %get-tuple-element.133, pred[512,1024]{1,0:T(8,128)(4,1)S(1)} %copy-done.15), kind=kLoop, calls=%fused_computation.6 | loop fusion | flops 25159680 | bytes 25739264 | tf_op jit(solution)/shard_map/while/body/eval_jaxpr/reduce_sum | solution.py:153
  124.9 2.6 copy.68
  127.5 13.1 %fusion.64 = bf16[12,64,512]{2,1,0:T(8,128)(2,1)S(1)} fusion(bf16[1024,12,64]{0,2,1:T(8,128)(2,1)} %bitcast.280, f32[12,512]{1,0:T(8,128)} %copy-done.39, f32[12,512]{1,0:T(8,128)} %copy-done.38, f32[12,512,1024]{2,1,0:T(8,128)} %get-tuple-element.133, pred[512,1024]{1,0:T(8,128)(4,1)} %compare_and_fusion), kind=kOutput, calls=%fused_computation.130 | convolution fusion | flops 837156864 | bytes 28098560 | tf_op jit(solution)/shard_map/while/body/eval_jaxpr/hqk,khd->qhd/dot_general | solution.py:155
  140.7 2.7 fusion.102
  145.1 2.6 fusion.69
  147.9 5.1 fusion.30
  153.1 11.9 %convert_reduce_fusion = (f32[3072]{0:T(1024)}, bf16[512,3072]{1,0:T(8,128)(2,1)}, f32[512,3072]{1,0:T(8,128)}) fusion(f32[512,3072]{1,0:T(8,128)S(1)} %fusion.69, f32[3072]{0:T(1024)S(1)} %copy-done.59, bf16[3072,768]{1,0:T(8,128)(2,1)} %param.27, bf16[1,512,768]{2,1,0:T(8,128)(2,1)S(1)} %get-tuple-element.85), kind=kOutput, calls=%fused_computation.46 | convolution fusion | flops 2458383360 | bytes 21258240 | tf_op jit(solution)/shard_map/kav,cv->kac/dot_general | solution.py:208
  165.0 7.6 multiply_reduce_fusion.1
  179.8 18.8 %multiply_reduce_fusion = (f32[12,512]{1,0:T(8,128)}, f32[12,512,1024]{2,1,0:T(8,128)}) fusion(f32[12,512]{1,0:T(8,128)} %log_add_fusion, f32[12,512,1024]{2,1,0:T(8,128)} %get-tuple-element.133, pred[512,1024]{1,0:T(8,128)(4,1)} %compare_and_fusion, bf16[512,12,64]{0,2,1:T(8,128)(2,1)} %bitcast.302, bf16[1024,12,64]{0,2,1:T(8,128)(2,1)} %bitcast.281), kind=kOutput, calls=%fused_computation.1 | convolution fusion | flops 836757504 | bytes 53264384 | tf_op jit(solution)/shard_map/while/body/eval_jaxpr/qhd,khd->hqk/dot_general | solution.py:257
  198.6 17.8 %multiply_convert_fusion = bf16[12,512,1024]{2,1,0:T(8,128)(2,1)S(1)} fusion(f32[12,512,1024]{2,1,0:T(8,128)} %get-tuple-element.138, f32[12,512]{1,0:T(8,128)} %get-tuple-element.137, f32[12,512]{1,0:T(8,128)} %log_add_fusion, f32[12,512,1024]{2,1,0:T(8,128)} %get-tuple-element.133, pred[512,1024]{1,0:T(8,128)(4,1)} %compare_and_fusion), kind=kLoop, calls=%fused_computation | loop fusion | flops 37748736 | bytes 63488000 | tf_op jit(solution)/shard_map/while/body/eval_jaxpr/convert_element_type | solution.py:261
  216.4 4.1 multiply_convert_fusion.2
  221.6 13.7 %fusion.38 = bf16[12,64,1024]{2,1,0:T(8,128)(2,1)} fusion(bf16[512,12,64]{0,2,1:T(8,128)(2,1)} %bitcast.303, f32[12,512]{1,0:T(8,128)} %log_add_fusion, f32[12,512,1024]{2,1,0:T(8,128)} %get-tuple-element.133, pred[512,1024]{1,0:T(8,128)(4,1)} %compare_and_fusion), kind=kOutput, calls=%fused_computation.77 | convolution fusion | flops 831258624 | bytes 28073984 | tf_op jit(solution)/shard_map/while/body/eval_jaxpr/hqk,qhd->khd/dot_general | solution.py:251
  242.5 3.3 copy.83
  245.8 4.3 reshape.1485
  250.1 9.0 fusion.107
  262.0 3.2 fusion.59
  267.9 8.4 reduce-scatter.10.cloned.1.call-done
  276.3 3.7 bitcast_dynamic-update-slice_fusion
  289.9 4.4 fusion.106
  302.6 10.8 %multiply_convert_fusion.1 = (bf16[3072,512]{0,1:T(8,128)(2,1)}, bf16[3072,512]{0,1:T(8,128)(2,1)}) fusion(f32[512,3072]{1,0:T(8,128)} %copy-done.8, f32[3072]{0:T(1024)S(1)} %copy-done.60, f32[512,3072]{1,0:T(8,128)} %get-tuple-element.135), kind=kLoop, calls=%fused_computation.45 | loop fusion | flops 42467328 | bytes 18886656 | tf_op jit(solution)/shard_map/convert_element_type | solution.py:182
  313.4 4.8 copy.84
  318.1 4.8 convolution_bitcast_fusion.2
  323.0 12.7 %copy.86 = f32[16,2,384,192]{2,1,0,3:T(2,128)} copy(f32[16,2,384,192]{2,3,0,1:T(8,128)S(1)} %convolution_bitcast_fusion.2) | data formatting | bytes 18874368 | tf_op jit(solution)/shard_map/transpose | solution.py:67
  335.7 12.5 %reshape.1486 = f32[12288,192]{0,1:T(8,128)} reshape(f32[16,2,384,192]{2,1,0,3:T(2,128)} %copy.86) | data formatting | bytes 18874368 | tf_op jit(solution)/shard_map/reshape | solution.py:68
  350.6 5.1 copy.99
  355.8 4.7 convolution_bitcast_fusion
  360.5 11.1 %copy.89 = f32[16,2,1536,48]{2,1,0,3:T(2,128)} copy(f32[16,2,1536,48]{2,3,0,1:T(8,128)S(1)} %convolution_bitcast_fusion) | data formatting | bytes 18874368 | tf_op jit(solution)/shard_map/transpose | solution.py:67
  371.6 12.2 %reshape.1487 = f32[49152,48]{0,1:T(8,128)} reshape(f32[16,2,1536,48]{2,1,0,3:T(2,128)} %copy.89) | data formatting | bytes 18874368 | tf_op jit(solution)/shard_map/reshape | solution.py:68
  388.1 4.4 convolution_bitcast_fusion.3
  392.5 11.4 %copy.81 = f32[16,2,384,144]{2,1,0,3:T(2,128)} copy(f32[16,2,384,144]{2,3,0,1:T(8,128)} %convolution_bitcast_fusion.3) | data formatting | bytes 14155776 | tf_op jit(solution)/shard_map/transpose | solution.py:67
  403.9 9.8 %reshape.1484 = f32[12288,144]{0,1:T(8,128)} reshape(f32[16,2,384,144]{2,1,0,3:T(2,128)} %copy.81) | data formatting | bytes 14155776 | tf_op jit(solution)/shard_map/reshape | solution.py:68
  414.5 3.9 concatenate.72
  418.4 40.4 %psum.7 = f32[9988]{0:T(1024)} all-reduce(f32[9988]{0:T(1024)} %concatenate.72), channel_id=1, replica_groups=mesh['dp'=16,'seq'=2] {'dp','seq'}, use_global_device_ids=true, to_apply=%region_26.27 | all-reduce | flops 9988 | bytes 79904 | tf_op jit(solution)/shard_map/psum | solution.py:342
  465.8 22.5 %reduce-scatter.12.cloned.1.call-done = f32[64,288]{1,0:T(8,128)} async-done(((f32[2048,288]{1,0:T(8,128)}), f32[64,288]{1,0:T(8,128)}) %reduce-scatter.12.cloned.1.call-update) | async-done | bytes 73744 | tf_op jit(solution)/shard_map/reduce_scatter | solution.py:351
  488.3 142.1 %reduce-scatter.18.cloned.1.call-done = f32[384,192]{0,1:T(8,128)} async-done(((f32[12288,192]{0,1:T(8,128)}), f32[384,192]{0,1:T(8,128)}) %reduce-scatter.18.cloned.1.call-update) | async-done | bytes 294928 | tf_op jit(solution)/shard_map/reduce_scatter | solution.py:369
  630.4 142.5 %reduce-scatter.20.cloned.1.call-done = f32[1536,48]{0,1:T(8,128)} async-done(((f32[49152,48]{0,1:T(8,128)}), f32[1536,48]{0,1:T(8,128)}) %reduce-scatter.20.cloned.1.call-update) | async-done | bytes 294928 | tf_op jit(solution)/shard_map/reduce_scatter | solution.py:375
  772.9 125.5 %reduce-scatter.14.cloned.1.call-done = f32[384,144]{0,1:T(8,128)} async-done(((f32[12288,144]{0,1:T(8,128)}), f32[384,144]{0,1:T(8,128)}) %reduce-scatter.14.cloned.1.call-update) | async-done | bytes 221200 | tf_op jit(solution)/shard_map/reduce_scatter | solution.py:357
  (243 shorter events, 95.1 us)
Async XLA Ops:
  7.2 36.2 %copy-start = (bf16[768,2304]{1,0:T(8,128)(2,1)S(1)}, bf16[768,2304]{1,0:T(8,128)(2,1)}, u32[]{:S(2)}) copy-start(bf16[768,2304]{1,0:T(8,128)(2,1)} %param.22) | copy-start | bytes 10616836
  7.2 87.2 %all-gather.5.cloned.1.call-start = ((), (), s32[]{:S(2)}) async-start(), calls=%async_computation.8 | async-start | bytes 2359296 | tf_op jit(solution)/shard_map/all_gather | solution.py:138
  11.4 31.4 %copy-start.41 = (f32[512]{0:T(512)}, f32[512]{0:T(512)S(1)}, u32[]{:S(2)}) copy-start(f32[512]{0:T(512)S(1)} %broadcast_multiply_fusion.4) | copy-start | bytes 6148
  13.5 29.3 %copy-start.45 = (f32[512]{0:T(512)}, f32[512]{0:T(512)S(1)}, u32[]{:S(2)}) copy-start(f32[512]{0:T(512)S(1)} %fusion.84) | copy-start | bytes 6148
  18.6 3.2 copy-start.51
  36.2 6.6 copy-start.5
  36.2 6.6 copy-start.43
  42.9 3.6 copy-start.2
  43.4 3.3 copy-start.23
  64.3 3.6 copy-start.48
  64.3 60.6 %all-gather.3.cloned.1.call-start = ((), (), s32[]{:S(2)}) async-start(), calls=%async_computation.7 | async-start | bytes 2359296 | tf_op jit(solution)/shard_map/all_gather | solution.py:139
  66.7 198.4 %reduce-scatter.8.cloned.1.call-start = ((), (), s32[]{:S(2)}) async-start(), calls=%async_computation.9 | async-start | bytes 2359296 | tf_op jit(solution)/shard_map/reduce_scatter | solution.py:280
  68.5 4.8 copy-start.61
  68.5 4.8 copy-start.62
  97.0 14.8 %copy-start.15 = (pred[512,1024]{1,0:T(8,128)(4,1)S(1)}, pred[512,1024]{1,0:T(8,128)(4,1)}, u32[]{:S(2)}) copy-start(pred[512,1024]{1,0:T(8,128)(4,1)} %compare_and_fusion) | copy-start | bytes 1572868
  111.8 11.8 %copy-start.38 = (f32[12,512]{1,0:T(8,128)}, f32[12,512]{1,0:T(8,128)S(1)}, u32[]{:S(2)}) copy-start(f32[12,512]{1,0:T(8,128)S(1)} %get-tuple-element.132) | copy-start | bytes 73732
  127.5 16.2 %slice-start = ((s8[9437184]{0:T(1024)(128)(4,1)}), s8[4194304]{0:T(1024)(128)(4,1)S(1)}, s32[]{:S(2)}) async-start(s8[9437184]{0:T(1024)(128)(4,1)} %bitcast.271), calls=%async_computation.16 | async-start | bytes 8388608
  127.5 13.2 %copy-start.6 = (bf16[1,512,768]{2,1,0:T(8,128)(2,1)S(1)}, bf16[1,512,768]{2,1,0:T(8,128)(2,1)}, u32[]{:S(2)}) copy-start(bf16[1,512,768]{2,1,0:T(8,128)(2,1)} %param.15) | copy-start | bytes 2359300
  127.5 13.2 %copy-start.34 = (bf16[768,768]{1,0:T(8,128)(2,1)S(1)}, bf16[768,768]{1,0:T(8,128)(2,1)}, u32[]{:S(2)}) copy-start(bf16[768,768]{1,0:T(8,128)(2,1)} %param.23) | copy-start | bytes 3538948
  127.5 16.3 %slice-start.1 = ((s8[9437184]{0:T(1024)(128)(4,1)}), s8[4194304]{0:T(1024)(128)(4,1)S(1)}, s32[]{:S(2)}) async-start(s8[9437184]{0:T(1024)(128)(4,1)} %bitcast.271), calls=%async_computation.17 | async-start | bytes 8388608
  127.5 16.3 %slice-start.2 = ((s8[9437184]{0:T(1024)(128)(4,1)}), s8[1048576]{0:T(1024)(128)(4,1)S(1)}, s32[]{:S(2)}) async-start(s8[9437184]{0:T(1024)(128)(4,1)} %bitcast.271), calls=%async_computation.18 | async-start | bytes 2097152
  140.7 3.1 copy-start.16
  140.7 3.1 copy-start.47
  140.7 4.4 slice-start.3
  143.4 21.6 %copy-start.21 = (f32[512,768]{1,0:T(8,128)}, f32[512,768]{1,0:T(8,128)S(1)}, u32[]{:S(2)}) copy-start(f32[512,768]{1,0:T(8,128)S(1)} %get-tuple-element.134) | copy-start | bytes 4718596
  143.4 29.1 %copy-start.3 = (f32[1,512,768]{2,1,0:T(8,128)}, f32[1,512,768]{2,1,0:T(8,128)S(1)}, u32[]{:S(2)}) copy-start(f32[1,512,768]{2,1,0:T(8,128)S(1)} %get-tuple-element.94) | copy-start | bytes 4718596
  143.8 4.0 slice-start.5
  145.1 8.0 copy-start.24
  147.9 5.1 copy-start.8
  153.1 11.9 %copy-start.64 = (f32[768]{0:T(1024)S(1)}, f32[768]{0:T(1024)}, u32[]{:S(2)}) copy-start(f32[768]{0:T(1024)} %param.28) | copy-start | bytes 9220
  198.6 17.8 %copy-start.18 = (bf16[512,12,64]{0,2,1:T(8,128)(2,1)S(1)}, bf16[512,12,64]{0,2,1:T(8,128)(2,1)}, u32[]{:S(2)}) copy-start(bf16[512,12,64]{0,2,1:T(8,128)(2,1)} %fusion.57) | copy-start | bytes 2359300
  216.4 5.1 copy-start.1
  221.5 54.8 %reduce-scatter.10.cloned.1.call-start = ((), (), s32[]{:S(2)}) async-start(), calls=%async_computation.10 | async-start | bytes 2359296 | tf_op jit(solution)/shard_map/reduce_scatter | solution.py:283
  235.3 230.5 %reduce-scatter.16.cloned.1.call-start = ((), (), s32[]{:S(2)}) async-start(), calls=%async_computation.13 | async-start | bytes 2433024 | tf_op jit(solution)/shard_map/reduce_scatter | solution.py:363
  250.1 10.3 %copy-start.37 = (f32[512,64]{0,1:T(8,128)S(1)}, f32[512,64]{0,1:T(8,128)}, u32[]{:S(2)}) copy-start(f32[512,64]{0,1:T(8,128)} %get-tuple-element.114) | copy-start | bytes 393220
  261.9 226.4 %reduce-scatter.12.cloned.1.call-start = ((), (), s32[]{:S(2)}) async-start(), calls=%async_computation.11 | async-start | bytes 3244032 | tf_op jit(solution)/shard_map/reduce_scatter | solution.py:351
  276.3 3.7 copy-start.7
  276.3 3.7 copy-start.42
  276.3 3.8 copy-start.44
  276.3 3.8 copy-start.46
  280.1 3.8 copy-start.13
  280.1 3.8 copy-start.17
  280.1 3.8 copy-start.22
  280.1 3.8 copy-start.55
  289.9 6.1 copy-start.58
  300.2 330.2 %reduce-scatter.18.cloned.1.call-start = ((), (), s32[]{:S(2)}) async-start(), calls=%async_computation.14 | async-start | bytes 9732096 | tf_op jit(solution)/shard_map/reduce_scatter | solution.py:369
  348.3 424.7 %reduce-scatter.20.cloned.1.call-start = ((), (), s32[]{:S(2)}) async-start(), calls=%async_computation.15 | async-start | bytes 9732096 | tf_op jit(solution)/shard_map/reduce_scatter | solution.py:375
  383.9 514.6 %reduce-scatter.14.cloned.1.call-start = ((), (), s32[]{:S(2)}) async-start(), calls=%async_computation.12 | async-start | bytes 7299072 | tf_op jit(solution)/shard_map/reduce_scatter | solution.py:357
  (34 other events, 58.1 us)
Sparse Core Ops, SparseCore 0:
  64.4 29.8 all-gather.4
  96.5 27.2 all-gather.2
  221.6 26.3 reduce-scatter.7
  250.2 26.0 reduce-scatter.9
  282.0 99.0 reduce-scatter.15
  387.9 100.3 reduce-scatter.11
  495.8 134.5 reduce-scatter.17
  636.9 136.0 reduce-scatter.19
  780.2 118.2 reduce-scatter.13
where the time goes:
time: 914 us; the launch traced here: 905 us
  waiting for transfers between devices  460 us (50%)
  local copies, waits for them, and re-layouts  157 us (17%)
  matrix products  135 us (15%)
  other arithmetic  96.4 us (11%)
  blocking collectives  40.4 us (4%)
  between operations  15.4 us (2%)
    reduce_scatter x1, waiting for transfers between devices, local(): lax.psum_scatter(block_order(reduce_weight_grad, seq_count, data_count),...  143 us
    reduce_scatter x1, waiting for transfers between devices, local(): lax.psum_scatter(block_order(expand_weight_grad, seq_count, data_count),...  142 us
    reduce_scatter x1, waiting for transfers between devices, local(): lax.psum_scatter(block_order(triple_weight_grad, seq_count, data_count),...  126 us
    transpose x5, local copies, waits for them, and re-layouts, block_order(): arranged = arranged.transpose(2, 0, 1, 3)  40.4 us
    psum x1, blocking collectives, local(): summed_small = lax.psum(flat_small, ('dp', 'seq'))  40.4 us
    reshape x4, local copies, waits for them, and re-layouts, block_order(): return arranged.reshape(data_count * rows, cols // data_count)  38.9 us
    reduce_scatter x1, waiting for transfers between devices, local(): lax.psum_scatter(block_order(modulation_weight_grad, seq_count, data_coun...  22.5 us
    dot_general x1, matrix products, attend_back(): jnp.einsum('qhd,khd->hqk', grad_rows, values, preferred_element_type=jnp....  18.8 us
  transfers between devices with their start and end apart: 9, of which 6 were waited for; matrix products, arithmetic and copies ran while one was open for 25% of the time, Pallas kernels for 0%

commit v1 on v0

--- a/solution.py
+++ b/solution.py
@@ -3,6 +3,8 @@
 import jax
 import jax.numpy as jnp
 from jax import lax
+from jax.experimental import pallas as pl
+from jax.experimental.pallas import tpu as pltpu
 from jax.sharding import PartitionSpec as P
 
 HEADS = 12
@@ -61,11 +63,187 @@
     return (membership, positions, validity)
 
 
-def block_order(matrix, seq_count, data_count):
-    rows, cols = matrix.shape
-    arranged = matrix.reshape(seq_count, rows // seq_count, data_count, cols // data_count)
-    arranged = arranged.transpose(2, 0, 1, 3)
-    return arranged.reshape(data_count * rows, cols // data_count)
+LANES = 384
+GROUP_BITS = 4
+MESH_ID = pl.DeviceIdType.MESH
+Z2, Z1, Y, CORE, X = 0, 1, 2, 3, 4
+
+
+def exchange_partner(axis, extra_bits):
+    dp, seq = lax.axis_index("dp"), lax.axis_index("seq")
+    if axis == X:
+        return (dp, 1 - seq)
+    return (dp ^ (1 << (GROUP_BITS - 1 - axis + extra_bits)), seq)
+
+
+def own_bit(axis, extra_bits):
+    if axis == X:
+        return lax.axis_index("seq")
+    return (lax.axis_index("dp") >> (GROUP_BITS - 1 - axis + extra_bits)) & 1
+
+
+def reduce_tasks(rows):
+    streams = (
+        (0, 112, (CORE, X, Y, Z1, Z2)),
+        (224, 112, (CORE, Y, Z1, X, Z2)),
+        (448, 96, (CORE, Z1, X, Y, Z2)),
+        (112, 112, (CORE, X, Y, Z1, Z2)),
+        (336, 112, (CORE, Y, Z1, X, Z2)),
+        (544, 80, (CORE, Z1, X, Y, Z2)),
+    )
+    return streams
+
+
+def reduce_kernel(extra_bits, all_bits, parts_ref, small_ref, sum_ref, small_out, acc, got_a, got_b, got_c, got_d, got_e, small_acc, small_got, local_sem, send_sem, recv_sem, small_send, small_recv):
+    tasks = reduce_tasks(parts_ref.shape[-2])
+    got = (got_a, got_b, got_c, got_d, got_e)
+    bits = [own_bit(axis, extra_bits) for axis in range(5)]
+    small_partners = [(lax.axis_index("dp"), 1 - lax.axis_index("seq"))] + [
+        (lax.axis_index("dp") ^ (1 << bit), lax.axis_index("seq")) for bit in range(all_bits)
+    ]
+    barrier = pltpu.get_barrier_semaphore()
+    for partner in small_partners:
+        pl.semaphore_signal(barrier, inc=1, device_id=partner, device_id_type=MESH_ID)
+    pl.semaphore_wait(barrier, len(small_partners))
+
+    def region(order, stage, other):
+        index = [slice(None)] * 5
+        for axis in order[:stage]:
+            index[axis] = bits[axis]
+        index[order[stage]] = 1 - bits[order[stage]] if other else bits[order[stage]]
+        return index
+
+    copies = {}
+    local_copies = []
+    for number, (first, count, order) in enumerate(tasks):
+        keep = pltpu.make_async_copy(
+            parts_ref.at[tuple(region(order, 0, False)) + (pl.ds(first, count),)],
+            acc.at[:, :, :, :, pl.ds(first, count)],
+            local_sem.at[number],
+        )
+        keep.start()
+        local_copies.append(keep)
+
+    def send(number, stage):
+        first, count, order = tasks[number]
+        index = region(order, stage, True)
+        if stage == 0:
+            source = parts_ref.at[tuple(index) + (pl.ds(first, count),)]
+        else:
+            del index[CORE]
+            source = acc.at[tuple(index) + (pl.ds(first, count),)]
+        target = got[stage].at[(slice(None),) * (4 - stage) + (pl.ds(first, count),)]
+        copy = pltpu.make_async_remote_copy(
+            source, target, send_sem.at[number, stage], recv_sem.at[number, stage],
+            device_id=exchange_partner(order[stage], extra_bits), device_id_type=MESH_ID,
+        )
+        copy.start()
+        copies[number, stage] = copy
+
+    def add(number, stage):
+        first, count, order = tasks[number]
+        copies[number, stage].wait_recv()
+        if stage == 0:
+            local_copies[number].wait()
+        free = [axis for axis in range(5) if axis not in order[: stage + 1]]
+
+        def one(step, carry):
+            index = list(bits)
+            got_index = []
+            for place, axis in enumerate(free):
+                index[axis] = (step >> (len(free) - 1 - place)) & 1
+                got_index.append(index[axis])
+            del index[CORE]
+            rows = pl.ds(first, count)
+            mine = acc[tuple(index) + (rows,)].astype(jnp.float32)
+            total = mine + got[stage][tuple(got_index) + (rows,)].astype(jnp.float32)
+            if stage == 4:
+                sum_ref[rows] = total
+            else:
+                acc[tuple(index) + (rows,)] = total.astype(jnp.bfloat16)
+            return carry
+
+        if free:
+            lax.fori_loop(0, 2 ** len(free), one, 0)
+        else:
+            one(0, 0)
+
+    small_copies = []
+
+    def small_send_step(step):
+        copy = pltpu.make_async_remote_copy(
+            small_acc.at[step], small_got.at[step], small_send.at[step], small_recv.at[step],
+            device_id=small_partners[step], device_id_type=MESH_ID,
+        )
+        copy.start()
+        small_copies.append(copy)
+
+    def small_add(step):
+        small_copies[step].wait_recv()
+        small_acc[step + 1] = small_acc[step] + small_got[step]
+
+    small_acc[0] = small_ref[...]
+    for number in range(len(tasks)):
+        send(number, 0)
+    small_send_step(0)
+    for stage in range(1, 5):
+        for number in range(len(tasks)):
+            add(number, stage - 1)
+            send(number, stage)
+        small_add(stage - 1)
+        small_send_step(stage)
+    for number in range(len(tasks)):
+        add(number, 4)
+    for step in range(4, len(small_partners)):
+        small_add(step)
+        if step + 1 < len(small_partners):
+            small_send_step(step + 1)
+    small_out[...] = small_acc[len(small_partners)]
+    for copy in copies.values():
+        copy.wait_send()
+    for copy in small_copies:
+        copy.wait_send()
+
+
+def reduce_everywhere(parts, small):
+    dp_size = lax.axis_size("dp")
+    all_bits = dp_size.bit_length() - 1
+    extra_bits = all_bits - GROUP_BITS
+    rows = parts.shape[2]
+    parts = parts.reshape((2,) * 5 + parts.shape[2:])
+    task_count = len(reduce_tasks(rows))
+    steps = all_bits + 1
+    bf16 = jnp.bfloat16
+    got_shapes = [pltpu.VMEM((2,) * (4 - stage) + (rows, LANES), bf16) for stage in range(5)]
+    return pl.pallas_call(
+        lambda *refs: reduce_kernel(extra_bits, all_bits, *refs),
+        out_shape=(
+            jax.ShapeDtypeStruct((rows, LANES), jnp.float32),
+            jax.ShapeDtypeStruct(small.shape, jnp.float32),
+        ),
+        in_specs=[pl.BlockSpec(memory_space=pl.ANY), pl.BlockSpec(memory_space=pltpu.VMEM)],
+        out_specs=(pl.BlockSpec(memory_space=pltpu.VMEM), pl.BlockSpec(memory_space=pltpu.VMEM)),
+        scratch_shapes=[pltpu.VMEM((2, 2, 2, 2, rows, LANES), bf16)] + got_shapes + [
+            pltpu.VMEM((steps + 1,) + small.shape, jnp.float32),
+            pltpu.VMEM((steps,) + small.shape, jnp.float32),
+            pltpu.SemaphoreType.DMA((task_count,)),
+            pltpu.SemaphoreType.DMA((task_count, 5)),
+            pltpu.SemaphoreType.DMA((task_count, 5)),
+            pltpu.SemaphoreType.DMA((steps,)),
+            pltpu.SemaphoreType.DMA((steps,)),
+        ],
+        compiler_params=pltpu.CompilerParams(
+            collective_id=0, has_side_effects=True, vmem_limit_bytes=48 << 20
+        ),
+    )(parts, small)
+
+
+def scatter_rest(block, dp_size):
+    group = dp_size >> GROUP_BITS
+    if group == 1:
+        return block
+    groups = [[first * group + place for place in range(group)] for first in range(dp_size // group)]
+    return lax.psum_scatter(block, "dp", scatter_dimension=0, axis_index_groups=groups, tiled=True)
 
 
 def local(
@@ -339,46 +517,39 @@
         stat_terms,
     ]
     flat_small = jnp.concatenate(vectors)
-    summed_small = lax.psum(flat_small, ("dp", "seq"))
+    small_rows = -(-flat_small.shape[0] // 1024) * 8
+    flat_small = jnp.pad(flat_small, (0, small_rows * 128 - flat_small.shape[0]))
+    groups = 2**GROUP_BITS
+    bf16 = jnp.bfloat16
+    expand_part = expand_weight_grad.T.astype(bf16).reshape(groups, -1, 2, LANES).transpose(0, 2, 1, 3)
+    reduce_part = reduce_weight_grad.T.astype(bf16).reshape(groups, -1, 2, 4, LANES)
+    reduce_part = reduce_part.transpose(0, 2, 3, 1, 4).reshape(groups, 2, -1, LANES)
+    output_part = output_weight_grad.T.astype(bf16).reshape(groups, -1, 2, LANES).transpose(0, 2, 1, 3)
+    triple_part = triple_weight_grad.T.astype(bf16).reshape(groups, -1, 2, LANES).transpose(0, 2, 1, 3)
+    mod_part = modulation_weight_grad.T.astype(bf16).reshape(groups, 6, -1, 2, LANES // 6)
+    mod_part = mod_part.transpose(0, 3, 2, 1, 4).reshape(groups, 2, -1, LANES)
+    parts = jnp.concatenate([expand_part, reduce_part, output_part, triple_part, mod_part], axis=2)
+    block_sum, summed_small = reduce_everywhere(parts, flat_small.reshape(small_rows, 128))
+    summed_small = summed_small.reshape(-1)
     small_results = []
     cursor = 0
     for vector in vectors:
         small_results.append(summed_small[cursor : cursor + vector.shape[0]])
         cursor = cursor + vector.shape[0]
-    seq_count = lax.axis_size("seq")
-    data_count = lax.axis_size("dp")
-    matrix_parts = (
-        lax.psum_scatter(
-            block_order(modulation_weight_grad, seq_count, data_count),
-            ("dp", "seq"),
-            scatter_dimension=0,
-            tiled=True,
-        ),
-        lax.psum_scatter(
-            block_order(triple_weight_grad, seq_count, data_count),
-            ("dp", "seq"),
-            scatter_dimension=0,
-            tiled=True,
-        ),
-        lax.psum_scatter(
-            block_order(output_weight_grad, seq_count, data_count),
-            ("dp", "seq"),
-            scatter_dimension=0,
-            tiled=True,
-        ),
-        lax.psum_scatter(
-            block_order(expand_weight_grad, seq_count, data_count),
-            ("dp", "seq"),
-            scatter_dimension=0,
-            tiled=True,
-        ),
-        lax.psum_scatter(
-            block_order(reduce_weight_grad, seq_count, data_count),
-            ("dp", "seq"),
-            scatter_dimension=0,
-            tiled=True,
-        ),
-    )
+    dp_size = lax.axis_size("dp")
+    cuts = []
+    cursor = 0
+    for part in (expand_part, reduce_part, output_part, triple_part, mod_part):
+        cuts.append(block_sum[cursor : cursor + part.shape[2]])
+        cursor = cursor + part.shape[2]
+    expand_block = scatter_rest(cuts[0], dp_size).T
+    reduce_block = cuts[1].reshape(4, -1, LANES).transpose(1, 0, 2).reshape(-1, 4 * LANES)
+    reduce_block = scatter_rest(reduce_block, dp_size).T
+    output_block = scatter_rest(cuts[2], dp_size).T
+    triple_block = scatter_rest(cuts[3], dp_size).T
+    mod_block = cuts[4].reshape(-1, 6, LANES // 6).transpose(1, 0, 2).reshape(-1, LANES // 6)
+    mod_block = scatter_rest(mod_block, dp_size).T
+    matrix_parts = (mod_block, triple_block, output_block, expand_block, reduce_block)
     totals = small_results[5]
     masked_rms = jnp.sqrt(totals[:3] / (totals[3] * width))
     return (

time: 914 us -> 476 us (0.52)
  waiting for transfers between devices: 460 us -> 19.4 us
  Pallas kernels: 0 us -> 81.3 us
  blocking collectives: 40.4 us -> 0 us
  other arithmetic: 96.4 us -> 72.3 us
  local copies, waits for them, and re-layouts: 157 us -> 139 us
    reduce_scatter x5 -> x0, waiting for transfers between devices: 433 us -> none  [the longest x1 143 us: local(): lax.psum_scatter(block_order(reduce_weight_grad, seq_count, data_count),...]
    pallas_call x0 -> x1, Pallas kernels: none -> 81.3 us  [reduce_everywhere(): pl.pallas_call(lambda *refs: reduce_kernel(extra_bits, all_bits, *refs),...]
    psum x1 -> x0, blocking collectives: 40.4 us -> none  [local(): summed_small = lax.psum(flat_small, ('dp', 'seq'))]
    transpose x5 -> x3, local copies, waits for them, and re-layouts: 40.4 us -> 2.98 us  [the longest x1 1.62 us: local(): cuts[4].reshape(-1, 6, LANES // 6).transpose(1, 0, 2)]
    reshape x4 -> x13, local copies, waits for them, and re-layouts: 38.9 us -> 61.8 us  [the longest x2 15.7 us: local(): expand_weight_grad.T.astype(bf16).reshape(groups, -1, 2, LANES)]
    dot_general x7 -> x0, local copies, waits for them, and re-layouts: 17.5 us -> none  [the longest x2 7.45 us: local(): jnp.einsum('mhg,mhn->gn', gelu_activations, gradient_narrowed, preferred_...]
    unnamed x147 -> x180, local copies, waits for them, and re-layouts: 13.6 us -> 28.5 us
    convert_element_type x3 -> x0, other arithmetic: 11.6 us -> none  [the longest x1 10.8 us: local(): gelu_activations = gelu_tanh(expanded).astype(jnp.bfloat16)]
  transfers between devices with their start and end apart: 9 -> 4, of which waited for: 6 -> 1; matrix products, arithmetic and copies ran while one was open for 25% -> 28% of each run, Pallas kernels for 0% -> 0%
where the time goes in v1:
time: 476 us; the launch traced here: 468 us
  matrix products  140 us (29%)
  local copies, waits for them, and re-layouts  139 us (29%)
  Pallas kernels  81.3 us (17%)
  other arithmetic  72.3 us (15%)
  waiting for transfers between devices  19.4 us (4%)
  between operations  15.7 us (3%)
    pallas_call x1, Pallas kernels, reduce_everywhere(): pl.pallas_call(lambda *refs: reduce_kernel(extra_bits, all_bits, *refs),...  81.3 us
    unnamed x180, local copies, waits for them, and re-layouts  28.5 us
    all_gather x1, waiting for transfers between devices, local(): lax.all_gather(key_rot, 'seq', axis=1, tiled=True)  19.3 us
    dot_general x1, matrix products, attend_back(): jnp.einsum('qhd,khd->hqk', grad_rows, values, preferred_element_type=jnp....  18.8 us
    convert_element_type x1, other arithmetic, attend_back(): grad_scores = (probability * (grad_prob - row_delta)).astype(jnp.bfloat16)  17.8 us
    reshape x2, local copies, waits for them, and re-layouts, local(): expand_weight_grad.T.astype(bf16).reshape(groups, -1, 2, LANES)  15.7 us
    reshape x2, local copies, waits for them, and re-layouts, local(): reduce_weight_grad.T.astype(bf16).reshape(groups, -1, 2, 4, LANES)  15.2 us
    dot_general x1, matrix products, attend(): jnp.einsum('qhd,khd->hqk', queries, keys, preferred_element_type=jnp.floa...  14.8 us
  transfers between devices with their start and end apart: 4, of which 1 were waited for; matrix products, arithmetic and copies ran while one was open for 28% of the time, Pallas kernels for 0%

profile of v1, /device:TPU:0, one launch (start us, length us, event | category | flops | bytes accessed | tf_op | source)
XLA Modules:
  0.0 468.1 jit_solution(4540356604062988939)
XLA Ops:
  16.8 6.6 %multiply_add_fusion.1 = f32[1,512,4608]{2,1,0:T(8,128)S(1)} fusion(f32[4608]{0:T(1024)} %get-tuple-element.102, f32[512]{0:T(512)S(1)} %bitcast.263, f32[4608]{0:T(1024)} %get-tuple-element.103, f32[512]{0:T(512)S(1)} %bitcast.262, f32[4608]{0:T(1024)} %get-tuple-element.104, f32[512]{0:T(512)S(1)} %bitcast.257, f32[4608]{0:T(1024)} %get-tuple-element.105, ...), kind=kLoop, calls=%fused_computation.14 | loop fusion | flops 35389440 | bytes 9601024 | tf_op jit(solution)/shard_map/add | solution.py:286
  30.8 3.0 copy.67
  36.7 3.1 copy.68
  44.6 3.1 copy.66
  47.7 2.3 mul.764
  50.0 3.0 copy.69
  53.0 5.1 %add_convert_fusion.1 = (bf16[1,512,768]{2,1,0:T(8,128)(2,1)}, f32[1,512,768]{2,1,0:T(8,128)}) fusion(f32[1,512,768]{2,1,0:T(8,128)} %copy.68, f32[1,512,768]{2,1,0:T(8,128)} %copy.69, f32[1,512,768]{2,1,0:T(8,128)} %copy.66, f32[1,512,2304]{2,1,0:T(8,128)} %copy-done.21), kind=kLoop, calls=%fused_computation.106 | loop fusion | flops 1572864 | bytes 10223616 | tf_op jit(solution)/shard_map/convert_element_type | solution.py:312
  58.2 2.4 split.108
  61.6 3.1 copy.64
  68.9 19.3 %all-gather.5.cloned.1.call-done = bf16[1,1024,768]{2,1,0:T(8,128)(2,1)} async-done(((bf16[1,512,768]{2,1,0:T(8,128)(2,1)}), bf16[1,1024,768]{2,1,0:T(8,128)(2,1)}) %all-gather.5.cloned.1.call-update) | async-done | bytes 1572880 | tf_op jit(solution)/shard_map/all_gather | solution.py:316
  88.2 2.6 copy.70
  90.8 14.8 %fusion.8 = (f32[12,512]{1,0:T(8,128)S(1)}, f32[12,512,1024]{2,1,0:T(8,128)}) fusion(pred[512,1024]{1,0:T(8,128)(4,1)} %compare_and_fusion, bf16[512,12,64]{0,2,1:T(8,128)(2,1)} %fusion.43, bf16[1024,12,64]{0,2,1:T(8,128)(2,1)} %bitcast.217), kind=kOutput, calls=%fused_computation.17 | convolution fusion | flops 824174592 | bytes 28073984 | tf_op jit(solution)/shard_map/while/body/eval_jaxpr/qhd,khd->hqk/dot_general | solution.py:325
  105.6 11.8 %fusion = f32[12,512]{1,0:T(8,128)S(1)} fusion(f32[12,512]{1,0:T(8,128)S(1)} %get-tuple-element.162, f32[12,512,1024]{2,1,0:T(8,128)} %get-tuple-element.163, pred[512,1024]{1,0:T(8,128)(4,1)S(1)} %copy-done.16), kind=kLoop, calls=%fused_computation.6 | loop fusion | flops 25159680 | bytes 25739264 | tf_op jit(solution)/shard_map/while/body/eval_jaxpr/reduce_sum | solution.py:331
  118.6 2.6 copy.63
  121.3 13.1 %fusion.50 = bf16[12,64,512]{2,1,0:T(8,128)(2,1)S(1)} fusion(bf16[1024,12,64]{0,2,1:T(8,128)(2,1)} %bitcast.221, f32[12,512]{1,0:T(8,128)} %copy-done.50, f32[12,512]{1,0:T(8,128)} %copy-done.49, f32[12,512,1024]{2,1,0:T(8,128)} %get-tuple-element.163, pred[512,1024]{1,0:T(8,128)(4,1)} %compare_and_fusion), kind=kOutput, calls=%fused_computation.109 | convolution fusion | flops 837156864 | bytes 28098560 | tf_op jit(solution)/shard_map/while/body/eval_jaxpr/hqk,khd->qhd/dot_general | solution.py:333
  134.5 2.7 fusion.87
  138.9 2.6 fusion.92
  141.7 5.1 %fusion.83 = f32[512,768]{1,0:T(8,128)} fusion(bf16[3072,768]{1,0:T(8,128)(2,1)S(1)} %bitcast.268, f32[512,3072]{1,0:T(8,128)S(1)} %fusion.92, f32[3072]{0:T(1024)S(1)} %copy-done.75), kind=kOutput, calls=%fused_computation.207 | convolution fusion | flops 2431647744 | bytes 12595200 | tf_op jit(solution)/shard_map/jpb,bc->jpc/dot_general | solution.py:362
  146.8 11.0 %convert_reduce_fusion = (f32[3072]{0:T(1024)}, bf16[512,3072]{1,0:T(8,128)(2,1)}) fusion(f32[512,3072]{1,0:T(8,128)S(1)} %fusion.92, f32[3072]{0:T(1024)S(1)} %copy-done.75, bf16[3072,768]{1,0:T(8,128)(2,1)} %param.27, bf16[1,512,768]{2,1,0:T(8,128)(2,1)S(1)} %get-tuple-element.115), kind=kOutput, calls=%fused_computation.25 | convolution fusion | flops 2458383360 | bytes 14966784 | tf_op jit(solution)/shard_map/kav,cv->kac/dot_general | solution.py:386
  157.8 7.6 %multiply_reduce_fusion.1 = (f32[768]{0:T(1024)}, f32[512]{0:T(512)S(1)}, f32[]{:T(128)}, f32[]{:T(128)}, f32[]{:T(128)}, /*index=5*/f32[1,512,768]{2,1,0:T(8,128)}, f32[512,768]{1,0:T(8,128)S(1)}) fusion(f32[1,512,768]{2,1,0:T(8,128)S(1)} %get-tuple-element.122, f32[512]{0:T(512)S(1)} %fusion.71, f32[512]{0:T(512)S(1)} %broadcast_multiply_fusion.3, ...), kind=kOutput, calls=%fused_computation.98 | convolution fusion | flops 2424568576 | bytes 20464652 | tf_op jit(solution)/shard_map/yma,ja->ymj/dot_general | solution.py:394
  172.7 18.8 %multiply_reduce_fusion = (f32[12,512]{1,0:T(8,128)}, f32[12,512,1024]{2,1,0:T(8,128)}) fusion(f32[12,512]{1,0:T(8,128)} %log_add_fusion, f32[12,512,1024]{2,1,0:T(8,128)} %get-tuple-element.163, pred[512,1024]{1,0:T(8,128)(4,1)} %compare_and_fusion, bf16[512,12,64]{0,2,1:T(8,128)(2,1)} %bitcast.232, bf16[1024,12,64]{0,2,1:T(8,128)(2,1)} %bitcast.222), kind=kOutput, calls=%fused_computation.1 | convolution fusion | flops 836757504 | bytes 53264384 | tf_op jit(solution)/shard_map/while/body/eval_jaxpr/qhd,khd->hqk/dot_general | solution.py:435
  191.6 17.8 %multiply_convert_fusion = bf16[12,512,1024]{2,1,0:T(8,128)(2,1)S(1)} fusion(f32[12,512,1024]{2,1,0:T(8,128)} %get-tuple-element.167, f32[12,512]{1,0:T(8,128)} %get-tuple-element.166, f32[12,512]{1,0:T(8,128)} %log_add_fusion, f32[12,512,1024]{2,1,0:T(8,128)} %get-tuple-element.163, pred[512,1024]{1,0:T(8,128)(4,1)} %compare_and_fusion), kind=kLoop, calls=%fused_computation | loop fusion | flops 37748736 | bytes 63488000 | tf_op jit(solution)/shard_map/while/body/eval_jaxpr/convert_element_type | solution.py:439
  209.4 4.0 multiply_convert_fusion.1
  214.5 6.9 %convolution_convert_fusion.3 = bf16[3072,768]{1,0:T(8,128)(2,1)} fusion(bf16[512,3072]{1,0:T(8,128)(2,1)} %get-tuple-element.173, bf16[512,768]{1,0:T(8,128)(2,1)} %copy-done.26), kind=kOutput, calls=%fused_computation.33 | convolution fusion | flops 2418278400 | bytes 8650752 | tf_op jit(solution)/shard_map/cqe,cqr->er/dot_general | solution.py:390
  221.5 8.2 %convolution_convert_fusion.2 = bf16[768,3072]{1,0:T(8,128)(2,1)} fusion(bf16[1,512,768]{2,1,0:T(8,128)(2,1)S(1)} %copy-done.40, f32[512,3072]{1,0:T(8,128)} %copy-done.22, f32[3072]{0:T(1024)S(1)} %copy-done.76), kind=kOutput, calls=%fused_computation.32 | convolution fusion | flops 2434007040 | bytes 11808768 | tf_op jit(solution)/shard_map/mhg,mhn->gn/dot_general | solution.py:382
  229.7 13.1 %fusion.24 = bf16[12,64,1024]{2,1,0:T(8,128)(2,1)} fusion(bf16[512,12,64]{0,2,1:T(8,128)(2,1)S(1)} %bitcast.233, f32[12,512]{1,0:T(8,128)S(1)} %copy-done.48, f32[12,512,1024]{2,1,0:T(8,128)} %get-tuple-element.163, pred[512,1024]{1,0:T(8,128)(4,1)S(1)} %copy-done.17), kind=kOutput, calls=%fused_computation.55 | convolution fusion | flops 831258624 | bytes 28073984 | tf_op jit(solution)/shard_map/while/body/eval_jaxpr/hqk,qhd->khd/dot_general | solution.py:429
  242.8 3.2 convolution_convert_fusion.4
  246.0 10.2 %reshape.1500 = bf16[16,192,2,384]{3,2,1,0:T(2,128)(2,1)} reshape(bf16[3072,768]{1,0:T(8,128)(2,1)} %convolution_convert_fusion.3) | data formatting | bytes 9437184 | tf_op jit(solution)/shard_map/reshape | solution.py:524
  256.2 5.5 %copy.72 = bf16[16,192,2,384]{3,1,2,0:T(8,128)(2,1)} copy(bf16[16,192,2,384]{3,2,1,0:T(2,128)(2,1)} %reshape.1500) | data formatting | bytes 9437184 | tf_op jit(solution)/shard_map/reshape | solution.py:524
  261.7 9.7 %reshape.1501 = bf16[16,48,2,4,384]{4,3,2,1,0:T(4,128)(2,1)} reshape(bf16[768,3072]{1,0:T(8,128)(2,1)} %convolution_convert_fusion.2) | data formatting | bytes 9437184 | tf_op jit(solution)/shard_map/reshape | solution.py:525
  271.4 5.6 %copy.73 = bf16[16,48,2,4,384]{4,1,3,2,0:T(8,128)(2,1)} copy(bf16[16,48,2,4,384]{4,3,2,1,0:T(4,128)(2,1)} %reshape.1501) | data formatting | bytes 9437184 | tf_op jit(solution)/shard_map/reshape | solution.py:525
  276.9 3.7 reshape.1502
  282.3 5.3 %constant_dynamic-update-slice_fusion.4 = bf16[2,2,2,2,2,624,384]{6,5,4,3,2,1,0:T(8,128)(2,1)} fusion(bf16[2,2,2,2,2,192,384]{6,5,4,3,2,1,0:T(8,128)(2,1)} %bitcast.210), kind=kLoop, calls=%fused_computation.143 | loop fusion | bytes 9437184
  287.6 2.7 constant_dynamic-update-slice_fusion.3
  292.1 8.5 %fusion.93 = f32[12,64,512]{2,1,0:T(8,128)S(1)} fusion(bf16[1024,12,64]{0,2,1:T(8,128)(2,1)S(1)} %bitcast.218, bf16[12,512,1024]{2,1,0:T(8,128)(2,1)} %copy-done.2), kind=kOutput, calls=%fused_computation.216 | convolution fusion | flops 805306368 | bytes 15728640 | tf_op jit(solution)/shard_map/while/body/eval_jaxpr/hqk,khd->qhd/dot_general | solution.py:441
  305.9 3.8 bitcast_dynamic-update-slice_fusion
  309.8 3.8 convolution_convert_fusion.1
  313.6 2.3 fusion.37
  323.4 4.4 fusion.91
  327.8 3.9 concatenate.92
  333.1 7.9 %reshape.1503 = bf16[16,144,2,384]{3,2,1,0:T(2,128)(2,1)} reshape(bf16[2304,768]{1,0:T(8,128)(2,1)} %convolution_convert_fusion.1) | data formatting | bytes 7077888 | tf_op jit(solution)/shard_map/reshape | solution.py:528
  341.0 4.3 copy.75
  345.3 3.1 convolution_convert_fusion
  348.4 5.2 %reshape.1506 = bf16[16,6,48,2,64]{4,3,2,1,0:T(2,128)(2,1)} reshape(bf16[4608,128]{1,0:T(8,128)(2,1)} %convolution_convert_fusion) | data formatting | bytes 2359296 | tf_op jit(solution)/shard_map/reshape | solution.py:529
  353.6 4.4 copy.82
  358.0 5.0 %concatenate.90 = bf16[2,2,2,2,2,48,384]{6,5,4,3,2,1,0:T(8,128)(2,1)} reshape(bf16[16,2,48,6,64]{4,3,2,1,0:T(8,128)(2,1)} %bitcast.219) | data formatting | bytes 2359296 | tf_op jit(solution)/shard_map/concatenate | solution.py:531
  363.0 4.3 constant_dynamic-update-slice_fusion.1
  368.5 81.3 %shard_map.249 = (f32[624,384]{1,0:T(8,128)S(1)}, f32[80,128]{1,0:T(8,128)S(1)}) custom-call(bf16[2,2,2,2,2,624,384]{6,5,4,3,2,1,0:T(8,128)(2,1)} %constant_dynamic-update-slice_fusion.refs_0_, f32[80,128]{1,0:T(8,128)S(1)} %copy-done.1), custom_call_target="tpu_custom_call" | custom-call | tf_op jit(solution)/shard_map/pallas_call | solution.py:218
  (261 shorter events, 70.6 us)
Async XLA Ops:
  7.2 16.7 %copy-start = (bf16[768,2304]{1,0:T(8,128)(2,1)S(1)}, bf16[768,2304]{1,0:T(8,128)(2,1)}, u32[]{:S(2)}) copy-start(bf16[768,2304]{1,0:T(8,128)(2,1)} %param.22) | copy-start | bytes 10616836
  7.2 81.0 %all-gather.5.cloned.1.call-start = ((), (), s32[]{:S(2)}) async-start(), calls=%async_computation.3 | async-start | bytes 2359296 | tf_op jit(solution)/shard_map/all_gather | solution.py:316
  9.4 5.3 %copy-start.6 = (bf16[1,512,768]{2,1,0:T(8,128)(2,1)S(1)}, bf16[1,512,768]{2,1,0:T(8,128)(2,1)}, u32[]{:S(2)}) copy-start(bf16[1,512,768]{2,1,0:T(8,128)(2,1)} %param.15) | copy-start | bytes 2359300
  14.7 8.7 %copy-start.52 = (f32[512]{0:T(512)}, f32[512]{0:T(512)S(1)}, u32[]{:S(2)}) copy-start(f32[512]{0:T(512)S(1)} %broadcast_multiply_fusion.4) | copy-start | bytes 6148
  15.6 7.8 %copy-start.56 = (f32[512]{0:T(512)}, f32[512]{0:T(512)S(1)}, u32[]{:S(2)}) copy-start(f32[512]{0:T(512)S(1)} %fusion.70) | copy-start | bytes 6148
  16.8 6.6 %copy-start.7 = (bf16[1,512,768]{2,1,0:T(8,128)(2,1)S(1)}, bf16[1,512,768]{2,1,0:T(8,128)(2,1)}, u32[]{:S(2)}) copy-start(bf16[1,512,768]{2,1,0:T(8,128)(2,1)} %param.15) | copy-start | bytes 2359300
  16.8 6.6 %copy-start.54 = (f32[768]{0:T(1024)S(1)}, f32[768]{0:T(1024)}, u32[]{:S(2)}) copy-start(f32[768]{0:T(1024)} %param.19) | copy-start | bytes 9220
  58.1 60.5 %all-gather.3.cloned.1.call-start = ((), (), s32[]{:S(2)}) async-start(), calls=%async_computation.2 | async-start | bytes 2359296 | tf_op jit(solution)/shard_map/all_gather | solution.py:317
  60.5 242.5 %reduce-scatter.3.cloned.1.call-start = ((), (), s32[]{:S(2)}) async-start(), calls=%async_computation.4 | async-start | bytes 2359296 | tf_op jit(solution)/shard_map/reduce_scatter | solution.py:458
  90.7 14.8 %copy-start.16 = (pred[512,1024]{1,0:T(8,128)(4,1)S(1)}, pred[512,1024]{1,0:T(8,128)(4,1)}, u32[]{:S(2)}) copy-start(pred[512,1024]{1,0:T(8,128)(4,1)} %compare_and_fusion) | copy-start | bytes 1572868
  105.6 11.8 %copy-start.49 = (f32[12,512]{1,0:T(8,128)}, f32[12,512]{1,0:T(8,128)S(1)}, u32[]{:S(2)}) copy-start(f32[12,512]{1,0:T(8,128)S(1)} %get-tuple-element.162) | copy-start | bytes 73732
  121.2 16.2 %slice-start = ((s8[9437184]{0:T(1024)(128)(4,1)}), s8[4194304]{0:T(1024)(128)(4,1)S(1)}, s32[]{:S(2)}) async-start(s8[9437184]{0:T(1024)(128)(4,1)} %bitcast.208), calls=%async_computation.6 | async-start | bytes 8388608
  121.2 13.2 %copy-start.8 = (bf16[1,512,768]{2,1,0:T(8,128)(2,1)S(1)}, bf16[1,512,768]{2,1,0:T(8,128)(2,1)}, u32[]{:S(2)}) copy-start(bf16[1,512,768]{2,1,0:T(8,128)(2,1)} %param.15) | copy-start | bytes 2359300
  121.2 13.2 %copy-start.35 = (bf16[768,768]{1,0:T(8,128)(2,1)S(1)}, bf16[768,768]{1,0:T(8,128)(2,1)}, u32[]{:S(2)}) copy-start(bf16[768,768]{1,0:T(8,128)(2,1)} %param.23) | copy-start | bytes 3538948
  121.2 16.2 %slice-start.1 = ((s8[9437184]{0:T(1024)(128)(4,1)}), s8[4194304]{0:T(1024)(128)(4,1)S(1)}, s32[]{:S(2)}) async-start(s8[9437184]{0:T(1024)(128)(4,1)} %bitcast.208), calls=%async_computation.7 | async-start | bytes 8388608
  121.2 16.3 %slice-start.2 = ((s8[9437184]{0:T(1024)(128)(4,1)}), s8[1048576]{0:T(1024)(128)(4,1)S(1)}, s32[]{:S(2)}) async-start(s8[9437184]{0:T(1024)(128)(4,1)} %bitcast.208), calls=%async_computation.8 | async-start | bytes 2097152
  134.4 4.4 slice-start.5
  137.1 20.7 %copy-start.23 = (f32[512,768]{1,0:T(8,128)}, f32[512,768]{1,0:T(8,128)S(1)}, u32[]{:S(2)}) copy-start(f32[512,768]{1,0:T(8,128)S(1)} %get-tuple-element.164) | copy-start | bytes 4718596
  137.1 28.3 %copy-start.4 = (f32[1,512,768]{2,1,0:T(8,128)}, f32[1,512,768]{2,1,0:T(8,128)S(1)}, u32[]{:S(2)}) copy-start(f32[1,512,768]{2,1,0:T(8,128)S(1)} %get-tuple-element.122) | copy-start | bytes 4718596
  137.5 4.0 slice-start.7
  138.8 8.0 %copy-start.39 = (bf16[1,512,768]{2,1,0:T(8,128)(2,1)}, bf16[1,512,768]{2,1,0:T(8,128)(2,1)S(1)}, u32[]{:S(2)}) copy-start(bf16[1,512,768]{2,1,0:T(8,128)(2,1)S(1)} %get-tuple-element.115) | copy-start | bytes 2359300
  141.6 5.1 %copy-start.22 = (f32[512,3072]{1,0:T(8,128)}, f32[512,3072]{1,0:T(8,128)S(1)}, u32[]{:S(2)}) copy-start(f32[512,3072]{1,0:T(8,128)S(1)} %fusion.92) | copy-start | bytes 18874372
  146.8 11.0 %copy-start.72 = (f32[768]{0:T(1024)S(1)}, f32[768]{0:T(1024)}, u32[]{:S(2)}) copy-start(f32[768]{0:T(1024)} %param.28) | copy-start | bytes 9220
  191.6 17.8 %copy-start.20 = (bf16[512,12,64]{0,2,1:T(8,128)(2,1)S(1)}, bf16[512,12,64]{0,2,1:T(8,128)(2,1)}, u32[]{:S(2)}) copy-start(bf16[512,12,64]{0,2,1:T(8,128)(2,1)} %fusion.43) | copy-start | bytes 2359300
  209.4 5.0 %copy-start.2 = (bf16[12,512,1024]{2,1,0:T(8,128)(2,1)}, bf16[12,512,1024]{2,1,0:T(8,128)(2,1)S(1)}, u32[]{:S(2)}) copy-start(bf16[12,512,1024]{2,1,0:T(8,128)(2,1)S(1)} %multiply_convert_fusion) | copy-start | bytes 37748740
  214.4 91.4 %reduce-scatter.5.cloned.1.call-start = ((), (), s32[]{:S(2)}) async-start(), calls=%async_computation.5 | async-start | bytes 2359296 | tf_op jit(solution)/shard_map/reduce_scatter | solution.py:461
  214.5 7.0 %copy-start.40 = (bf16[1,512,768]{2,1,0:T(8,128)(2,1)S(1)}, bf16[1,512,768]{2,1,0:T(8,128)(2,1)}, u32[]{:S(2)}) copy-start(bf16[1,512,768]{2,1,0:T(8,128)(2,1)} %copy-done.39) | copy-start | bytes 2359300
  214.5 7.0 %copy-start.76 = (f32[3072]{0:T(1024)S(1)}, f32[3072]{0:T(1024)}, u32[]{:S(2)}) copy-start(f32[3072]{0:T(1024)} %param.26) | copy-start | bytes 36868
  221.5 8.2 %copy-start.17 = (pred[512,1024]{1,0:T(8,128)(4,1)S(1)}, pred[512,1024]{1,0:T(8,128)(4,1)}, u32[]{:S(2)}) copy-start(pred[512,1024]{1,0:T(8,128)(4,1)} %compare_and_fusion) | copy-start | bytes 1572868
  221.5 8.2 %copy-start.28 = (bf16[512,768]{0,1:T(8,128)(2,1)S(1)}, bf16[512,768]{0,1:T(8,128)(2,1)}, u32[]{:S(2)}) copy-start(bf16[512,768]{0,1:T(8,128)(2,1)} %copy.71) | copy-start | bytes 2359300
  221.5 8.2 %copy-start.48 = (f32[12,512]{1,0:T(8,128)S(1)}, f32[12,512]{1,0:T(8,128)}, u32[]{:S(2)}) copy-start(f32[12,512]{1,0:T(8,128)} %log_add_fusion) | copy-start | bytes 73732
  280.7 6.9 %slice-start.3 = ((s8[4718592]{0:T(1024)(128)(4,1)}), s8[4194304]{0:T(1024)(128)(4,1)S(1)}, s32[]{:S(2)}) async-start(s8[4718592]{0:T(1024)(128)(4,1)} %bitcast.211), calls=%async_computation.9 | async-start | bytes 8388608
  282.3 5.3 %slice-start.4 = ((s8[4718592]{0:T(1024)(128)(4,1)}), s8[524288]{0:T(1024)(128)(4,1)S(1)}, s32[]{:S(2)}) async-start(s8[4718592]{0:T(1024)(128)(4,1)} %bitcast.211), calls=%async_computation.10 | async-start | bytes 1048576
  292.1 8.5 %copy-start.47 = (f32[512,64]{0,1:T(8,128)S(1)}, f32[512,64]{0,1:T(8,128)}, u32[]{:S(2)}) copy-start(f32[512,64]{0,1:T(8,128)} %get-tuple-element.144) | copy-start | bytes 393220
  305.9 3.8 copy-start.38
  305.9 3.8 copy-start.41
  305.9 3.8 copy-start.44
  305.9 3.8 copy-start.74
  309.7 3.8 copy-start.9
  309.7 3.8 copy-start.53
  309.7 3.8 copy-start.55
  323.4 4.4 copy-start.68
  323.4 4.4 copy-start.69
  323.4 4.4 copy-start.71
  341.0 4.3 copy-start.45
  341.0 4.3 copy-start.60
  341.0 4.3 copy-start.62
  363.0 4.3 copy-start.25
  (43 other events, 84.7 us)
Sparse Core Ops, SparseCore 0:
  58.2 29.8 all-gather.4
  90.3 27.2 all-gather.2
  214.6 26.3 reduce-scatter.2
  243.1 26.3 reduce-scatter.4

commit v2 on v1

v2 whole, which is shorter than its diff:
```python
import functools
import math

import jax
import jax.numpy as jnp
import numpy as np
from jax import lax
from jax.experimental import pallas as pl
from jax.experimental.pallas import tpu as pltpu
from jax.sharding import PartitionSpec as P

HEADS = 12
BLOCK = 128
MAX_SEQUENCES = 8
SEGMENT_LANE = 40
MASKED = -1000000000.0
LANES = 384
GROUP_BITS = 4
MESH_ID = pl.DeviceIdType.MESH
F32, BF16 = jnp.float32, jnp.bfloat16

ROTARY_COS, ROTARY_SIN, BLOCK_COS, BLOCK_SIN = 0, 128, 256, 264
HIGH_COS, HIGH_SIN, LOW_COS, LOW_SIN, TABLE_ROWS = 272, 304, 336, 368, 400

FIRST_GAIN, MOD_BIAS, SECOND_GAIN, EXPAND_BIAS, REDUCE_BIAS, STATS, SMALL_ROWS = 0, 1, 7, 8, 12, 13, 16


def angle_table():
    lane = np.arange(128)
    rotary = np.exp((lane % 32) * (-2.0 * math.log(10000.0) / 64))
    timing = np.exp((lane % 64) * (-math.log(10000.0) / 64))
    steps = np.arange(128)[:, None]
    angles = [
        (np.cos, steps * rotary), (np.sin, steps * rotary),
        (np.cos, steps[:8] * 128 * rotary), (np.sin, steps[:8] * 128 * rotary),
        (np.cos, steps[:32] * 32 * timing), (np.sin, steps[:32] * 32 * timing),
        (np.cos, steps[:32] * timing), (np.sin, steps[:32] * timing),
    ]
    return np.concatenate([fn(angle) for fn, angle in angles]).astype(np.float32)


def dot(left, right):
    return jnp.dot(left, right, preferred_element_type=F32)


def dot_nt(left, right):
    return lax.dot_general(left, right, (((1,), (1,)), ((), ())), preferred_element_type=F32)


def dot_tn(left, right):
    return lax.dot_general(left, right, (((0,), (0,)), ((), ())), preferred_element_type=F32)


def lane_iota(shape):
    return lax.broadcasted_iota(jnp.int32, shape, len(shape) - 1)


def row_iota(shape):
    return lax.broadcasted_iota(jnp.int32, shape, 0)


def block_place(segments, lengths, block):
    segment = segments[0, block * BLOCK]
    before = jnp.int32(0)
    for other in range(segments.shape[1] // BLOCK):
        same = (segments[0, other * BLOCK] == segment) & (other < block)
        before = before + jnp.where(same, 1, 0)
    return segment, before, lengths[0, segment] - before * BLOCK


def rotary_block(table, before):
    cos_row, sin_row = table[pl.ds(ROTARY_COS, 128), :], table[pl.ds(ROTARY_SIN, 128), :]
    cos_block = table[pl.ds(BLOCK_COS + before, 1), :]
    sin_block = table[pl.ds(BLOCK_SIN + before, 1), :]
    cosine = cos_row * cos_block - sin_row * sin_block
    sine = sin_row * cos_block + cos_row * sin_block
    first_half = lane_iota(sine.shape) % 64 < 32
    return cosine, jnp.where(first_half, -sine, sine)


def turn(values, cosine, sine):
    first_half = lane_iota(values.shape) % 64 < 32
    swapped = jnp.where(first_half, pltpu.roll(values, 96, 1), pltpu.roll(values, 32, 1))
    return values * cosine + swapped * sine


def mean_of(values):
    return jnp.mean(values, axis=-1, keepdims=True)


def split_three(values):
    first = values.astype(BF16)
    rest = values - first.astype(F32)
    second = rest.astype(BF16)
    third = (rest - second.astype(F32)).astype(BF16)
    place = lane_iota(values.shape) % 3
    picked = jnp.where(place == 0, first.astype(F32), jnp.where(place == 1, second.astype(F32), third.astype(F32)))
    return picked.astype(BF16)


def forward_kernel(
    segments, lengths, times, hidden, table, first_gain, mod_weight, mod_bias, weight,
    normed, queries, keys, values, attended, query_features, key_features, modulation, condition,
    other_hidden, turned_values, out_t, peak, total, send_sem, recv_sem,
):
    tokens, width = hidden.shape
    blocks = tokens // BLOCK
    seq = lax.axis_index("seq")
    partner = (lax.axis_index("dp"), 1 - seq)
    barrier = pltpu.get_barrier_semaphore()
    pl.semaphore_signal(barrier, inc=1, device_id=partner, device_id_type=MESH_ID)
    pl.semaphore_wait(barrier, 1)
    exchange = pltpu.make_async_remote_copy(
        hidden, other_hidden, send_sem, recv_sem, device_id=partner, device_id_type=MESH_ID
    )
    exchange.start()

    places = []
    for number in range(2 * blocks):
        block = (seq if number < blocks else 1 - seq) * blocks + number % blocks
        places.append(block_place(segments, lengths, block))
        time = times[0, places[number][0]]
        high, low = time // 32, time % 32
        cos_high, sin_high = table[pl.ds(HIGH_COS + high, 1), :], table[pl.ds(HIGH_SIN + high, 1), :]
        cos_low, sin_low = table[pl.ds(LOW_COS + low, 1), :], table[pl.ds(LOW_SIN + low, 1), :]
        cosine = cos_high * cos_low - sin_high * sin_low
        sine = sin_high * cos_low + cos_high * sin_low
        row = jnp.where(lane_iota(cosine.shape) < 64, cosine, sine)
        condition[pl.ds(number, 1), :] = row.astype(BF16).astype(F32)
    modulation[...] = dot(condition[...].astype(BF16), mod_weight[...]) + mod_bias[...]

    lane = lane_iota((BLOCK, 128))
    row = row_iota((BLOCK, 128))

    for part in range(2):
        source = hidden if part == 0 else other_hidden
        if part == 1:
            exchange.wait_recv()
        turns = []
        for number in range(blocks):
            rows = pl.ds(number * BLOCK, BLOCK)
            segment, before, valid_count = places[part * blocks + number]
            turns.append(rotary_block(table, before))
            mine = lane == SEGMENT_LANE + segment
            in_lanes = (lane >= SEGMENT_LANE) & (lane < SEGMENT_LANE + MAX_SEQUENCES)
            blocked = in_lanes & jnp.logical_not(mine & (row < valid_count))
            key_features[part, rows, :] = jnp.where(blocked, MASKED, 0.0).astype(BF16)
            if part == 0:
                query_features[rows, :] = jnp.where(mine, 1.0, 0.0).astype(BF16)
            mod_row = pl.ds(part * blocks + number, 1)
            shift, scale = modulation[mod_row, pl.ds(0, width)], modulation[mod_row, pl.ds(width, width)]
            value = source[rows, :].astype(F32)
            centered = value - mean_of(value)
            spread = mean_of(centered * centered)
            line = centered * lax.rsqrt(spread + 1e-05) * first_gain[...]
            result = (line * (1.0 + scale) + shift).astype(BF16)
            if part == 0:
                normed[rows, :] = result
            else:
                other_hidden[rows, :] = result
        normed_source = normed if part == 0 else other_hidden
        for tile in range(3 * width // LANES):
            which, first = divmod(tile * LANES, width)
            product = dot(normed_source[...], weight[:, pl.ds(tile * LANES, LANES)])
            target = (queries, keys, values)[which]
            for number in range(blocks):
                cosine, sine = turns[number]
                for pair in range(LANES // 128):
                    piece = product[number * BLOCK : (number + 1) * BLOCK, pair * 128 : (pair + 1) * 128]
                    if which < 2:
                        piece = turn(piece, cosine, sine)
                    if which == 0:
                        piece = piece.astype(BF16).astype(F32) * 0.125
                    target[part, pl.ds(number * BLOCK, BLOCK), pl.ds(first + pair * 128, 128)] = piece.astype(BF16)
        turned_values[...] = jnp.transpose(values[part])

        def attend(pair, carry):
            lanes = pl.ds(pl.multiple_of(pair * 128, 128), 128)
            query_pair, key_pair = queries[0, :, lanes], keys[part, :, lanes]
            left = jnp.concatenate([key_pair, key_features[part]], axis=1)
            pair_lane = lane_iota(query_pair.shape)
            for half in range(2):
                head = pair * 2 + half
                head_rows = pl.ds(pl.multiple_of(head * 64, 64), 64)
                one_row = pl.ds(head, 1)
                query = jnp.where((pair_lane < 64) == (half == 0), query_pair, jnp.zeros_like(query_pair))
                scores = dot_nt(left, jnp.concatenate([query, query_features[...]], axis=1))
                top = jnp.max(scores, axis=0, keepdims=True)
                if part == 1:
                    top = jnp.maximum(top, peak[one_row, :])
                weights = jnp.exp(scores - top)
                summed = jnp.sum(weights, axis=0, keepdims=True)
                mixed = dot(turned_values[head_rows, :], weights.astype(BF16))
                if part == 0:
                    out_t[head_rows, :] = mixed
                    total[one_row, :] = summed
                    peak[one_row, :] = top
                else:
                    rescale = jnp.exp(peak[one_row, :] - top)
                    summed = summed + rescale * total[one_row, :]
                    out_t[head_rows, :] = (out_t[head_rows, :] * rescale + mixed) * (1.0 / summed)
                    peak[one_row, :] = top + jnp.log(summed)
            return carry

        lax.fori_loop(0, HEADS // 2, attend, 0)

    attended[...] = jnp.transpose(out_t[...].astype(BF16))
    log_rows = jnp.concatenate(
        [jnp.broadcast_to(peak[pl.ds(head, 1), :], (3, tokens)) for head in range(HEADS)]
        + [jnp.zeros((128 - 3 * HEADS, tokens), F32)], axis=0,
    )
    query_features[...] = query_features[...] + split_three(jnp.transpose(log_rows))
    exchange.wait_send()


def forward(segments, lengths, times, hidden, table, first_gain, mod_weight, mod_bias, weight):
    tokens, width = hidden.shape
    blocks = 2 * tokens // BLOCK
    half = jax.ShapeDtypeStruct((tokens, width), BF16)
    both = jax.ShapeDtypeStruct((2, tokens, width), BF16)
    smem, vmem = pl.BlockSpec(memory_space=pltpu.SMEM), pl.BlockSpec(memory_space=pltpu.VMEM)
    return pl.pallas_call(
        forward_kernel,
        out_shape=(
            half, both, both, both, half,
            jax.ShapeDtypeStruct((tokens, 128), BF16),
            jax.ShapeDtypeStruct((2, tokens, 128), BF16),
            jax.ShapeDtypeStruct((blocks, 6 * width), F32),
            jax.ShapeDtypeStruct((blocks, 128), F32),
        ),
        in_specs=[smem] * 3 + [vmem] * 6,
        out_specs=(vmem,) * 9,
        scratch_shapes=[
            pltpu.VMEM((tokens, width), BF16),
            pltpu.VMEM((width, tokens), BF16),
            pltpu.VMEM((width, tokens), F32),
            pltpu.VMEM((16, tokens), F32),
            pltpu.VMEM((16, tokens), F32),
            pltpu.SemaphoreType.DMA,
            pltpu.SemaphoreType.DMA,
        ],
        compiler_params=pltpu.CompilerParams(
            collective_id=1, has_side_effects=True, vmem_limit_bytes=56 << 20
        ),
    )(segments, lengths, times, hidden, table, first_gain, mod_weight, mod_bias, weight)


TILE = 384


def mlp_kernel(
    segments, lengths, hidden, attended, cotangent, modulation, second_gain, expand_bias, reduce_bias,
    out_weight_hbm, widen_hbm, narrow_hbm,
    block_out, grad_middle, grad_attended, delta_features, mod_grads, small, expand_hbm, reduce_hbm, output_hbm,
    out_weight, widen, narrow, expand_part, reduce_part, output_part,
    projected, middle, normal, spread_row, normed, slope, activated, reduced, grad_low, grad_low_t, grad_normed,
    load_sem, store_sem,
):
    tokens, width = hidden.shape
    hidden_units = widen.shape[1]
    tiles = hidden_units // TILE
    blocks = tokens // BLOCK
    seq = lax.axis_index("seq")
    loads = [
        pltpu.make_async_copy(source, target, load_sem.at[number])
        for number, (source, target) in enumerate(
            ((out_weight_hbm, out_weight), (widen_hbm, widen), (narrow_hbm, narrow))
        )
    ]
    for load in loads:
        load.start()
    row = row_iota((BLOCK, 1))
    keep = []
    for number in range(blocks):
        valid_count = block_place(segments, lengths, seq * blocks + number)[2]
        keep.append(jnp.where(row < valid_count, 1.0, 0.0))

    def mod_part(number, part):
        return modulation[pl.ds(number, 1), pl.ds(part * width, width)]

    loads[0].wait()
    for first in range(0, width, 256):
        lanes = pl.ds(first, 256)
        projected[:, lanes] = dot(attended[...], out_weight[:, lanes])
    branch_sum = jnp.zeros((1, width), F32)
    for number in range(blocks):
        rows = pl.ds(number * BLOCK, BLOCK)
        branch = mod_part(number, 2) * projected[rows, :]
        branch_sum = branch_sum + jnp.sum(keep[number] * branch * branch, axis=0, keepdims=True)
        value = hidden[rows, :].astype(F32) + branch
        middle[rows, :] = value
        centered = value - mean_of(value)
        inverse = lax.rsqrt(mean_of(centered * centered) + 1e-05)
        normal[rows, :] = centered * inverse
        spread_row[rows, :] = jnp.broadcast_to(inverse, (BLOCK, 128))
        line = normal[rows, :] * second_gain[...]
        normed[rows, :] = (line * (1.0 + mod_part(number, 4)) + mod_part(number, 3)).astype(BF16)

    reduced[...] = jnp.zeros_like(reduced)
    loads[1].wait()
    loads[2].wait()

    def ahead(tile):
        lanes = pl.ds(pl.multiple_of(tile * TILE, TILE), TILE)
        u = dot(normed[...], widen[:, lanes]) + expand_bias[:, lanes]
        square = u * u
        tanh = jnp.tanh(u * (0.7978845608028654 + 0.7978845608028654 * 0.044715 * square))
        half_sum = 0.5 + 0.5 * tanh
        active = (u * half_sum).astype(BF16)
        inner = 0.7978845608028654 + 3.0 * 0.7978845608028654 * 0.044715 * square
        slope[:, lanes] = half_sum + (0.5 * u) * (1.0 - tanh * tanh) * inner
        activated[:, lanes] = active
        reduced[...] += dot(active, narrow[lanes, :])

    def ahead_two(step, carry):
        ahead(2 * step)
        ahead(2 * step + 1)
        return carry

    lax.fori_loop(0, tiles // 2, ahead_two, 0)

    value_sum = jnp.zeros((1, width), F32)
    mlp_sum = jnp.zeros((1, width), F32)
    bias_sum = jnp.zeros((1, width), F32)
    for number in range(blocks):
        rows = pl.ds(number * BLOCK, BLOCK)
        gate = mod_part(number, 5)
        full = reduced[rows, :] + reduce_bias[...]
        branch = gate * full
        value = middle[rows, :] + branch
        block_out[rows, :] = value.astype(BF16)
        value_sum = value_sum + jnp.sum(keep[number] * value * value, axis=0, keepdims=True)
        mlp_sum = mlp_sum + jnp.sum(keep[number] * branch * branch, axis=0, keepdims=True)
        grad_out = cotangent[rows, :].astype(F32) * keep[number]
        mod_grads[pl.ds(number, 1), pl.ds(3 * width, width)] = jnp.sum(grad_out * full, axis=0, keepdims=True)
        low = (gate * grad_out).astype(BF16)
        grad_low[rows, :] = low
        bias_sum = bias_sum + jnp.sum(low.astype(F32), axis=0, keepdims=True)
    grad_low_t[...] = jnp.transpose(grad_low[...])
    grad_normed[...] = jnp.zeros_like(grad_normed)
    small[...] = jnp.zeros_like(small)
    small[pl.ds(REDUCE_BIAS, 1), :] = bias_sum

    def stores(tile):
        expand_copy = pltpu.make_async_copy(
            expand_part.at[pl.ds(2 * tile, 2)], expand_hbm.at[pl.ds(2 * tile, 2)], store_sem.at[0, tile]
        )
        reduce_copy = pltpu.make_async_copy(
            reduce_part.at[:, tile // 4, tile % 4], reduce_hbm.at[:, tile // 4, tile % 4], store_sem.at[1, tile]
        )
        return expand_copy, reduce_copy

    def back(tile):
        lanes = pl.ds(pl.multiple_of(tile * TILE, TILE), TILE)
        grad_active = dot_nt(grad_low[...], narrow[lanes, :])
        grad_wide = (grad_active * slope[:, lanes]).astype(BF16)
        slope[pl.ds(0, 1), lanes] = jnp.sum(grad_wide.astype(F32), axis=0, keepdims=True)
        grad_normed[...] += dot_nt(grad_wide, widen[:, lanes])
        expand_t = dot_tn(grad_wide, normed[...]).astype(BF16)
        for group in range(2):
            for side in range(2):
                expand_part[2 * tile + group, side] = expand_t[
                    group * 192 : group * 192 + 192, side * LANES : side * LANES + LANES
                ]
        reduce_t = dot(grad_low_t[...], activated[:, lanes]).astype(BF16)
        reduce_part[:, tile // 4, tile % 4] = reduce_t.reshape(16, 48, TILE)
        for copy in stores(tile):
            copy.start()

    def back_two(step, carry):
        back(2 * step)
        back(2 * step + 1)
        return carry

    lax.fori_loop(0, tiles // 2, back_two, 0)
    for part in range(hidden_units // width):
        small[pl.ds(EXPAND_BIAS + part, 1), :] = slope[pl.ds(0, 1), pl.ds(part * width, width)]

    gain_sum = jnp.zeros((1, width), F32)
    for number in range(blocks):
        rows = pl.ds(number * BLOCK, BLOCK)
        one = pl.ds(number, 1)
        grad = grad_normed[rows, :]
        line = normal[rows, :] * second_gain[...]
        mod_grads[one, pl.ds(width, width)] = jnp.sum(grad, axis=0, keepdims=True)
        mod_grads[one, pl.ds(2 * width, width)] = jnp.sum(grad * line, axis=0, keepdims=True)
        grad_line = grad * (1.0 + mod_part(number, 4))
        gain_sum = gain_sum + jnp.sum(grad_line * normal[rows, :], axis=0, keepdims=True)
        grad_normal = grad_line * second_gain[...]
        along = mean_of(grad_normal * normal[rows, :])
        term = (grad_normal - mean_of(grad_normal) - normal[rows, :] * along) * spread_row[rows, :1]
        total = cotangent[rows, :].astype(F32) * keep[number] + term
        grad_middle[rows, :] = total
        mod_grads[one, pl.ds(0, width)] = jnp.sum(total * projected[rows, :], axis=0, keepdims=True)
        grad_low[rows, :] = (mod_part(number, 2) * total).astype(BF16)
    small[pl.ds(SECOND_GAIN, 1), :] = gain_sum

    for first in range(0, width, TILE):
        output_t = dot_tn(grad_low[:, pl.ds(first, TILE)], attended[...]).astype(BF16)
        for group in range(TILE // 48):
            for side in range(2):
                output_part[first // 48 + group, side] = output_t[
                    group * 48 : group * 48 + 48, side * LANES : side * LANES + LANES
                ]
    output_copy = pltpu.make_async_copy(output_part, output_hbm, load_sem.at[0])
    output_copy.start()
    for first in range(0, width, 256):
        grad_attended[:, pl.ds(first, 256)] = dot_nt(
            grad_low[...], out_weight[pl.ds(first, 256), :]
        ).astype(BF16)
    head_lane = row_iota((width, 128)) // 64 == lane_iota((width, 128)) // 3
    chooser = jnp.where(head_lane & (lane_iota((width, 128)) < 3 * HEADS), 1.0, 0.0).astype(BF16)
    for number in range(blocks):
        rows = pl.ds(number * BLOCK, BLOCK)
        product = grad_attended[rows, :].astype(F32) * attended[rows, :].astype(F32)
        upper = product.astype(BF16)
        lower = (product - upper.astype(F32)).astype(BF16)
        delta_features[rows, :] = split_three(dot(upper, chooser) + dot(lower, chooser))

    lane = lane_iota((1, width))
    counts = jnp.zeros((1, 1), F32)
    for number in range(blocks):
        counts = counts + jnp.sum(keep[number], axis=0, keepdims=True)
    sums = [jnp.sum(term, axis=1, keepdims=True) for term in (value_sum, branch_sum, mlp_sum)] + [counts]
    stats = jnp.zeros((1, width), F32)
    for place, term in enumerate(sums):
        stats = jnp.where(lane == place, term, stats)
    small[pl.ds(STATS, 1), :] = stats

    def drain(tile, carry):
        for copy in stores(tile):
            copy.wait()
        return carry

    lax.fori_loop(0, tiles, drain, 0)
    output_copy.wait()


def mlp(segments, lengths, hidden, attended, cotangent, modulation, second_gain, expand_bias, reduce_bias, out_weight, widen, narrow):
    tokens, width = hidden.shape
    units = widen.shape[1]
    smem, vmem = pl.BlockSpec(memory_space=pltpu.SMEM), pl.BlockSpec(memory_space=pltpu.VMEM)
    hbm = pl.BlockSpec(memory_space=pl.ANY)
    groups = 2**GROUP_BITS
    expand_shape = (groups, 2, units // groups, LANES)
    reduce_shape = (groups, 2, 4, width // groups, LANES)
    output_shape = (groups, 2, width // groups, LANES)
    wide, half = (tokens, units), (tokens, width)
    return pl.pallas_call(
        mlp_kernel,
        out_shape=(
            jax.ShapeDtypeStruct(half, BF16),
            jax.ShapeDtypeStruct(half, F32),
            jax.ShapeDtypeStruct(half, BF16),
            jax.ShapeDtypeStruct((tokens, 128), BF16),
            jax.ShapeDtypeStruct((tokens // BLOCK, 4 * width), F32),
            jax.ShapeDtypeStruct((SMALL_ROWS, width), F32),
            jax.ShapeDtypeStruct(expand_shape, BF16),
            jax.ShapeDtypeStruct(reduce_shape, BF16),
            jax.ShapeDtypeStruct(output_shape, BF16),
        ),
        in_specs=[smem] * 2 + [vmem] * 7 + [hbm] * 3,
        out_specs=(vmem,) * 6 + (hbm,) * 3,
        scratch_shapes=[
            pltpu.VMEM(out_weight.shape, BF16),
            pltpu.VMEM(widen.shape, BF16),
            pltpu.VMEM(narrow.shape, BF16),
            pltpu.VMEM(expand_shape, BF16),
            pltpu.VMEM(reduce_shape, BF16),
            pltpu.VMEM(output_shape, BF16),
            pltpu.VMEM(half, F32),
            pltpu.VMEM(half, F32),
            pltpu.VMEM(half, F32),
            pltpu.VMEM((tokens, 128), F32),
            pltpu.VMEM(half, BF16),
            pltpu.VMEM(wide, F32),
            pltpu.VMEM(wide, BF16),
            pltpu.VMEM(half, F32),
            pltpu.VMEM(half, BF16),
            pltpu.VMEM((width, tokens), BF16),
            pltpu.VMEM(half, F32),
            pltpu.SemaphoreType.DMA((3,)),
            pltpu.SemaphoreType.DMA((2, units // TILE)),
        ],
        compiler_params=pltpu.CompilerParams(vmem_limit_bytes=58 << 20),
    )(segments, lengths, hidden, attended, cotangent, modulation, second_gain, expand_bias, reduce_bias, out_weight, widen, narrow)


def backward_kernel(
    segments, lengths, hidden, normed, queries, keys, values, query_features, key_features, grad_attended, delta_features,
    grad_middle, modulation, mod_grads, small_in, table, first_gain, weight,
    input_grad, small, triple_part, mod_rows,
    other_grad, other_delta, other_features, keys_t, grad_query_t, grad_key, grad_value, grad_triple, grad_normed,
    send_sem, recv_sem,
):
    tokens, width = hidden.shape
    blocks = tokens // BLOCK
    seq = lax.axis_index("seq")
    partner = (lax.axis_index("dp"), 1 - seq)
    barrier = pltpu.get_barrier_semaphore()
    pl.semaphore_signal(barrier, inc=1, device_id=partner, device_id_type=MESH_ID)
    pl.semaphore_wait(barrier, 1)
    exchanges = [
        pltpu.make_async_remote_copy(
            source, target, send_sem.at[number], recv_sem.at[number], device_id=partner, device_id_type=MESH_ID
        )
        for number, (source, target) in enumerate(
            ((grad_attended, other_grad), (delta_features, other_delta), (query_features, other_features))
        )
    ]
    for exchange in exchanges:
        exchange.start()

    for part in range(2):
        keys_t[part] = jnp.transpose(keys[part])

    def own_queries(pair, carry):
        lanes = pl.ds(pl.multiple_of(pair * 128, 128), 128)
        query_pair, grad_pair = queries[0, :, lanes], grad_attended[:, lanes]
        pair_lane = lane_iota(query_pair.shape)
        grad_k = jnp.zeros((tokens, 128), F32)
        grad_v = jnp.zeros((tokens, 128), F32)
        for half in range(2):
            head = pair * 2 + half
            head_rows = pl.ds(pl.multiple_of(head * 64, 64), 64)
            mine = (pair_lane < 64) == (half == 0)
            query = jnp.where(mine, query_pair, jnp.zeros_like(query_pair))
            grad = jnp.where(mine, grad_pair, jnp.zeros_like(grad_pair))
            right_scores = jnp.concatenate([query, query_features[...]], axis=1)
            right_grads = jnp.concatenate([grad, delta_features[...]], axis=1)
            head_lanes = (pair_lane >= 3 * head) & (pair_lane < 3 * head + 3)
            grad_q = jnp.zeros((64, tokens), F32)
            for part in range(2):
                features = jnp.where(head_lanes, jnp.full_like(query_pair, -1.0), key_features[part])
                scores = dot_nt(jnp.concatenate([keys[part, :, lanes], features], axis=1), right_scores)
                weights = jnp.exp(scores)
                grad_weights = dot_nt(jnp.concatenate([values[part, :, lanes], features], axis=1), right_grads)
                grad_scores = (weights * grad_weights).astype(BF16)
                if part == 0:
                    grad_v = grad_v + dot(weights.astype(BF16), grad)
                    grad_k = grad_k + dot(grad_scores, query)
                grad_q = grad_q + dot(keys_t[part, head_rows, :], grad_scores)
            grad_query_t[head_rows, :] = grad_q
        grad_key[:, lanes] = grad_k
        grad_value[:, lanes] = grad_v
        return carry

    lax.fori_loop(0, HEADS // 2, own_queries, 0)
    for exchange in exchanges:
        exchange.wait_recv()

    def other_queries(pair, carry):
        lanes = pl.ds(pl.multiple_of(pair * 128, 128), 128)
        query_pair, grad_pair = queries[1, :, lanes], other_grad[:, lanes]
        pair_lane = lane_iota(query_pair.shape)
        grad_k = grad_key[:, lanes]
        grad_v = grad_value[:, lanes]
        for half in range(2):
            head = pair * 2 + half
            mine = (pair_lane < 64) == (half == 0)
            query = jnp.where(mine, query_pair, jnp.zeros_like(query_pair))
            grad = jnp.where(mine, grad_pair, jnp.zeros_like(grad_pair))
            head_lanes = (pair_lane >= 3 * head) & (pair_lane < 3 * head + 3)
            features = jnp.where(head_lanes, jnp.full_like(query_pair, -1.0), key_features[0])
            scores = dot_nt(
                jnp.concatenate([keys[0, :, lanes], features], axis=1),
                jnp.concatenate([query, other_features[...]], axis=1),
            )
            weights = jnp.exp(scores)
            grad_weights = dot_nt(
                jnp.concatenate([values[0, :, lanes], features], axis=1),
                jnp.concatenate([grad, other_delta[...]], axis=1),
            )
            grad_scores = (weights * grad_weights).astype(BF16)
            grad_v = grad_v + dot(weights.astype(BF16), grad)
            grad_k = grad_k + dot(grad_scores, query)
        grad_key[:, lanes] = grad_k
        grad_value[:, lanes] = grad_v
        return carry

    lax.fori_loop(0, HEADS // 2, other_queries, 0)

    grad_normed[...] = jnp.transpose(grad_query_t[...])
    for number in range(blocks):
        rows = pl.ds(number * BLOCK, BLOCK)
        before = block_place(segments, lengths, seq * blocks + number)[1]
        cosine, sine = rotary_block(table, before)
        for pair in range(HEADS // 2):
            lanes = pl.ds(pair * 128, 128)
            grad_triple[rows, lanes] = (turn(grad_normed[rows, lanes], cosine, -sine) * 0.125).astype(BF16)
            grad_triple[rows, pl.ds(width + pair * 128, 128)] = turn(grad_key[rows, lanes], cosine, -sine).astype(BF16)
        grad_triple[rows, pl.ds(2 * width, width)] = grad_value[rows, :].astype(BF16)

    for part in range(2):
        triple_t = dot_tn(grad_triple[:, pl.ds(part * 1152, 1152)], normed[...]).astype(BF16)
        for group in range(8):
            for side in range(2):
                triple_part[part * 8 + group, side] = triple_t[
                    group * 144 : group * 144 + 144, side * LANES : side * LANES + LANES
                ]
    grad_normed[...] = jnp.zeros_like(grad_normed)
    for first in range(0, 3 * width, width):
        lanes = pl.ds(first, width)
        grad_normed[...] += dot_nt(grad_triple[:, lanes], weight[:, lanes])

    small[...] = small_in[...]
    gain_sum = jnp.zeros((1, width), F32)
    for number in range(blocks):
        rows, one = pl.ds(number * BLOCK, BLOCK), pl.ds(number, 1)
        value = hidden[rows, :].astype(F32)
        centered = value - mean_of(value)
        inverse = lax.rsqrt(mean_of(centered * centered) + 1e-05)
        normal = centered * inverse
        grad = grad_normed[rows, :]
        mod_rows[one, pl.ds(0, width)] = jnp.sum(grad, axis=0, keepdims=True)
        mod_rows[one, pl.ds(width, width)] = jnp.sum(grad * (normal * first_gain[...]), axis=0, keepdims=True)
        mod_rows[one, pl.ds(2 * width, 4 * width)] = mod_grads[one, :]
        grad_line = grad * (1.0 + modulation[one, pl.ds(width, width)])
        gain_sum = gain_sum + jnp.sum(grad_line * normal, axis=0, keepdims=True)
        grad_normal = grad_line * first_gain[...]
        along = mean_of(grad_normal * normal)
        term = (grad_normal - mean_of(grad_normal) - normal * along) * inverse
        input_grad[rows, :] = (grad_middle[rows, :] + term).astype(BF16)
    small[pl.ds(FIRST_GAIN, 1), :] = gain_sum
    for part in range(6):
        small[pl.ds(MOD_BIAS + part, 1), :] = jnp.sum(mod_rows[:, pl.ds(part * width, width)], axis=0, keepdims=True)
    for exchange in exchanges:
        exchange.wait_send()


def backward(*args):
    hidden = args[2]
    tokens, width = hidden.shape
    smem, vmem = pl.BlockSpec(memory_space=pltpu.SMEM), pl.BlockSpec(memory_space=pltpu.VMEM)
    groups = 2**GROUP_BITS
    half = (tokens, width)
    return pl.pallas_call(
        backward_kernel,
        out_shape=(
            jax.ShapeDtypeStruct(half, BF16),
            jax.ShapeDtypeStruct((SMALL_ROWS, width), F32),
            jax.ShapeDtypeStruct((groups, 2, 3 * width // groups, LANES), BF16),
            jax.ShapeDtypeStruct((tokens // BLOCK, 6 * width), F32),
        ),
        in_specs=[smem] * 2 + [vmem] * (len(args) - 2),
        out_specs=(vmem,) * 4,
        scratch_shapes=[
            pltpu.VMEM(half, BF16),
            pltpu.VMEM((tokens, 128), BF16),
            pltpu.VMEM((tokens, 128), BF16),
            pltpu.VMEM((2, width, tokens), BF16),
            pltpu.VMEM((width, tokens), F32),
            pltpu.VMEM(half, F32),
            pltpu.VMEM(half, F32),
            pltpu.VMEM((tokens, 3 * width), BF16),
            pltpu.VMEM(half, F32),
            pltpu.SemaphoreType.DMA((3,)),
            pltpu.SemaphoreType.DMA((3,)),
        ],
        compiler_params=pltpu.CompilerParams(
            collective_id=2, has_side_effects=True, vmem_limit_bytes=58 << 20
        ),
    )(*args)


Z2, Z1, Y, CORE, X = 0, 1, 2, 3, 4


def exchange_partner(axis, extra_bits):
    dp, seq = lax.axis_index("dp"), lax.axis_index("seq")
    if axis == X:
        return (dp, 1 - seq)
    return (dp ^ (1 << (GROUP_BITS - 1 - axis + extra_bits)), seq)


def own_bit(axis, extra_bits):
    if axis == X:
        return lax.axis_index("seq")
    return (lax.axis_index("dp") >> (GROUP_BITS - 1 - axis + extra_bits)) & 1


def reduce_tasks(rows):
    streams = (
        (0, 112, (CORE, X, Y, Z1, Z2)),
        (224, 112, (CORE, Y, Z1, X, Z2)),
        (448, 96, (CORE, Z1, X, Y, Z2)),
        (112, 112, (CORE, X, Y, Z1, Z2)),
        (336, 112, (CORE, Y, Z1, X, Z2)),
        (544, 80, (CORE, Z1, X, Y, Z2)),
    )
    return streams


def reduce_kernel(extra_bits, all_bits, parts_ref, small_ref, sum_ref, small_out, acc, got_a, got_b, got_c, got_d, got_e, small_acc, small_got, local_sem, send_sem, recv_sem, small_send, small_recv):
    tasks = reduce_tasks(parts_ref.shape[-2])
    got = (got_a, got_b, got_c, got_d, got_e)
    bits = [own_bit(axis, extra_bits) for axis in range(5)]
    small_partners = [(lax.axis_index("dp"), 1 - lax.axis_index("seq"))] + [
        (lax.axis_index("dp") ^ (1 << bit), lax.axis_index("seq")) for bit in range(all_bits)
    ]
    barrier = pltpu.get_barrier_semaphore()
    for partner in small_partners:
        pl.semaphore_signal(barrier, inc=1, device_id=partner, device_id_type=MESH_ID)
    pl.semaphore_wait(barrier, len(small_partners))

    def region(order, stage, other):
        index = [slice(None)] * 5
        for axis in order[:stage]:
            index[axis] = bits[axis]
        index[order[stage]] = 1 - bits[order[stage]] if other else bits[order[stage]]
        return index

    copies = {}
    local_copies = []
    for number, (first, count, order) in enumerate(tasks):
        keep = pltpu.make_async_copy(
            parts_ref.at[tuple(region(order, 0, False)) + (pl.ds(first, count),)],
            acc.at[:, :, :, :, pl.ds(first, count)],
            local_sem.at[number],
        )
        keep.start()
        local_copies.append(keep)

    def send(number, stage):
        first, count, order = tasks[number]
        index = region(order, stage, True)
        if stage == 0:
            source = parts_ref.at[tuple(index) + (pl.ds(first, count),)]
        else:
            del index[CORE]
            source = acc.at[tuple(index) + (pl.ds(first, count),)]
        target = got[stage].at[(slice(None),) * (4 - stage) + (pl.ds(first, count),)]
        copy = pltpu.make_async_remote_copy(
            source, target, send_sem.at[number, stage], recv_sem.at[number, stage],
            device_id=exchange_partner(order[stage], extra_bits), device_id_type=MESH_ID,
        )
        copy.start()
        copies[number, stage] = copy

    def add(number, stage):
        first, count, order = tasks[number]
        copies[number, stage].wait_recv()
        if stage == 0:
            local_copies[number].wait()
        free = [axis for axis in range(5) if axis not in order[: stage + 1]]

        def one(step, carry):
            index = list(bits)
            got_index = []
            for place, axis in enumerate(free):
                index[axis] = (step >> (len(free) - 1 - place)) & 1
                got_index.append(index[axis])
            del index[CORE]
            rows = pl.ds(first, count)
            mine = acc[tuple(index) + (rows,)].astype(jnp.float32)
            total = mine + got[stage][tuple(got_index) + (rows,)].astype(jnp.float32)
            if stage == 4:
                sum_ref[rows] = total
            else:
                acc[tuple(index) + (rows,)] = total.astype(jnp.bfloat16)
            return carry

        if free:
            lax.fori_loop(0, 2 ** len(free), one, 0)
        else:
            one(0, 0)

    small_copies = []

    def small_send_step(step):
        copy = pltpu.make_async_remote_copy(
            small_acc.at[step], small_got.at[step], small_send.at[step], small_recv.at[step],
            device_id=small_partners[step], device_id_type=MESH_ID,
        )
        copy.start()
        small_copies.append(copy)

    def small_add(step):
        small_copies[step].wait_recv()
        small_acc[step + 1] = small_acc[step] + small_got[step]

    small_acc[0] = small_ref[...]
    for number in range(len(tasks)):
        send(number, 0)
    small_send_step(0)
    for stage in range(1, 5):
        for number in range(len(tasks)):
            add(number, stage - 1)
            send(number, stage)
        small_add(stage - 1)
        small_send_step(stage)
    for number in range(len(tasks)):
        add(number, 4)
    for step in range(4, len(small_partners)):
        small_add(step)
        if step + 1 < len(small_partners):
            small_send_step(step + 1)
    small_out[...] = small_acc[len(small_partners)]
    for copy in copies.values():
        copy.wait_send()
    for copy in small_copies:
        copy.wait_send()


def reduce_everywhere(parts, small):
    dp_size = lax.axis_size("dp")
    all_bits = dp_size.bit_length() - 1
    extra_bits = all_bits - GROUP_BITS
    rows = parts.shape[2]
    parts = parts.reshape((2,) * 5 + parts.shape[2:])
    task_count = len(reduce_tasks(rows))
    steps = all_bits + 1
    bf16 = jnp.bfloat16
    got_shapes = [pltpu.VMEM((2,) * (4 - stage) + (rows, LANES), bf16) for stage in range(5)]
    return pl.pallas_call(
        lambda *refs: reduce_kernel(extra_bits, all_bits, *refs),
        out_shape=(
            jax.ShapeDtypeStruct((rows, LANES), jnp.float32),
            jax.ShapeDtypeStruct(small.shape, jnp.float32),
        ),
        in_specs=[pl.BlockSpec(memory_space=pl.ANY), pl.BlockSpec(memory_space=pltpu.VMEM)],
        out_specs=(pl.BlockSpec(memory_space=pltpu.VMEM), pl.BlockSpec(memory_space=pltpu.VMEM)),
        scratch_shapes=[pltpu.VMEM((2, 2, 2, 2, rows, LANES), bf16)] + got_shapes + [
            pltpu.VMEM((steps + 1,) + small.shape, jnp.float32),
            pltpu.VMEM((steps,) + small.shape, jnp.float32),
            pltpu.SemaphoreType.DMA((task_count,)),
            pltpu.SemaphoreType.DMA((task_count, 5)),
            pltpu.SemaphoreType.DMA((task_count, 5)),
            pltpu.SemaphoreType.DMA((steps,)),
            pltpu.SemaphoreType.DMA((steps,)),
        ],
        compiler_params=pltpu.CompilerParams(
            collective_id=0, has_side_effects=True, vmem_limit_bytes=48 << 20
        ),
    )(parts, small)


def scatter_rest(block, dp_size):
    group = dp_size >> GROUP_BITS
    if group == 1:
        return block
    groups = [[first * group + place for place in range(group)] for first in range(dp_size // group)]
    return lax.psum_scatter(block, "dp", scatter_dimension=0, axis_index_groups=groups, tiled=True)


def local(
    hidden_in,
    segment_ids,
    piece_lengths,
    time_index,
    first_gain,
    modulation_weight,
    modulation_bias,
    query_key_value_weight,
    attention_output_matrix,
    second_gain,
    widen_weight,
    expand_bias,
    narrow_weight,
    reduce_bias,
    cotangent,
):
    slot_count, own_rows, width = hidden_in.shape
    hidden, cot = hidden_in[0], cotangent[0]
    table = jnp.asarray(angle_table())
    gain_one, gain_two = first_gain[None, :], second_gain[None, :]
    normed, queries, keys, values, attended, query_features, key_features, modulation, condition = forward(
        segment_ids, piece_lengths, time_index, hidden, table, gain_one, modulation_weight,
        modulation_bias[None, :], query_key_value_weight,
    )
    block_out, grad_middle, grad_attended, delta_features, mod_grads, small, expand_part, reduce_part, output_part = mlp(
        segment_ids, piece_lengths, hidden, attended, cot, modulation, gain_two, expand_bias[None, :],
        reduce_bias[None, :], attention_output_matrix, widen_weight, narrow_weight,
    )
    input_grad, small, triple_part, mod_rows = backward(
        segment_ids, piece_lengths, hidden, normed, queries, keys, values, query_features, key_features,
        grad_attended, delta_features, grad_middle, modulation, mod_grads, small, table, gain_one,
        query_key_value_weight,
    )
    groups = 2**GROUP_BITS
    own_condition = condition[: own_rows // BLOCK]
    mod_weight_grad = jnp.einsum("bc,bf->fc", own_condition, mod_rows, precision=lax.Precision.HIGHEST)
    mod_part = mod_weight_grad.astype(BF16).reshape(groups, 6, -1, 2, LANES // 6)
    mod_part = mod_part.transpose(0, 3, 2, 1, 4).reshape(groups, 2, -1, LANES)
    reduce_part = reduce_part.reshape(groups, 2, -1, LANES)
    parts = jnp.concatenate([expand_part, reduce_part, output_part, triple_part, mod_part], axis=2)
    block_sum, small_sum = reduce_everywhere(parts, small)
    dp_size = lax.axis_size("dp")
    cuts = []
    cursor = 0
    for part in (expand_part, reduce_part, output_part, triple_part, mod_part):
        cuts.append(block_sum[cursor : cursor + part.shape[2]])
        cursor = cursor + part.shape[2]
    expand_block = scatter_rest(cuts[0], dp_size).T
    reduce_block = cuts[1].reshape(4, -1, LANES).transpose(1, 0, 2).reshape(-1, 4 * LANES)
    reduce_block = scatter_rest(reduce_block, dp_size).T
    output_block = scatter_rest(cuts[2], dp_size).T
    triple_block = scatter_rest(cuts[3], dp_size).T
    mod_block = cuts[4].reshape(-1, 6, LANES // 6).transpose(1, 0, 2).reshape(-1, LANES // 6)
    mod_block = scatter_rest(mod_block, dp_size).T
    stats = small_sum[STATS]
    return (
        block_out[None],
        input_grad[None],
        small_sum[FIRST_GAIN],
        mod_block,
        small_sum[MOD_BIAS : MOD_BIAS + 6].reshape(-1),
        triple_block,
        output_block,
        small_sum[SECOND_GAIN],
        expand_block,
        small_sum[EXPAND_BIAS : EXPAND_BIAS + 4].reshape(-1),
        reduce_block,
        small_sum[REDUCE_BIAS],
        jnp.sqrt(stats[:3] / (stats[3] * width)),
    )


def solution(mesh):
    in_specs = (
        P("dp", "seq", None),
        P("dp", None),
        P("dp", None),
        P("dp", None),
        P(),
        P(),
        P(),
        P(),
        P(),
        P(),
        P(),
        P(),
        P(),
        P(),
        P("dp", "seq", None),
    )
    out_specs = (
        P("dp", "seq", None),
        P("dp", "seq", None),
        P(),
        P("seq", "dp"),
        P(),
        P("seq", "dp"),
        P("seq", "dp"),
        P(),
        P("seq", "dp"),
        P(),
        P("seq", "dp"),
        P(),
        P(),
    )
    return jax.shard_map(local, mesh=mesh, in_specs=in_specs, out_specs=out_specs, check_vma=False)
```

time: 476 us -> 241 us (0.51)
  matrix products: 140 us -> 3.84 us
  Pallas kernels: 81.3 us -> 200 us
  local copies, waits for them, and re-layouts: 139 us -> 30.6 us
  other arithmetic: 72.3 us -> 0.53 us
  waiting for transfers between devices: 19.4 us -> 0 us
  between operations: 15.7 us -> 1.7 us
    dot_general x21 -> x1, matrix products: 140 us -> 3.84 us  [local(): jnp.einsum('bc,bf->fc', own_condition, mod_rows, precision=lax.Precision....]
    pallas_call x0 -> x3, Pallas kernels: none -> 120 us  [the longest x1 46.7 us: backward(): pl.pallas_call(backward_kernel, out_shape=(jax.ShapeDtypeStruct(half, BF1...]
    reshape x11 -> x4, local copies, waits for them, and re-layouts: 59.4 us -> 5.23 us  [the longest x2 4.01 us: local(): mod_weight_grad.astype(BF16).reshape(groups, 6, -1, 2, LANES // 6)]
    convert_element_type x3 -> x0, other arithmetic: 24.2 us -> none  [the longest x1 17.8 us: attend_back(): grad_scores = (probability * (grad_prob - row_delta)).astype(jnp.bfloat16)]
    reduce_sum x11 -> x0, other arithmetic: 20.3 us -> none  [the longest x1 11.8 us: attend(): row_total = jnp.sum(exponent, axis=-1, keepdims=True)]
    all_gather x2 -> x0, waiting for transfers between devices: 19.3 us -> none  [the longest x1 19.3 us: local(): lax.all_gather(key_rot, 'seq', axis=1, tiled=True)]
    unnamed x180 -> x26, local copies, waits for them, and re-layouts: 28.5 us -> 12 us
    mul x4 -> x0, local copies, waits for them, and re-layouts: 9.8 us -> none  [rotate(): return values * cosine + turned * sine_part]
  transfers between devices with their start and end apart: 4 -> 0, of which waited for: 1 -> 0; matrix products, arithmetic and copies ran while one was open for 28% -> 0% of each run, Pallas kernels for 0% -> 0%
where the time goes in v2:
time: 241 us; the launch traced here: 237 us
  Pallas kernels  200 us (83%)
  local copies, waits for them, and re-layouts  30.6 us (13%)
  matrix products  3.84 us (2%)
    pallas_call x1, Pallas kernels, reduce_everywhere(): pl.pallas_call(lambda *refs: reduce_kernel(extra_bits, all_bits, *refs),...  80.3 us
    pallas_call x1, Pallas kernels, backward(): pl.pallas_call(backward_kernel, out_shape=(jax.ShapeDtypeStruct(half, BF1...  46.7 us
    pallas_call x1, Pallas kernels, forward(): pl.pallas_call(forward_kernel, out_shape=(half, both, both, both, half, j...  37.5 us
    pallas_call x1, Pallas kernels, mlp(): pl.pallas_call(mlp_kernel, out_shape=(jax.ShapeDtypeStruct(half, BF16), j...  35.9 us
    unnamed x26, local copies, waits for them, and re-layouts  12 us
    concatenate x2, local copies, waits for them, and re-layouts, local(): jnp.concatenate([expand_part, reduce_part, output_part, triple_part, mod_...  5.43 us

profile of v2, /device:TPU:0, one launch (start us, length us, event | category | flops | bytes accessed | tf_op | source)
XLA Modules:
  0.0 237.1 jit_solution(1297090654452255839)
XLA Ops:
  0.6 0.0 copy-start.8
  0.7 0.0 copy-start.9
  0.7 1.3 broadcast_in_dim.21.first_gain
  1.9 1.3 broadcast_in_dim.22.mod_bias
  3.3 37.5 %shard_map.255 = (bf16[512,768]{1,0:T(8,128)(2,1)}, bf16[2,512,768]{2,1,0:T(8,128)(2,1)}, bf16[2,512,768]{2,1,0:T(8,128)(2,1)}, bf16[2,512,768]{2,1,0:T(8,128)(2...) custom-call(s32[1,1024]{1,0:T(1,128)} %segments.5, ...), custom_call_target="tpu_custom_call" | custom-call | tf_op jit(solution)/shard_map/pallas_call | solution.py:222
  40.8 0.0 copy-done.8
  40.8 0.6 broadcast_in_dim.23.second_gain
  41.4 0.0 copy-done.9
  41.4 0.6 broadcast_in_dim.25.reduce_bias
  42.0 35.9 %shard_map.256 = (bf16[512,768]{1,0:T(8,128)(2,1)}, f32[512,768]{1,0:T(8,128)}, bf16[512,768]{1,0:T(8,128)(2,1)}, bf16[512,128]{1,0:T(8,128)(2,1)}, f32[4,3072]{...) custom-call(s32[1,1024]{1,0:T(1,128)} %segments.5, ...), custom_call_target="tpu_custom_call" | custom-call | tf_op jit(solution)/shard_map/pallas_call | solution.py:449
  77.9 0.0 copy-start.2
  77.9 46.7 %shard_map.257 = (bf16[512,768]{1,0:T(8,128)(2,1)}, f32[16,768]{1,0:T(8,128)}, bf16[16,2,144,384]{3,2,1,0:T(8,128)(2,1)}, f32[4,4608]{1,0:T(4,128)}) custom-call(s32[1,1024]{1,0:T(1,128)} %segments.5, s32[1,8]{1,0:T(1,128)} %lengths.5, bf16[512,768]{1,0:T(8,128)(2,1)} %bitcast.36, bf16[512,768]{1,0:T(8,128)(2,1)} %get-tuple-element.40.normed, ...), custom_call_target="tpu_custom_call" | custom-call | tf_op jit(solution)/shard_map/pallas_call | solution.py:637
  124.6 0.0 copy-done.2
  124.6 0.0 copy-start.1
  124.6 3.1 %constant_dynamic-update-slice_fusion.4 = bf16[2,2,2,2,2,624,384]{6,5,4,3,2,1,0:T(8,128)(2,1)} fusion(bf16[2,2,2,2,2,192,384]{6,5,4,3,2,1,0:T(8,128)(2,1)S(1)} %bitcast.38), kind=kLoop, calls=%fused_computation.9 | loop fusion | bytes 9437184
  127.7 1.0 copy-done.1
  128.7 0.0 copy-start.4
  128.7 0.0 copy-start.3
  128.7 2.9 %constant_dynamic-update-slice_fusion.3 = bf16[2,2,2,2,2,624,384]{6,5,4,3,2,1,0:T(8,128)(2,1)} fusion(bf16[2,2,2,2,2,624,384]{6,5,4,3,2,1,0:T(8,128)(2,1)} %constant_dynamic-update-slice_fusion.4, bf16[2,2,2,2,2,192,384]{6,5,4,3,2,1,0:T(8,128)(2,1)S(1)} %bitcast.37), kind=kLoop, calls=%fused_computation.8 | loop fusion | bytes 9437184
  131.6 0.0 copy-done.4
  131.6 0.0 copy-start.6
  131.6 0.0 copy-start.7
  131.6 1.2 constant_dynamic-update-slice_fusion.2
  132.8 0.1 copy-done.3
  132.8 2.2 constant_dynamic-update-slice_fusion.1
  135.0 0.0 copy-done.6
  135.0 0.0 copy-done.7
  135.0 3.8 %convolution_convert_fusion = bf16[4608,128]{1,0:T(8,128)(2,1)S(1)} fusion(f32[4,4608]{1,0:T(4,128)S(1)} %copy-done.6, f32[8,128]{1,0:T(8,128)S(1)} %copy-done.7), kind=kOutput, calls=%fused_computation | convolution fusion | flops 28901376 | bytes 1255424 | tf_op jit(solution)/shard_map/bc,bf->fc/dot_general | solution.py:882
  138.9 1.3 reshape.65
  140.2 2.7 %copy.38 = bf16[16,6,48,2,64]{4,1,2,3,0:T(8,128)(2,1)} copy(bf16[16,6,48,2,64]{4,3,2,1,0:T(2,128)(2,1)S(1)} %reshape.65) | data formatting | bytes 2359296 | tf_op jit(solution)/shard_map/reshape | solution.py:883
  142.9 0.0 copy-start
  142.9 4.2 %concatenate.18 = bf16[2,2,2,2,2,48,384]{6,5,4,3,2,1,0:T(8,128)(2,1)S(1)} reshape(bf16[16,2,48,6,64]{4,3,2,1,0:T(8,128)(2,1)} %bitcast.33) | data formatting | bytes 2359296 | tf_op jit(solution)/shard_map/concatenate | solution.py:886
  147.1 1.2 constant_dynamic-update-slice_fusion.refs_0_
  148.3 0.0 copy-done
  148.3 80.3 %shard_map.258 = (f32[624,384]{1,0:T(8,128)S(1)}, f32[16,768]{1,0:T(8,128)S(1)}) custom-call(bf16[2,2,2,2,2,624,384]{6,5,4,3,2,1,0:T(8,128)(2,1)} %constant_dynamic-update-slice_fusion.refs_0_, f32[16,768]{1,0:T(8,128)S(1)} %copy-done), custom_call_target="tpu_custom_call" | custom-call | tf_op jit(solution)/shard_map/pallas_call | solution.py:815
  228.6 0.6 slice_reduce_fusion
  229.2 0.6 slice_bitcast_fusion.2
  229.9 0.1 reshape.66
  230.0 0.8 copy.35
  230.8 0.6 reshape.68
  231.4 0.7 slice_bitcast_fusion.1
  232.1 0.8 fusion.1
  232.8 0.6 reshape.69
  233.4 0.7 copy.36
  234.2 0.6 slice.56
  235.4 0.5 sqrt_bitcast_fusion
  235.9 0.0 copy-done.5
  235.9 0.9 copy.44
  (4 shorter events, 0.0 us)
Async XLA Ops:
  0.6 40.2 %copy-start.8 = (f32[768]{0:T(1024)S(1)}, f32[768]{0:T(1024)}, u32[]{:S(2)}) copy-start(f32[768]{0:T(1024)} %param.25) | copy-start | bytes 9220
  0.7 40.8 %copy-start.9 = (f32[768]{0:T(1024)S(1)}, f32[768]{0:T(1024)}, u32[]{:S(2)}) copy-start(f32[768]{0:T(1024)} %param.29) | copy-start | bytes 9220
  77.9 46.7 %copy-start.2 = (bf16[16,2,192,384]{3,2,1,0:T(8,128)(2,1)S(1)}, bf16[16,2,192,384]{3,2,1,0:T(8,128)(2,1)}, u32[]{:S(2)}) copy-start(bf16[16,2,192,384]{3,2,1,0:T(8,128)(2,1)} %get-tuple-element.52) | copy-start | bytes 14155780
  124.6 4.0 %copy-start.1 = (bf16[16,2,4,48,384]{4,3,2,1,0:T(8,128)(2,1)S(1)}, bf16[16,2,4,48,384]{4,3,2,1,0:T(8,128)(2,1)}, u32[]{:S(2)}) copy-start(bf16[16,2,4,48,384]{4,3,2,1,0:T(8,128)(2,1)} %get-tuple-element.53) | copy-start | bytes 14155780
  128.7 2.9 %copy-start.4 = (bf16[16,2,48,384]{3,2,1,0:T(8,128)(2,1)S(1)}, bf16[16,2,48,384]{3,2,1,0:T(8,128)(2,1)}, u32[]{:S(2)}) copy-start(bf16[16,2,48,384]{3,2,1,0:T(8,128)(2,1)} %get-tuple-element.54) | copy-start | bytes 3538948
  128.7 4.2 %copy-start.3 = (bf16[16,2,144,384]{3,2,1,0:T(8,128)(2,1)S(1)}, bf16[16,2,144,384]{3,2,1,0:T(8,128)(2,1)}, u32[]{:S(2)}) copy-start(bf16[16,2,144,384]{3,2,1,0:T(8,128)(2,1)} %get-tuple-element.55) | copy-start | bytes 10616836
  131.6 3.4 %copy-start.6 = (f32[4,4608]{1,0:T(4,128)S(1)}, f32[4,4608]{1,0:T(4,128)}, u32[]{:S(2)}) copy-start(f32[4,4608]{1,0:T(4,128)} %get-tuple-element.56) | copy-start | bytes 221188
  131.6 3.4 %copy-start.7 = (f32[8,128]{1,0:T(8,128)S(1)}, f32[8,128]{1,0:T(8,128)}, u32[]{:S(2)}) copy-start(f32[8,128]{1,0:T(8,128)} %get-tuple-element.57) | copy-start | bytes 12292
  142.9 5.4 %copy-start = (f32[16,768]{1,0:T(8,128)S(1)}, f32[16,768]{1,0:T(8,128)}, u32[]{:S(2)}) copy-start(f32[16,768]{1,0:T(8,128)} %get-tuple-element.58.refs_1_) | copy-start | bytes 147460
  148.3 87.6 %copy-start.5 = (bf16[512,768]{1,0:T(8,128)(2,1)S(1)}, bf16[512,768]{1,0:T(8,128)(2,1)}, u32[]{:S(2)}) copy-start(bf16[512,768]{1,0:T(8,128)(2,1)} %get-tuple-element.51) | copy-start | bytes 2359300

commit v3 on v2

v3 whole, which is shorter than its diff:
```python
import functools
import math

import jax
import jax.numpy as jnp
import numpy as np
from jax import lax
from jax.experimental import pallas as pl
from jax.experimental.pallas import tpu as pltpu
from jax.sharding import PartitionSpec as P

HEADS = 12
BLOCK = 128
MAX_SEQUENCES = 8
SEGMENT_LANE = 40
MASKED = -1000000000.0
LANES = 384
GROUP_BITS = 4
MESH_ID = pl.DeviceIdType.MESH
F32, BF16 = jnp.float32, jnp.bfloat16

ROTARY_COS, ROTARY_SIN, BLOCK_COS, BLOCK_SIN = 0, 128, 256, 264
HIGH_COS, HIGH_SIN, LOW_COS, LOW_SIN, TABLE_ROWS = 272, 304, 336, 368, 400

FIRST_GAIN, MOD_BIAS, SECOND_GAIN, EXPAND_BIAS, REDUCE_BIAS, STATS, SMALL_ROWS = 0, 1, 7, 8, 12, 13, 16


def angle_table():
    lane = np.arange(128)
    rotary = np.exp((lane % 32) * (-2.0 * math.log(10000.0) / 64))
    timing = np.exp((lane % 64) * (-math.log(10000.0) / 64))
    steps = np.arange(128)[:, None]
    angles = [
        (np.cos, steps * rotary), (np.sin, steps * rotary),
        (np.cos, steps[:8] * 128 * rotary), (np.sin, steps[:8] * 128 * rotary),
        (np.cos, steps[:32] * 32 * timing), (np.sin, steps[:32] * 32 * timing),
        (np.cos, steps[:32] * timing), (np.sin, steps[:32] * timing),
    ]
    return np.concatenate([fn(angle) for fn, angle in angles]).astype(np.float32)


def dot(left, right):
    return jnp.dot(left, right, preferred_element_type=F32)


def dot_nt(left, right):
    return lax.dot_general(left, right, (((1,), (1,)), ((), ())), preferred_element_type=F32)


def dot_tn(left, right):
    return lax.dot_general(left, right, (((0,), (0,)), ((), ())), preferred_element_type=F32)


def lane_iota(shape):
    return lax.broadcasted_iota(jnp.int32, shape, len(shape) - 1)


def row_iota(shape):
    return lax.broadcasted_iota(jnp.int32, shape, 0)


def block_place(segments, lengths, block):
    segment = segments[0, block * BLOCK]
    before = jnp.int32(0)
    for other in range(segments.shape[1] // BLOCK):
        same = (segments[0, other * BLOCK] == segment) & (other < block)
        before = before + jnp.where(same, 1, 0)
    return segment, before, lengths[0, segment] - before * BLOCK


def rotary_block(table, before):
    cos_row, sin_row = table[pl.ds(ROTARY_COS, 128), :], table[pl.ds(ROTARY_SIN, 128), :]
    cos_block = table[pl.ds(BLOCK_COS + before, 1), :]
    sin_block = table[pl.ds(BLOCK_SIN + before, 1), :]
    cosine = cos_row * cos_block - sin_row * sin_block
    sine = sin_row * cos_block + cos_row * sin_block
    first_half = lane_iota(sine.shape) % 64 < 32
    return cosine, jnp.where(first_half, -sine, sine)


def turn(values, cosine, sine):
    first_half = lane_iota(values.shape) % 64 < 32
    swapped = jnp.where(first_half, pltpu.roll(values, 96, 1), pltpu.roll(values, 32, 1))
    return values * cosine + swapped * sine


def mean_of(values):
    return jnp.mean(values, axis=-1, keepdims=True)


def split_three(values):
    first = values.astype(BF16)
    rest = values - first.astype(F32)
    second = rest.astype(BF16)
    third = (rest - second.astype(F32)).astype(BF16)
    place = lane_iota(values.shape) % 3
    picked = jnp.where(place == 0, first.astype(F32), jnp.where(place == 1, second.astype(F32), third.astype(F32)))
    return picked.astype(BF16)


def forward_kernel(
    segments, lengths, times, hidden, table, first_gain, mod_weight, mod_bias, weight,
    normed, queries, keys, values, attended, query_features, key_features, modulation, condition,
    other_hidden, turned_values, out_t, peak, total, send_sem, recv_sem,
):
    tokens, width = hidden.shape
    blocks = tokens // BLOCK
    seq = lax.axis_index("seq")
    partner = (lax.axis_index("dp"), 1 - seq)
    barrier = pltpu.get_barrier_semaphore()
    pl.semaphore_signal(barrier, inc=1, device_id=partner, device_id_type=MESH_ID)
    pl.semaphore_wait(barrier, 1)
    exchange = pltpu.make_async_remote_copy(
        hidden, other_hidden, send_sem, recv_sem, device_id=partner, device_id_type=MESH_ID
    )
    exchange.start()

    places = []
    for number in range(2 * blocks):
        block = (seq if number < blocks else 1 - seq) * blocks + number % blocks
        places.append(block_place(segments, lengths, block))
        time = times[0, places[number][0]]
        high, low = time // 32, time % 32
        cos_high, sin_high = table[pl.ds(HIGH_COS + high, 1), :], table[pl.ds(HIGH_SIN + high, 1), :]
        cos_low, sin_low = table[pl.ds(LOW_COS + low, 1), :], table[pl.ds(LOW_SIN + low, 1), :]
        cosine = cos_high * cos_low - sin_high * sin_low
        sine = sin_high * cos_low + cos_high * sin_low
        row = jnp.where(lane_iota(cosine.shape) < 64, cosine, sine)
        condition[pl.ds(number, 1), :] = row.astype(BF16).astype(F32)
    modulation[...] = dot(condition[...].astype(BF16), mod_weight[...]) + mod_bias[...]

    lane = lane_iota((BLOCK, 128))
    row = row_iota((BLOCK, 128))

    for part in range(2):
        source = hidden if part == 0 else other_hidden
        if part == 1:
            exchange.wait_recv()
        turns = []
        for number in range(blocks):
            rows = pl.ds(number * BLOCK, BLOCK)
            segment, before, valid_count = places[part * blocks + number]
            turns.append(rotary_block(table, before))
            mine = lane == SEGMENT_LANE + segment
            in_lanes = (lane >= SEGMENT_LANE) & (lane < SEGMENT_LANE + MAX_SEQUENCES)
            blocked = in_lanes & jnp.logical_not(mine & (row < valid_count))
            key_features[part, rows, :] = jnp.where(blocked, MASKED, 0.0).astype(BF16)
            if part == 0:
                query_features[rows, :] = jnp.where(mine, 1.0, 0.0).astype(BF16)
            mod_row = pl.ds(part * blocks + number, 1)
            shift, scale = modulation[mod_row, pl.ds(0, width)], modulation[mod_row, pl.ds(width, width)]
            value = source[rows, :].astype(F32)
            centered = value - mean_of(value)
            spread = mean_of(centered * centered)
            line = centered * lax.rsqrt(spread + 1e-05) * first_gain[...]
            result = (line * (1.0 + scale) + shift).astype(BF16)
            if part == 0:
                normed[rows, :] = result
            else:
                other_hidden[rows, :] = result
        normed_source = normed if part == 0 else other_hidden
        for tile in range(3 * width // LANES):
            which, first = divmod(tile * LANES, width)
            product = dot(normed_source[...], weight[:, pl.ds(tile * LANES, LANES)])
            target = (queries, keys, values)[which]
            for number in range(blocks):
                cosine, sine = turns[number]
                for pair in range(LANES // 128):
                    piece = product[number * BLOCK : (number + 1) * BLOCK, pair * 128 : (pair + 1) * 128]
                    if which < 2:
                        piece = turn(piece, cosine, sine)
                    if which == 0:
                        piece = piece.astype(BF16).astype(F32) * 0.125
                    target[part, pl.ds(number * BLOCK, BLOCK), pl.ds(first + pair * 128, 128)] = piece.astype(BF16)
        turned_values[...] = jnp.transpose(values[part])

        def attend(pair, carry):
            lanes = pl.ds(pl.multiple_of(pair * 128, 128), 128)
            query_pair, key_pair = queries[0, :, lanes], keys[part, :, lanes]
            left = jnp.concatenate([key_pair, key_features[part]], axis=1)
            pair_lane = lane_iota(query_pair.shape)
            for half in range(2):
                head = pair * 2 + half
                head_rows = pl.ds(pl.multiple_of(head * 64, 64), 64)
                one_row = pl.ds(head, 1)
                query = jnp.where((pair_lane < 64) == (half == 0), query_pair, jnp.zeros_like(query_pair))
                scores = dot_nt(left, jnp.concatenate([query, query_features[...]], axis=1))
                top = jnp.max(scores, axis=0, keepdims=True)
                if part == 1:
                    top = jnp.maximum(top, peak[one_row, :])
                weights = jnp.exp(scores - top)
                summed = jnp.sum(weights, axis=0, keepdims=True)
                mixed = dot(turned_values[head_rows, :], weights.astype(BF16))
                if part == 0:
                    out_t[head_rows, :] = mixed
                    total[one_row, :] = summed
                    peak[one_row, :] = top
                else:
                    rescale = jnp.exp(peak[one_row, :] - top)
                    summed = summed + rescale * total[one_row, :]
                    out_t[head_rows, :] = (out_t[head_rows, :] * rescale + mixed) * (1.0 / summed)
                    peak[one_row, :] = top + jnp.log(summed)
            return carry

        lax.fori_loop(0, HEADS // 2, attend, 0)

    attended[...] = jnp.transpose(out_t[...].astype(BF16))
    log_rows = jnp.concatenate(
        [jnp.broadcast_to(peak[pl.ds(head, 1), :], (3, tokens)) for head in range(HEADS)]
        + [jnp.zeros((128 - 3 * HEADS, tokens), F32)], axis=0,
    )
    query_features[...] = query_features[...] + split_three(jnp.transpose(log_rows))
    exchange.wait_send()


def forward(segments, lengths, times, hidden, table, first_gain, mod_weight, mod_bias, weight):
    tokens, width = hidden.shape
    blocks = 2 * tokens // BLOCK
    half = jax.ShapeDtypeStruct((tokens, width), BF16)
    both = jax.ShapeDtypeStruct((2, tokens, width), BF16)
    smem, vmem = pl.BlockSpec(memory_space=pltpu.SMEM), pl.BlockSpec(memory_space=pltpu.VMEM)
    return pl.pallas_call(
        forward_kernel,
        out_shape=(
            half, both, both, both, half,
            jax.ShapeDtypeStruct((tokens, 128), BF16),
            jax.ShapeDtypeStruct((2, tokens, 128), BF16),
            jax.ShapeDtypeStruct((blocks, 6 * width), F32),
            jax.ShapeDtypeStruct((blocks, 128), F32),
        ),
        in_specs=[smem] * 3 + [vmem] * 6,
        out_specs=(vmem,) * 9,
        scratch_shapes=[
            pltpu.VMEM((tokens, width), BF16),
            pltpu.VMEM((width, tokens), BF16),
            pltpu.VMEM((width, tokens), F32),
            pltpu.VMEM((16, tokens), F32),
            pltpu.VMEM((16, tokens), F32),
            pltpu.SemaphoreType.DMA,
            pltpu.SemaphoreType.DMA,
        ],
        compiler_params=pltpu.CompilerParams(
            collective_id=1, has_side_effects=True, vmem_limit_bytes=56 << 20
        ),
    )(segments, lengths, times, hidden, table, first_gain, mod_weight, mod_bias, weight)


TILE = 384


def mlp_kernel(
    segments, lengths, hidden, attended, cotangent, modulation, second_gain, expand_bias, reduce_bias,
    out_weight_hbm, widen_hbm, narrow_hbm,
    block_out, grad_low, normed, normal, spread_row, projected, gate_grads, small, activated_hbm, slope_hbm,
    out_weight, widen, narrow, activated, slope, middle, reduced,
    load_sem, tile_sem, store_sem,
):
    tokens, width = hidden.shape
    tiles = widen.shape[1] // TILE
    blocks = tokens // BLOCK
    seq = lax.axis_index("seq")

    def tile_lanes(tile):
        return pl.ds(pl.multiple_of(tile * TILE, TILE), TILE)

    def tile_loads(tile):
        lanes = tile_lanes(tile)
        return (
            pltpu.make_async_copy(widen_hbm.at[:, lanes], widen.at[:, lanes], tile_sem.at[0, tile]),
            pltpu.make_async_copy(narrow_hbm.at[lanes], narrow.at[lanes], tile_sem.at[1, tile]),
        )

    first_load = pltpu.make_async_copy(out_weight_hbm, out_weight, load_sem)
    first_load.start()
    for tile in range(tiles):
        for load in tile_loads(tile):
            load.start()
    row = row_iota((BLOCK, 1))
    keep = []
    for number in range(blocks):
        valid_count = block_place(segments, lengths, seq * blocks + number)[2]
        keep.append(jnp.where(row < valid_count, 1.0, 0.0))

    def mod_part(number, part):
        return modulation[pl.ds(number, 1), pl.ds(part * width, width)]

    first_load.wait()
    for first in range(0, width, 256):
        lanes = pl.ds(first, 256)
        projected[:, lanes] = dot(attended[...], out_weight[:, lanes])
    branch_sum = jnp.zeros((1, width), F32)
    for number in range(blocks):
        rows = pl.ds(number * BLOCK, BLOCK)
        branch = mod_part(number, 2) * projected[rows, :]
        branch_sum = branch_sum + jnp.sum(keep[number] * branch * branch, axis=0, keepdims=True)
        value = hidden[rows, :].astype(F32) + branch
        middle[rows, :] = value
        centered = value - mean_of(value)
        inverse = lax.rsqrt(mean_of(centered * centered) + 1e-05)
        normal[rows, :] = centered * inverse
        spread_row[rows, :] = jnp.broadcast_to(inverse, (BLOCK, 128))
        line = normal[rows, :] * second_gain[...]
        normed[rows, :] = (line * (1.0 + mod_part(number, 4)) + mod_part(number, 3)).astype(BF16)

    reduced[...] = jnp.zeros_like(reduced)

    def stores(tile):
        return (
            pltpu.make_async_copy(activated.at[tile], activated_hbm.at[tile], store_sem.at[0, tile]),
            pltpu.make_async_copy(slope.at[tile], slope_hbm.at[tile], store_sem.at[1, tile]),
        )

    def ahead(tile):
        lanes = tile_lanes(tile)
        for load in tile_loads(tile):
            load.wait()
        u = dot(normed[...], widen[:, lanes]) + expand_bias[:, lanes]
        square = u * u
        tanh = jnp.tanh(u * (0.7978845608028654 + 0.7978845608028654 * 0.044715 * square))
        half_sum = 0.5 + 0.5 * tanh
        active = (u * half_sum).astype(BF16)
        inner = 0.7978845608028654 + 3.0 * 0.7978845608028654 * 0.044715 * square
        slope[tile] = (half_sum + (0.5 * u) * (1.0 - tanh * tanh) * inner).astype(BF16)
        activated[tile] = active
        reduced[...] += dot(active, narrow[lanes, :])
        for copy in stores(tile):
            copy.start()

    def ahead_two(step, carry):
        ahead(2 * step)
        ahead(2 * step + 1)
        return carry

    lax.fori_loop(0, tiles // 2, ahead_two, 0)

    value_sum = jnp.zeros((1, width), F32)
    mlp_sum = jnp.zeros((1, width), F32)
    bias_sum = jnp.zeros((1, width), F32)
    for number in range(blocks):
        rows = pl.ds(number * BLOCK, BLOCK)
        gate = mod_part(number, 5)
        full = reduced[rows, :] + reduce_bias[...]
        branch = gate * full
        value = middle[rows, :] + branch
        block_out[rows, :] = value.astype(BF16)
        value_sum = value_sum + jnp.sum(keep[number] * value * value, axis=0, keepdims=True)
        mlp_sum = mlp_sum + jnp.sum(keep[number] * branch * branch, axis=0, keepdims=True)
        grad_out = cotangent[rows, :].astype(F32) * keep[number]
        gate_grads[pl.ds(number, 1), :] = jnp.sum(grad_out * full, axis=0, keepdims=True)
        low = (gate * grad_out).astype(BF16)
        grad_low[rows, :] = low
        bias_sum = bias_sum + jnp.sum(low.astype(F32), axis=0, keepdims=True)
    small[...] = jnp.zeros_like(small)
    small[pl.ds(REDUCE_BIAS, 1), :] = bias_sum
    lane = lane_iota((1, width))
    counts = jnp.zeros((1, 1), F32)
    for number in range(blocks):
        counts = counts + jnp.sum(keep[number], axis=0, keepdims=True)
    sums = [jnp.sum(term, axis=1, keepdims=True) for term in (value_sum, branch_sum, mlp_sum)] + [counts]
    stats = jnp.zeros((1, width), F32)
    for place, term in enumerate(sums):
        stats = jnp.where(lane == place, term, stats)
    small[pl.ds(STATS, 1), :] = stats

    def drain(tile, carry):
        for copy in stores(tile):
            copy.wait()
        return carry

    lax.fori_loop(0, tiles, drain, 0)


def mlp(segments, lengths, hidden, attended, cotangent, modulation, second_gain, expand_bias, reduce_bias, out_weight, widen, narrow):
    tokens, width = hidden.shape
    tiles = widen.shape[1] // TILE
    smem, vmem = pl.BlockSpec(memory_space=pltpu.SMEM), pl.BlockSpec(memory_space=pltpu.VMEM)
    hbm = pl.BlockSpec(memory_space=pl.ANY)
    half, by_tile = (tokens, width), (tiles, tokens, TILE)
    return pl.pallas_call(
        mlp_kernel,
        out_shape=(
            jax.ShapeDtypeStruct(half, BF16),
            jax.ShapeDtypeStruct(half, BF16),
            jax.ShapeDtypeStruct(half, BF16),
            jax.ShapeDtypeStruct(half, F32),
            jax.ShapeDtypeStruct((tokens, 128), F32),
            jax.ShapeDtypeStruct(half, F32),
            jax.ShapeDtypeStruct((tokens // BLOCK, width), F32),
            jax.ShapeDtypeStruct((SMALL_ROWS, width), F32),
            jax.ShapeDtypeStruct(by_tile, BF16),
            jax.ShapeDtypeStruct(by_tile, BF16),
        ),
        in_specs=[smem] * 2 + [vmem] * 7 + [hbm] * 3,
        out_specs=(vmem,) * 8 + (hbm,) * 2,
        scratch_shapes=[
            pltpu.VMEM(out_weight.shape, BF16),
            pltpu.VMEM(widen.shape, BF16),
            pltpu.VMEM(narrow.shape, BF16),
            pltpu.VMEM(by_tile, BF16),
            pltpu.VMEM(by_tile, BF16),
            pltpu.VMEM(half, F32),
            pltpu.VMEM(half, F32),
            pltpu.SemaphoreType.DMA,
            pltpu.SemaphoreType.DMA((2, tiles)),
            pltpu.SemaphoreType.DMA((2, tiles)),
        ],
        compiler_params=pltpu.CompilerParams(vmem_limit_bytes=56 << 20),
    )(segments, lengths, hidden, attended, cotangent, modulation, second_gain, expand_bias, reduce_bias, out_weight, widen, narrow)


Z2, Z1, Y, CORE, X = 0, 1, 2, 3, 4


def exchange_partner(axis, extra_bits):
    dp, seq = lax.axis_index("dp"), lax.axis_index("seq")
    if axis == X:
        return (dp, 1 - seq)
    return (dp ^ (1 << (GROUP_BITS - 1 - axis + extra_bits)), seq)


def own_bit(axis, extra_bits):
    if axis == X:
        return lax.axis_index("seq")
    return (lax.axis_index("dp") >> (GROUP_BITS - 1 - axis + extra_bits)) & 1


class Stream:
    def __init__(self, kit, number, part, first, count, fixed, order, got, got_first=0):
        self.kit, self.number, self.part, self.first, self.count = kit, number, part, first, count
        self.fixed, self.order, self.got, self.got_first = fixed, order, got, got_first

    def free(self, stage):
        return [axis for axis in range(5) if axis not in self.fixed and axis not in self.order[: stage + 1]]

    def copy(self, stage):
        bits = self.kit["bits"]
        index = [slice(None)] * 5
        for axis, value in self.fixed.items():
            index[axis] = value
        for axis in self.order[:stage]:
            index[axis] = bits[axis]
        index[self.order[stage]] = 1 - bits[self.order[stage]]
        target = (slice(None),) * len(self.free(stage)) + (pl.ds(self.got_first, self.count),)
        return pltpu.make_async_remote_copy(
            self.part.at[tuple(index) + (pl.ds(self.first, self.count),)],
            self.got[stage].at[target],
            self.kit["send"].at[self.number, stage],
            self.kit["recv"].at[self.number, stage],
            device_id=exchange_partner(self.order[stage], self.kit["extra"]),
            device_id_type=MESH_ID,
        )

    def send(self, stage):
        self.copy(stage).start()

    def add(self, stage, total=None, total_first=0):
        self.copy(stage).wait_recv()
        bits, free = self.kit["bits"], self.free(stage)
        rows, got_rows = pl.ds(self.first, self.count), pl.ds(self.got_first, self.count)

        def one(step, carry):
            index = list(bits)
            for axis, value in self.fixed.items():
                index[axis] = value
            place = []
            for order, axis in enumerate(free):
                index[axis] = (step >> (len(free) - 1 - order)) & 1
                place.append(index[axis])
            mine, theirs = self.part[tuple(index) + (rows,)], self.got[stage][tuple(place) + (got_rows,)]
            if total is None:
                self.part[tuple(index) + (rows,)] = mine + theirs
            else:
                total[pl.ds(total_first, self.count), :] = mine.astype(F32) + theirs.astype(F32)
            return carry

        if free:
            lax.fori_loop(0, 2 ** len(free), one, 0)
        else:
            one(0, 0)

    def done(self):
        for stage in range(len(self.order)):
            self.copy(stage).wait_send()


def backward_kernel(
    extra_bits, all_bits,
    segments, lengths, modulation, gate_grads, small_in, condition, table, first_gain, second_gain,
    narrow_hbm, widen_hbm, out_weight_hbm, activated_hbm, slope_hbm, normed_two_hbm, grad_low_hbm, normal_hbm, spread_hbm,
    projected_hbm, attended_hbm, cotangent_hbm, queries_hbm, keys_hbm, values_hbm, query_features_hbm, key_features_hbm,
    normed_hbm, hidden_hbm, weight_hbm,
    input_grad, sums, mod_out, small_out,
    expand_part, reduce_part, output_part,
    expand_got, reduce_got, one_x, one_z, one_y, one_last, two_z, two_y, two_x, two_last, red_y, red_z, red_w, red_last,
    out_a, out_b, out_c, out_d, out_e, tri_a, tri_b, tri_c, tri_d, tri_e,
    queries, keys, values, query_features, key_features,
    grad_middle, grad_attended, delta_features, other_grad, other_delta, other_features, mod_rows,
    small_acc, small_got, mod_zero, mod_got, mod_one, mod_two, mod_three, mod_four, mod_five,
    cond_zero, cond_got, cond_one, cond_two, cond_three, cond_four, cond_five,
    load_sem, tile_sem, core_send, core_recv, stream_send, stream_recv, swap_send, swap_recv,
    small_send, small_recv, mod_send, mod_recv,
):
    tokens, width = input_grad.shape
    tiles = activated_hbm.shape[0]
    blocks = tokens // BLOCK
    seq = lax.axis_index("seq")
    dp = lax.axis_index("dp")
    bits = [own_bit(axis, extra_bits) for axis in range(5)]
    kit = {"bits": bits, "send": stream_send, "recv": stream_recv, "extra": extra_bits}
    core = bits[CORE]
    own = {axis: bits[axis] for axis in range(5)}

    def others(*axes):
        return {axis: bits[axis] for axis in range(5) if axis not in axes}

    one = [Stream(kit, v, expand_part, 0, 96, {CORE: core, Z2: v}, (X, Z1, Y), (one_x.at[v], one_z.at[v], one_y.at[v])) for v in range(2)]
    two = [Stream(kit, 2 + v, expand_part, 96, 96, {CORE: core, Z2: v}, (Z1, Y, X), (two_z.at[v], two_y.at[v], two_x.at[v])) for v in range(2)]
    red = [Stream(kit, 4 + v, reduce_part, 0, 192, {CORE: core, X: v}, (Y, Z1, Z2), (red_y.at[v], red_z.at[v], red_w.at[v])) for v in range(2)]
    one_merge = Stream(kit, 6, expand_part, 0, 96, others(Z2), (Z2,), (one_last,))
    two_merge = Stream(kit, 7, expand_part, 96, 96, others(Z2), (Z2,), (two_last,))
    red_merge = Stream(kit, 8, reduce_part, 0, 192, others(X), (X,), (red_last,))
    out = Stream(kit, 9, output_part, 0, 48, {}, (CORE, Y, X, Z1, Z2), (out_a, out_b, out_c, out_d, out_e))

    greet = [(dp, 1 - seq)] + [(dp ^ (1 << bit), seq) for bit in range(all_bits)]
    barrier = pltpu.get_barrier_semaphore()
    for partner in greet:
        pl.semaphore_signal(barrier, inc=1, device_id=partner, device_id_type=MESH_ID)

    attention_loads = [
        pltpu.make_async_copy(source, target, load_sem.at[number])
        for number, (source, target) in enumerate(
            ((queries_hbm, queries), (keys_hbm, keys), (values_hbm, values),
             (query_features_hbm, query_features), (key_features_hbm, key_features))
        )
    ]
    row = row_iota((BLOCK, 1))
    keep = []
    for number in range(blocks):
        valid_count = block_place(segments, lengths, seq * blocks + number)[2]
        keep.append(jnp.where(row < valid_count, 1.0, 0.0))

    def mod_part(number, part):
        return modulation[pl.ds(number, 1), pl.ds(part * width, width)]

    def tile_lanes(tile):
        return pl.ds(pl.multiple_of(tile * TILE, TILE), TILE)

    def core_copies(tile):
        at = (tile >> 2, (tile >> 1) & 1, tile & 1)
        rows = pl.ds(pl.multiple_of((tile & 3) * 48, 16), 48)
        everywhere = (slice(None),) * 3
        partner = exchange_partner(CORE, extra_bits)
        return (
            pltpu.make_async_remote_copy(
                expand_part.at[at + (1 - core,)], expand_got.at[at], core_send.at[0, tile], core_recv.at[0, tile],
                device_id=partner, device_id_type=MESH_ID,
            ),
            pltpu.make_async_remote_copy(
                reduce_part.at[everywhere + (1 - core, tile >> 2, rows)], reduce_got.at[everywhere + (tile >> 2, rows)],
                core_send.at[1, tile], core_recv.at[1, tile], device_id=partner, device_id_type=MESH_ID,
            ),
        )

    def core_add(tile):
        at = (tile >> 2, (tile >> 1) & 1, tile & 1)
        rows = pl.ds(pl.multiple_of((tile & 3) * 48, 16), 48)
        for copy in core_copies(tile):
            copy.wait_recv()
        for side in range(2):
            expand_part[at + (core, side)] = expand_part[at + (core, side)] + expand_got[at + (side,)]
        for z2 in range(2):
            for z1 in range(2):
                for y in range(2):
                    index, got = (z2, z1, y, core, tile >> 2, rows), (z2, z1, y, tile >> 2, rows)
                    reduce_part[index] = reduce_part[index] + reduce_got[got]

    def mlp_phase(
        narrow, widen, out_weight, activated, slope, normed_two, grad_low, grad_low_t, normal, spread_row, projected,
        attended, cotangent, bias_row, grad_normed,
    ):
        def tile_loads(tile):
            lanes = tile_lanes(tile)
            pairs = (
                (narrow_hbm.at[lanes], narrow.at[lanes]), (slope_hbm.at[tile], slope.at[tile]),
                (widen_hbm.at[:, lanes], widen.at[:, lanes]), (activated_hbm.at[tile], activated.at[tile]),
            )
            return [pltpu.make_async_copy(source, target, tile_sem.at[place, tile]) for place, (source, target) in enumerate(pairs)]

        loads = [
            pltpu.make_async_copy(source, target, load_sem.at[5 + number])
            for number, (source, target) in enumerate(
                ((grad_low_hbm, grad_low), (normed_two_hbm, normed_two), (normal_hbm, normal), (spread_hbm, spread_row),
                 (projected_hbm, projected), (attended_hbm, attended), (cotangent_hbm, cotangent), (out_weight_hbm, out_weight))
            )
        ]
        for load in loads[:2]:
            load.start()
        for tile in range(tiles):
            for load in tile_loads(tile):
                load.start()
        for load in loads[2:] + attention_loads:
            load.start()
        grad_normed[...] = jnp.zeros_like(grad_normed)
        loads[0].wait()
        grad_low_t[...] = jnp.transpose(grad_low[...])
        loads[1].wait()
        pl.semaphore_wait(barrier, len(greet))

        def back(tile):
            lanes = tile_lanes(tile)
            for load in tile_loads(tile):
                load.wait()
            grad_active = dot_nt(grad_low[...], narrow[lanes, :])
            grad_wide = (grad_active * slope[tile].astype(F32)).astype(BF16)
            bias_row[pl.ds(0, 1), lanes] = jnp.sum(grad_wide.astype(F32), axis=0, keepdims=True)
            grad_normed[...] += dot_nt(grad_wide, widen[:, lanes])
            expand_t = dot_tn(grad_wide, normed_two[...]).astype(BF16)
            at = (tile >> 2, (tile >> 1) & 1, tile & 1)
            for group in range(2):
                for side in range(2):
                    expand_part[at + (group, side)] = expand_t[
                        group * 192 : group * 192 + 192, side * LANES : side * LANES + LANES
                    ]
            reduce_t = dot(grad_low_t[...], activated[tile]).astype(BF16)
            rows = pl.ds(pl.multiple_of((tile & 3) * 48, 16), 48)
            reduce_part[:, :, :, :, tile >> 2, rows] = reduce_t.reshape(2, 2, 2, 2, 48, TILE)
            for copy in core_copies(tile):
                copy.start()

        def back_two(step, carry):
            back(2 * step)

            @pl.when(step > 0)
            def _():
                core_add(2 * step - 1)

            @pl.when(step == 2)
            def _():
                one[0].send(0)
                two[0].send(0)
                red[0].send(0)

            back(2 * step + 1)
            core_add(2 * step)
            return carry

        lax.fori_loop(0, tiles // 2, back_two, 0)
        core_add(tiles - 1)
        one[1].send(0)
        two[1].send(0)
        red[1].send(0)
        small_acc[0] = small_in[...]
        for part in range(tiles * TILE // width):
            small_acc[0, pl.ds(EXPAND_BIAS + part, 1), :] = bias_row[pl.ds(0, 1), pl.ds(part * width, width)]

        for load in loads[2:]:
            load.wait()
        gain_sum = jnp.zeros((1, width), F32)
        for number in range(blocks):
            rows = pl.ds(number * BLOCK, BLOCK)
            here = pl.ds(number, 1)
            grad = grad_normed[rows, :]
            line = normal[rows, :] * second_gain[...]
            mod_rows[here, pl.ds(3 * width, width)] = jnp.sum(grad, axis=0, keepdims=True)
            mod_rows[here, pl.ds(4 * width, width)] = jnp.sum(grad * line, axis=0, keepdims=True)
            mod_rows[here, pl.ds(5 * width, width)] = gate_grads[here, :]
            grad_line = grad * (1.0 + mod_part(number, 4))
            gain_sum = gain_sum + jnp.sum(grad_line * normal[rows, :], axis=0, keepdims=True)
            grad_normal = grad_line * second_gain[...]
            along = mean_of(grad_normal * normal[rows, :])
            term = (grad_normal - mean_of(grad_normal) - normal[rows, :] * along) * spread_row[rows, :1]
            total = cotangent[rows, :].astype(F32) * keep[number] + term
            grad_middle[rows, :] = total
            mod_rows[here, pl.ds(2 * width, width)] = jnp.sum(total * projected[rows, :], axis=0, keepdims=True)
            grad_low[rows, :] = (mod_part(number, 2) * total).astype(BF16)
        small_acc[0, pl.ds(SECOND_GAIN, 1), :] = gain_sum

        for first in range(0, width, 256):
            grad_attended[:, pl.ds(first, 256)] = dot_nt(
                grad_low[...], out_weight[pl.ds(first, 256), :]
            ).astype(BF16)
        head_lane = row_iota((width, 128)) // 64 == lane_iota((width, 128)) // 3
        chooser = jnp.where(head_lane & (lane_iota((width, 128)) < 3 * HEADS), 1.0, 0.0).astype(BF16)
        for number in range(blocks):
            rows = pl.ds(number * BLOCK, BLOCK)
            product = grad_attended[rows, :].astype(F32) * attended[rows, :].astype(F32)
            upper = product.astype(BF16)
            lower = (product - upper.astype(F32)).astype(BF16)
            delta_features[rows, :] = split_three(dot(upper, chooser) + dot(lower, chooser))
        for load in attention_loads:
            load.wait()
        for swap in swaps():
            swap.start()
        for first in range(0, width, TILE):
            output_t = dot_tn(grad_low[:, pl.ds(first, TILE)], attended[...]).astype(BF16)
            for place in range(TILE // 48):
                group = first // 48 + place
                at = (group >> 3, (group >> 2) & 1, (group >> 1) & 1, group & 1)
                for side in range(2):
                    output_part[at + (side,)] = output_t[
                        place * 48 : place * 48 + 48, side * LANES : side * LANES + LANES
                    ]
        out.send(0)

    def swaps():
        partner = (dp, 1 - seq)
        return [
            pltpu.make_async_remote_copy(
                source, target, swap_send.at[number], swap_recv.at[number], device_id=partner, device_id_type=MESH_ID
            )
            for number, (source, target) in enumerate(
                ((grad_attended, other_grad), (delta_features, other_delta), (query_features, other_features))
            )
        ]

    units = tiles * TILE
    pl.run_scoped(
        mlp_phase,
        pltpu.VMEM((units, width), BF16), pltpu.VMEM((width, units), BF16), pltpu.VMEM((width, width), BF16),
        pltpu.VMEM((tiles, tokens, TILE), BF16), pltpu.VMEM((tiles, tokens, TILE), BF16),
        pltpu.VMEM((tokens, width), BF16), pltpu.VMEM((tokens, width), BF16), pltpu.VMEM((width, tokens), BF16),
        pltpu.VMEM((tokens, width), F32), pltpu.VMEM((tokens, 128), F32), pltpu.VMEM((tokens, width), F32),
        pltpu.VMEM((tokens, width), BF16), pltpu.VMEM((tokens, width), BF16), pltpu.VMEM((8, units), F32),
        pltpu.VMEM((tokens, width), F32),
    )

    def step(stream, stage):
        stream.add(stage)
        stream.send(stage + 1)

    def after_all(streams, stage, merge):
        for stream in streams:
            stream.add(stage)
        merge.send(0)

    plan = {
        0: [(step, one[0], 0), (step, two[0], 0)],
        1: [(step, one[1], 0), (step, two[1], 0)],
        2: [(step, red[0], 0)],
        3: [(step, one[0], 1), (step, two[0], 1)],
        4: [(step, one[1], 1), (step, two[1], 1)],
        5: [(step, out, 0)],
        6: [(step, red[1], 0)],
        7: [(step, red[0], 1)],
        8: [(after_all, one, 2, one_merge)],
        9: [(after_all, two, 2, two_merge)],
        10: [(step, red[1], 1), (step, out, 1)],
        11: [],
        12: [(step, out, 2), (after_all, red, 2, red_merge)],
        13: [(one_merge.add, 0, sums, 0), (two_merge.add, 0, sums, 96)],
        14: [(step, out, 3)],
        15: [],
        16: [(red_merge.add, 0, sums, 192)],
        17: [(out.add, 4, sums, 384)],
    }

    def run_plan(pair, first, stride, count):
        for place in range(count):
            actions = plan[first + stride * place]
            if actions:

                @pl.when(pair == place)
                def _(actions=actions):
                    for action in actions:
                        action[0](*action[1:])

    def attention_phase(normed, hidden, weight, keys_t, grad_query_t, grad_key, grad_value, grad_triple, grad_normed, triple_part):
        loads = [
            pltpu.make_async_copy(source, target, load_sem.at[13 + number])
            for number, (source, target) in enumerate(((normed_hbm, normed), (hidden_hbm, hidden), (weight_hbm, weight)))
        ]
        for load in loads:
            load.start()
        for part in range(2):
            keys_t[part] = jnp.transpose(keys[part])

        def own_queries(pair, carry):
            lanes = pl.ds(pl.multiple_of(pair * 128, 128), 128)
            query_pair, grad_pair = queries[0, :, lanes], grad_attended[:, lanes]
            pair_lane = lane_iota(query_pair.shape)
            for half in range(2):
                head = pair * 2 + half
                head_rows = pl.ds(pl.multiple_of(head * 64, 64), 64)
                mine = (pair_lane < 64) == (half == 0)
                query = jnp.where(mine, query_pair, jnp.zeros_like(query_pair))
                grad = jnp.where(mine, grad_pair, jnp.zeros_like(grad_pair))
                right_scores = jnp.concatenate([query, query_features[...]], axis=1)
                right_grads = jnp.concatenate([grad, delta_features[...]], axis=1)
                head_lanes = (pair_lane >= 3 * head) & (pair_lane < 3 * head + 3)
                grad_q = jnp.zeros((64, tokens), F32)
                for part in range(2):
                    features = jnp.where(head_lanes, jnp.full_like(query_pair, -1.0), key_features[part])
                    scores = dot_nt(jnp.concatenate([keys[part, :, lanes], features], axis=1), right_scores)
                    weights = jnp.exp(scores)
                    grad_weights = dot_nt(jnp.concatenate([values[part, :, lanes], features], axis=1), right_grads)
                    grad_scores = (weights * grad_weights).astype(BF16)
                    if part == 0:
                        grad_v = dot(weights.astype(BF16), grad)
                        grad_k = dot(grad_scores, query)
                        if half == 0:
                            grad_value[:, lanes] = grad_v
                            grad_key[:, lanes] = grad_k
                        else:
                            grad_value[:, lanes] += grad_v
                            grad_key[:, lanes] += grad_k
                    grad_q = grad_q + dot(keys_t[part, head_rows, :], grad_scores)
                grad_query_t[head_rows, :] = grad_q
                run_plan(pair, half, 2, HEADS // 2)
            return carry

        lax.fori_loop(0, HEADS // 2, own_queries, 0)
        for swap in swaps():
            swap.wait_recv()

        def other_queries(pair, carry):
            lanes = pl.ds(pl.multiple_of(pair * 128, 128), 128)
            query_pair, grad_pair = queries[1, :, lanes], other_grad[:, lanes]
            pair_lane = lane_iota(query_pair.shape)
            grad_k = grad_key[:, lanes]
            grad_v = grad_value[:, lanes]
            for half in range(2):
                head = pair * 2 + half
                mine = (pair_lane < 64) == (half == 0)
                query = jnp.where(mine, query_pair, jnp.zeros_like(query_pair))
                grad = jnp.where(mine, grad_pair, jnp.zeros_like(grad_pair))
                head_lanes = (pair_lane >= 3 * head) & (pair_lane < 3 * head + 3)
                features = jnp.where(head_lanes, jnp.full_like(query_pair, -1.0), key_features[0])
                scores = dot_nt(
                    jnp.concatenate([keys[0, :, lanes], features], axis=1),
                    jnp.concatenate([query, other_features[...]], axis=1),
                )
                weights = jnp.exp(scores)
                grad_weights = dot_nt(
                    jnp.concatenate([values[0, :, lanes], features], axis=1),
                    jnp.concatenate([grad, other_delta[...]], axis=1),
                )
                grad_scores = (weights * grad_weights).astype(BF16)
                grad_v = grad_v + dot(weights.astype(BF16), grad)
                grad_k = grad_k + dot(grad_scores, query)
            grad_key[:, lanes] = grad_k
            grad_value[:, lanes] = grad_v
            run_plan(pair, 12, 1, HEADS // 2)
            return carry

        lax.fori_loop(0, HEADS // 2, other_queries, 0)

        grad_normed[...] = jnp.transpose(grad_query_t[...])
        for number in range(blocks):
            rows = pl.ds(number * BLOCK, BLOCK)
            before = block_place(segments, lengths, seq * blocks + number)[1]
            cosine, sine = rotary_block(table, before)
            for pair in range(HEADS // 2):
                lanes = pl.ds(pair * 128, 128)
                grad_triple[rows, lanes] = (turn(grad_normed[rows, lanes], cosine, -sine) * 0.125).astype(BF16)
                grad_triple[rows, pl.ds(width + pair * 128, 128)] = turn(grad_key[rows, lanes], cosine, -sine).astype(BF16)
            grad_triple[rows, pl.ds(2 * width, width)] = grad_value[rows, :].astype(BF16)

        for load in loads:
            load.wait()
        for part in range(2):
            triple_t = dot_tn(grad_triple[:, pl.ds(part * 1152, 1152)], normed[...]).astype(BF16)
            for place in range(8):
                at = (part, place >> 2, (place >> 1) & 1, place & 1)
                for side in range(2):
                    triple_part[at + (side,)] = triple_t[
                        place * 144 : place * 144 + 144, side * LANES : side * LANES + LANES
                    ]
        got = (tri_a, tri_b, tri_c, tri_d, tri_e)
        triple = [
            Stream(kit, 10 + number, triple_part, 48 * number, 48, {}, (CORE,) + order, got, 48 * number)
            for number, order in enumerate(((X, Y, Z1, Z2), (Y, Z1, X, Z2), (Z1, X, Y, Z2)))
        ]
        for stream in triple:
            stream.send(0)
        grad_normed[...] = jnp.zeros_like(grad_normed)
        for first in range(0, 3 * width, width):
            lanes = pl.ds(first, width)
            grad_normed[...] += dot_nt(grad_triple[:, lanes], weight[:, lanes])
        for stream in triple:
            step(stream, 0)

        gain_sum = jnp.zeros((1, width), F32)
        for number in range(blocks):
            rows, here = pl.ds(number * BLOCK, BLOCK), pl.ds(number, 1)
            value = hidden[rows, :].astype(F32)
            centered = value - mean_of(value)
            inverse = lax.rsqrt(mean_of(centered * centered) + 1e-05)
            normal = centered * inverse
            grad = grad_normed[rows, :]
            mod_rows[here, pl.ds(0, width)] = jnp.sum(grad, axis=0, keepdims=True)
            mod_rows[here, pl.ds(width, width)] = jnp.sum(grad * (normal * first_gain[...]), axis=0, keepdims=True)
            grad_line = grad * (1.0 + mod_part(number, 1))
            gain_sum = gain_sum + jnp.sum(grad_line * normal, axis=0, keepdims=True)
            grad_normal = grad_line * first_gain[...]
            along = mean_of(grad_normal * normal)
            term = (grad_normal - mean_of(grad_normal) - normal * along) * inverse
            input_grad[rows, :] = (grad_middle[rows, :] + term).astype(BF16)
        small_acc[0, pl.ds(FIRST_GAIN, 1), :] = gain_sum
        for part in range(6):
            small_acc[0, pl.ds(MOD_BIAS + part, 1), :] = jnp.sum(
                mod_rows[:, pl.ds(part * width, width)], axis=0, keepdims=True
            )

        def small_copy(number):
            return pltpu.make_async_remote_copy(
                small_acc.at[number], small_got.at[number], small_send.at[number], small_recv.at[number],
                device_id=greet[(1 + number) % len(greet)], device_id_type=MESH_ID,
            )

        def small_step(number):
            small_copy(number).wait_recv()
            small_acc[number + 1] = small_acc[number] + small_got[number]
            if number + 1 < len(greet):
                small_copy(number + 1).start()

        small_copy(0).start()

        mod_axes = (CORE, Y, Z1, Z2, X)

        def mod_copies(number):
            mods = (mod_zero, mod_one, mod_two, mod_three, mod_four)
            conds = (cond_zero, cond_one, cond_two, cond_three, cond_four)
            if number == 0:
                pairs = ((mod_zero.at[:, :, :, 1 - core], mod_got), (cond_zero, cond_got))
            else:
                later = ((mod_two, cond_two), (mod_three, cond_three), (mod_four, cond_four), (mod_five, cond_five))[number - 1]
                chunks = pl.ds(2 ** (number - 1), 2 ** (number - 1))
                if number == 1:
                    source = mod_one.at[:, :, :, 1 - bits[Y]]
                elif number == 2:
                    source = mod_two.at[:, :, 1 - bits[Z1]]
                elif number == 3:
                    source = mod_three.at[:, 1 - bits[Z2]]
                else:
                    source = mod_four
                pairs = ((source, later[0].at[chunks]), (conds[number], later[1].at[chunks]))
            return [
                pltpu.make_async_remote_copy(
                    source, target, mod_send.at[place, number], mod_recv.at[place, number],
                    device_id=exchange_partner(mod_axes[number], extra_bits), device_id_type=MESH_ID,
                )
                for place, (source, target) in enumerate(pairs)
            ]

        def mod_step(number):
            for copy in mod_copies(number):
                copy.wait_recv()
            if number == 0:
                mod_one[0] = mod_zero[:, :, :, core]
                mod_one[0, :, :, :, pl.ds(4, 4), :] = mod_got[:, :, :, pl.ds(0, 4), :]
                cond_one[0] = cond_zero[...]
                cond_one[0, pl.ds(4, 4), :] = cond_got[pl.ds(0, 4), :]
            if number == 0:
                mod_two[0] = mod_one[0, :, :, bits[Y]]
                cond_two[0] = cond_one[0]
            elif number == 1:
                mod_three[pl.ds(0, 2)] = mod_two[:, :, bits[Z1]]
                cond_three[pl.ds(0, 2)] = cond_two[...]
            elif number == 2:
                mod_four[pl.ds(0, 4)] = mod_three[:, bits[Z2]]
                cond_four[pl.ds(0, 4)] = cond_three[...]
            elif number == 3:
                mod_five[pl.ds(0, 8)] = mod_four[...]
                cond_five[pl.ds(0, 8)] = cond_four[...]
            if number < 4:
                for copy in mod_copies(number + 1):
                    copy.start()

        mod_zero[...] = jnp.zeros_like(mod_zero)
        columns = 6 * width // 16
        for group in range(16):
            at = (group >> 3, (group >> 2) & 1, (group >> 1) & 1, group & 1)
            mod_zero[at + (pl.ds(0, blocks), pl.ds(0, columns))] = mod_rows[:, pl.ds(group * columns, columns)]
        cond_zero[...] = condition[...]
        for copy in mod_copies(0):
            copy.start()

        for number in range(4):
            for stream in triple:
                if number < 3:
                    step(stream, number + 1)
            mod_step(number)
            small_step(number)
        for number, stream in enumerate(triple):
            stream.add(4, sums, 432 + 48 * number)
        mod_step(4)
        chunk_rows = mod_five.shape[0] * mod_five.shape[1]
        gathered = mod_five[...].reshape(chunk_rows, LANES)
        embedded = cond_five[...].reshape(chunk_rows, 128).astype(BF16)
        upper = gathered.astype(BF16)
        lower = (gathered - upper.astype(F32)).astype(BF16)
        mod_out[...] = dot_tn(embedded, upper) + dot_tn(embedded, lower)
        for number in range(4, len(greet)):
            small_step(number)
        small_out[...] = small_acc[len(greet)]
        for stream in triple:
            stream.done()
        for number in range(5):
            for copy in mod_copies(number):
                copy.wait_send()
        for number in range(len(greet)):
            small_copy(number).wait_send()

    pl.run_scoped(
        attention_phase,
        pltpu.VMEM((tokens, width), BF16), pltpu.VMEM((tokens, width), BF16), pltpu.VMEM((width, 3 * width), BF16),
        pltpu.VMEM((2, width, tokens), BF16), pltpu.VMEM((width, tokens), F32), pltpu.VMEM((tokens, width), F32),
        pltpu.VMEM((tokens, width), F32), pltpu.VMEM((tokens, 3 * width), BF16), pltpu.VMEM((tokens, width), F32),
        pltpu.VMEM((2, 2, 2, 2, 2, 144, LANES), BF16),
    )

    for tile in range(tiles):
        for copy in core_copies(tile):
            copy.wait_send()
    for stream in one + two + red + [one_merge, two_merge, red_merge, out]:
        stream.done()
    for swap in swaps():
        swap.wait_send()


def backward(segments, lengths, modulation, gate_grads, small, condition, table, first_gain, second_gain, *arrays):
    tokens, width = arrays[6].shape
    all_bits = lax.axis_size("dp").bit_length() - 1
    extra_bits = all_bits - GROUP_BITS
    steps = all_bits + 1
    smem, vmem = pl.BlockSpec(memory_space=pltpu.SMEM), pl.BlockSpec(memory_space=pltpu.VMEM)
    hbm = pl.BlockSpec(memory_space=pl.ANY)
    tiles = arrays[3].shape[0]

    def rows_of(count, free, lead=()):
        return pltpu.VMEM(lead + (2,) * free + (count, LANES), BF16)

    def half(dtype):
        return pltpu.VMEM((tokens, width), dtype)

    features = pltpu.VMEM((tokens, 128), BF16)
    both = pltpu.VMEM((2, tokens, width), BF16)
    group_rows = [rows_of(count, free) for count in (48, 144) for free in (4, 3, 2, 1, 0)]
    halves = [rows_of(count, free, (2,)) if free >= 0 else rows_of(count, 0) for count in (96, 96, 192) for free in (2, 1, 0, -1)]
    mods = [pltpu.VMEM(shape + (8, LANES), F32) for shape in ((2, 2, 2, 2), (2, 2, 2), (1, 2, 2, 2), (2, 2, 2), (4, 2), (8,), (16,))]
    conds = [pltpu.VMEM(shape + (8, 128), F32) for shape in ((), (), (1,), (2,), (4,), (8,), (16,))]
    dma = pltpu.SemaphoreType.DMA
    return pl.pallas_call(
        functools.partial(backward_kernel, extra_bits, all_bits),
        out_shape=(
            jax.ShapeDtypeStruct((tokens, width), BF16),
            jax.ShapeDtypeStruct((576, LANES), F32),
            jax.ShapeDtypeStruct((128, LANES), F32),
            jax.ShapeDtypeStruct((SMALL_ROWS, width), F32),
        ),
        in_specs=[smem] * 2 + [vmem] * 7 + [hbm] * len(arrays),
        out_specs=(vmem,) * 4,
        scratch_shapes=[rows_of(192, 5), rows_of(192, 5), rows_of(48, 5), rows_of(192, 4), rows_of(192, 4)]
        + halves
        + group_rows
        + [both, both, both, features, pltpu.VMEM((2, tokens, 128), BF16)]
        + [half(F32), half(BF16), features, half(BF16), features, features]
        + [pltpu.VMEM((tokens // BLOCK, 6 * width), F32)]
        + [pltpu.VMEM((steps + 1, SMALL_ROWS, width), F32), pltpu.VMEM((steps, SMALL_ROWS, width), F32)]
        + mods
        + conds
        + [dma((16,)), dma((4, tiles)), dma((2, tiles)), dma((2, tiles)), dma((13, 5)), dma((13, 5)), dma((3,)), dma((3,))]
        + [dma((steps,)), dma((steps,)), dma((2, 5)), dma((2, 5))],
        compiler_params=pltpu.CompilerParams(
            collective_id=2, has_side_effects=True, vmem_limit_bytes=63 << 20
        ),
    )(segments, lengths, modulation, gate_grads, small, condition, table, first_gain, second_gain, *arrays)


def scatter_rest(block, dp_size):
    group = dp_size >> GROUP_BITS
    if group == 1:
        return block
    groups = [[first * group + place for place in range(group)] for first in range(dp_size // group)]
    return lax.psum_scatter(block, "dp", scatter_dimension=0, axis_index_groups=groups, tiled=True)


def local(
    hidden_in,
    segment_ids,
    piece_lengths,
    time_index,
    first_gain,
    modulation_weight,
    modulation_bias,
    query_key_value_weight,
    attention_output_matrix,
    second_gain,
    widen_weight,
    expand_bias,
    narrow_weight,
    reduce_bias,
    cotangent,
):
    slot_count, own_rows, width = hidden_in.shape
    hidden, cot = hidden_in[0], cotangent[0]
    table = jnp.asarray(angle_table())
    gain_one, gain_two = first_gain[None, :], second_gain[None, :]
    normed, queries, keys, values, attended, query_features, key_features, modulation, condition = forward(
        segment_ids, piece_lengths, time_index, hidden, table, gain_one, modulation_weight,
        modulation_bias[None, :], query_key_value_weight,
    )
    block_out, grad_low, normed_two, normal, spread_row, projected, gate_grads, small, activated, slope = mlp(
        segment_ids, piece_lengths, hidden, attended, cot, modulation, gain_two, expand_bias[None, :],
        reduce_bias[None, :], attention_output_matrix, widen_weight, narrow_weight,
    )
    input_grad, block_sum, mod_sum, small_sum = backward(
        segment_ids, piece_lengths, modulation, gate_grads, small, condition, table, gain_one, gain_two,
        narrow_weight, widen_weight, attention_output_matrix, activated, slope, normed_two, grad_low, normal,
        spread_row, projected, attended, cot, queries, keys, values, query_features, key_features, normed, hidden,
        query_key_value_weight,
    )
    dp_size = lax.axis_size("dp")
    expand_block = scatter_rest(block_sum[:192], dp_size).T
    reduce_block = block_sum[192:384].reshape(4, -1, LANES).transpose(1, 0, 2).reshape(-1, 4 * LANES)
    reduce_block = scatter_rest(reduce_block, dp_size).T
    output_block = scatter_rest(block_sum[384:432], dp_size).T
    triple_block = scatter_rest(block_sum[432:576], dp_size).T
    half = mod_sum.shape[0] // 2
    mod_block = lax.dynamic_slice_in_dim(mod_sum, lax.axis_index("seq") * half, half, 0)[:, : 6 * width // 16]
    mod_block = scatter_rest(mod_block.T, dp_size).T
    stats = small_sum[STATS]
    return (
        block_out[None],
        input_grad[None],
        small_sum[FIRST_GAIN],
        mod_block,
        small_sum[MOD_BIAS : MOD_BIAS + 6].reshape(-1),
        triple_block,
        output_block,
        small_sum[SECOND_GAIN],
        expand_block,
        small_sum[EXPAND_BIAS : EXPAND_BIAS + 4].reshape(-1),
        reduce_block,
        small_sum[REDUCE_BIAS],
        jnp.sqrt(stats[:3] / (stats[3] * width)),
    )


def solution(mesh):
    in_specs = (
        P("dp", "seq", None),
        P("dp", None),
        P("dp", None),
        P("dp", None),
        P(),
        P(),
        P(),
        P(),
        P(),
        P(),
        P(),
        P(),
        P(),
        P(),
        P("dp", "seq", None),
    )
    out_specs = (
        P("dp", "seq", None),
        P("dp", "seq", None),
        P(),
        P("seq", "dp"),
        P(),
        P("seq", "dp"),
        P("seq", "dp"),
        P(),
        P("seq", "dp"),
        P(),
        P("seq", "dp"),
        P(),
        P(),
    )
    return jax.shard_map(local, mesh=mesh, in_specs=in_specs, out_specs=out_specs, check_vma=False)
```

time: 241 us -> 203 us (0.84); the launches traced: 237 us -> 202 us
  Pallas kernels: 200 us -> 182 us
  local copies, waits for them, and re-layouts: 30.6 us -> 17.3 us
  matrix products: 3.84 us -> 0 us
    pallas_call x1, Pallas kernels: 35.9 us -> 22.9 us  [mlp(): pl.pallas_call(mlp_kernel, out_shape=(jax.ShapeDtypeStruct(half, BF16), j...]
    unnamed x26 -> x7, local copies, waits for them, and re-layouts: 12 us -> 0.89 us
    concatenate x2 -> x0, local copies, waits for them, and re-layouts: 5.43 us -> none  [local(): jnp.concatenate([expand_part, reduce_part, output_part, triple_part, mod_...]
    pallas_call x2 -> x1, Pallas kernels: 127 us -> 122 us  [backward(): pl.pallas_call(functools.partial(backward_kernel, extra_bits, all_bits),...]
    reshape x4 -> x1, local copies, waits for them, and re-layouts: 4.83 us -> 0.74 us  [local(): block_sum[192:384].reshape(4, -1, LANES).transpose(1, 0, 2)]
    dot_general x1 -> x0, matrix products: 3.84 us -> none  [local(): jnp.einsum('bc,bf->fc', own_condition, mod_rows, precision=lax.Precision....]
    slice x1 -> x2, local copies, waits for them, and re-layouts: 0.75 us -> 3.34 us  [the longest x1 1.8 us: local(): block_sum[192:384].reshape(4, -1, LANES).transpose(1, 0, 2)]
where the time goes in v3:
time: 203 us; the launch traced here: 202 us
  Pallas kernels  182 us (90%)
  local copies, waits for them, and re-layouts  17.3 us (9%)
    pallas_call x1, Pallas kernels, backward(): pl.pallas_call(functools.partial(backward_kernel, extra_bits, all_bits),...  122 us
    pallas_call x1, Pallas kernels, forward(): pl.pallas_call(forward_kernel, out_shape=(half, both, both, both, half, j...  37.5 us
    pallas_call x1, Pallas kernels, mlp(): pl.pallas_call(mlp_kernel, out_shape=(jax.ShapeDtypeStruct(half, BF16), j...  22.9 us

profile of v3, /device:TPU:0, one launch (start us, length us, event | category | flops | bytes accessed | tf_op | source)
XLA Modules:
  0.0 202.3 jit_solution(2760175636311706991)
XLA Ops:
  0.6 1.3 broadcast_in_dim.21.first_gain
  1.9 1.3 broadcast_in_dim.22.mod_bias
  3.3 0.0 copy-start.1
  3.3 0.0 copy-start.2
  3.3 37.5 %shard_map.255 = (bf16[512,768]{1,0:T(8,128)(2,1)}, bf16[2,512,768]{2,1,0:T(8,128)(2,1)}, bf16[2,512,768]{2,1,0:T(8,128)(2,1)}, bf16[2,512,768]{2,1,0:T(8,128)(2...) custom-call(s32[1,1024]{1,0:T(1,128)} %segments.5, ...), custom_call_target="tpu_custom_call" | custom-call | tf_op jit(solution)/shard_map/pallas_call | solution.py:222
  40.8 0.0 copy-done.1
  40.8 0.6 broadcast_in_dim.23.second_gain
  41.4 0.0 copy-done.2
  41.4 0.6 broadcast_in_dim.25.reduce_bias
  42.0 22.9 %shard_map.256 = (bf16[512,768]{1,0:T(8,128)(2,1)}, bf16[512,768]{1,0:T(8,128)(2,1)}, bf16[512,768]{1,0:T(8,128)(2,1)}, f32[512,768]{1,0:T(8,128)}, f32[512,128]...) custom-call(s32[1,1024]{1,0:T(1,128)} %segments.5, ...), custom_call_target="tpu_custom_call" | custom-call | tf_op jit(solution)/shard_map/pallas_call | solution.py:379
  64.9 121.9 %shard_map.257 = (bf16[512,768]{1,0:T(8,128)(2,1)}, f32[576,384]{1,0:T(8,128)}, f32[128,384]{1,0:T(8,128)}, f32[16,768]{1,0:T(8,128)}) custom-call(s32[1,1024]{1,0:T(1,128)} %segments.5, s32[1,8]{1,0:T(1,128)} %lengths.5, f32[8,4608]{1,0:T(8,128)} %get-tuple-element.37.modulation, f32[4,768]{1,0:T(4,128)} %get-tuple-element.39.gate_grads, ...), custom_call_target="tpu_custom_call" | custom-call | tf_op jit(solution)/shard_map/pallas_call | solution.py:1043
  186.9 0.0 copy-start
  186.9 1.5 slice_reduce_fusion
  188.4 1.5 constant_dynamic-slice_fusion
  189.9 0.7 slice.43
  190.6 0.6 reshape.46
  191.3 1.6 slice_bitcast_fusion.1
  192.9 1.5 slice_bitcast_fusion.2
  194.4 1.8 fusion
  196.2 0.7 slice.48
  197.0 0.6 reshape.47
  197.6 0.7 copy.30
  198.3 1.3 slice.52
  200.2 1.2 sqrt_bitcast_fusion
  201.4 0.0 copy-done
  201.4 0.9 copy.32
Async XLA Ops:
  3.3 37.6 %copy-start.1 = (f32[768]{0:T(1024)S(1)}, f32[768]{0:T(1024)}, u32[]{:S(2)}) copy-start(f32[768]{0:T(1024)} %param.25) | copy-start | bytes 9220
  3.3 38.1 %copy-start.2 = (f32[768]{0:T(1024)S(1)}, f32[768]{0:T(1024)}, u32[]{:S(2)}) copy-start(f32[768]{0:T(1024)} %param.29) | copy-start | bytes 9220
  186.9 14.5 %copy-start = (bf16[512,768]{1,0:T(8,128)(2,1)S(1)}, bf16[512,768]{1,0:T(8,128)(2,1)}, u32[]{:S(2)}) copy-start(bf16[512,768]{1,0:T(8,128)(2,1)} %get-tuple-element.55) | copy-start | bytes 2359300

commit v4 on v3

--- a/solution.py
+++ b/solution.py
@@ -246,168 +246,6 @@
 
 
 TILE = 384
-
-
-def mlp_kernel(
-    segments, lengths, hidden, attended, cotangent, modulation, second_gain, expand_bias, reduce_bias,
-    out_weight_hbm, widen_hbm, narrow_hbm,
-    block_out, grad_low, normed, normal, spread_row, projected, gate_grads, small, activated_hbm, slope_hbm,
-    out_weight, widen, narrow, activated, slope, middle, reduced,
-    load_sem, tile_sem, store_sem,
-):
-    tokens, width = hidden.shape
-    tiles = widen.shape[1] // TILE
-    blocks = tokens // BLOCK
-    seq = lax.axis_index("seq")
-
-    def tile_lanes(tile):
-        return pl.ds(pl.multiple_of(tile * TILE, TILE), TILE)
-
-    def tile_loads(tile):
-        lanes = tile_lanes(tile)
-        return (
-            pltpu.make_async_copy(widen_hbm.at[:, lanes], widen.at[:, lanes], tile_sem.at[0, tile]),
-            pltpu.make_async_copy(narrow_hbm.at[lanes], narrow.at[lanes], tile_sem.at[1, tile]),
-        )
-
-    first_load = pltpu.make_async_copy(out_weight_hbm, out_weight, load_sem)
-    first_load.start()
-    for tile in range(tiles):
-        for load in tile_loads(tile):
-            load.start()
-    row = row_iota((BLOCK, 1))
-    keep = []
-    for number in range(blocks):
-        valid_count = block_place(segments, lengths, seq * blocks + number)[2]
-        keep.append(jnp.where(row < valid_count, 1.0, 0.0))
-
-    def mod_part(number, part):
-        return modulation[pl.ds(number, 1), pl.ds(part * width, width)]
-
-    first_load.wait()
-    for first in range(0, width, 256):
-        lanes = pl.ds(first, 256)
-        projected[:, lanes] = dot(attended[...], out_weight[:, lanes])
-    branch_sum = jnp.zeros((1, width), F32)
-    for number in range(blocks):
-        rows = pl.ds(number * BLOCK, BLOCK)
-        branch = mod_part(number, 2) * projected[rows, :]
-        branch_sum = branch_sum + jnp.sum(keep[number] * branch * branch, axis=0, keepdims=True)
-        value = hidden[rows, :].astype(F32) + branch
-        middle[rows, :] = value
-        centered = value - mean_of(value)
-        inverse = lax.rsqrt(mean_of(centered * centered) + 1e-05)
-        normal[rows, :] = centered * inverse
-        spread_row[rows, :] = jnp.broadcast_to(inverse, (BLOCK, 128))
-        line = normal[rows, :] * second_gain[...]
-        normed[rows, :] = (line * (1.0 + mod_part(number, 4)) + mod_part(number, 3)).astype(BF16)
-
-    reduced[...] = jnp.zeros_like(reduced)
-
-    def stores(tile):
-        return (
-            pltpu.make_async_copy(activated.at[tile], activated_hbm.at[tile], store_sem.at[0, tile]),
-            pltpu.make_async_copy(slope.at[tile], slope_hbm.at[tile], store_sem.at[1, tile]),
-        )
-
-    def ahead(tile):
-        lanes = tile_lanes(tile)
-        for load in tile_loads(tile):
-            load.wait()
-        u = dot(normed[...], widen[:, lanes]) + expand_bias[:, lanes]
-        square = u * u
-        tanh = jnp.tanh(u * (0.7978845608028654 + 0.7978845608028654 * 0.044715 * square))
-        half_sum = 0.5 + 0.5 * tanh
-        active = (u * half_sum).astype(BF16)
-        inner = 0.7978845608028654 + 3.0 * 0.7978845608028654 * 0.044715 * square
-        slope[tile] = (half_sum + (0.5 * u) * (1.0 - tanh * tanh) * inner).astype(BF16)
-        activated[tile] = active
-        reduced[...] += dot(active, narrow[lanes, :])
-        for copy in stores(tile):
-            copy.start()
-
-    def ahead_two(step, carry):
-        ahead(2 * step)
-        ahead(2 * step + 1)
-        return carry
-
-    lax.fori_loop(0, tiles // 2, ahead_two, 0)
-
-    value_sum = jnp.zeros((1, width), F32)
-    mlp_sum = jnp.zeros((1, width), F32)
-    bias_sum = jnp.zeros((1, width), F32)
-    for number in range(blocks):
-        rows = pl.ds(number * BLOCK, BLOCK)
-        gate = mod_part(number, 5)
-        full = reduced[rows, :] + reduce_bias[...]
-        branch = gate * full
-        value = middle[rows, :] + branch
-        block_out[rows, :] = value.astype(BF16)
-        value_sum = value_sum + jnp.sum(keep[number] * value * value, axis=0, keepdims=True)
-        mlp_sum = mlp_sum + jnp.sum(keep[number] * branch * branch, axis=0, keepdims=True)
-        grad_out = cotangent[rows, :].astype(F32) * keep[number]
-        gate_grads[pl.ds(number, 1), :] = jnp.sum(grad_out * full, axis=0, keepdims=True)
-        low = (gate * grad_out).astype(BF16)
-        grad_low[rows, :] = low
-        bias_sum = bias_sum + jnp.sum(low.astype(F32), axis=0, keepdims=True)
-    small[...] = jnp.zeros_like(small)
-    small[pl.ds(REDUCE_BIAS, 1), :] = bias_sum
-    lane = lane_iota((1, width))
-    counts = jnp.zeros((1, 1), F32)
-    for number in range(blocks):
-        counts = counts + jnp.sum(keep[number], axis=0, keepdims=True)
-    sums = [jnp.sum(term, axis=1, keepdims=True) for term in (value_sum, branch_sum, mlp_sum)] + [counts]
-    stats = jnp.zeros((1, width), F32)
-    for place, term in enumerate(sums):
-        stats = jnp.where(lane == place, term, stats)
-    small[pl.ds(STATS, 1), :] = stats
-
-    def drain(tile, carry):
-        for copy in stores(tile):
-            copy.wait()
-        return carry
-
-    lax.fori_loop(0, tiles, drain, 0)
-
-
-def mlp(segments, lengths, hidden, attended, cotangent, modulation, second_gain, expand_bias, reduce_bias, out_weight, widen, narrow):
-    tokens, width = hidden.shape
-    tiles = widen.shape[1] // TILE
-    smem, vmem = pl.BlockSpec(memory_space=pltpu.SMEM), pl.BlockSpec(memory_space=pltpu.VMEM)
-    hbm = pl.BlockSpec(memory_space=pl.ANY)
-    half, by_tile = (tokens, width), (tiles, tokens, TILE)
-    return pl.pallas_call(
-        mlp_kernel,
-        out_shape=(
-            jax.ShapeDtypeStruct(half, BF16),
-            jax.ShapeDtypeStruct(half, BF16),
-            jax.ShapeDtypeStruct(half, BF16),
-            jax.ShapeDtypeStruct(half, F32),
-            jax.ShapeDtypeStruct((tokens, 128), F32),
-            jax.ShapeDtypeStruct(half, F32),
-            jax.ShapeDtypeStruct((tokens // BLOCK, width), F32),
-            jax.ShapeDtypeStruct((SMALL_ROWS, width), F32),
-            jax.ShapeDtypeStruct(by_tile, BF16),
-            jax.ShapeDtypeStruct(by_tile, BF16),
-        ),
-        in_specs=[smem] * 2 + [vmem] * 7 + [hbm] * 3,
-        out_specs=(vmem,) * 8 + (hbm,) * 2,
-        scratch_shapes=[
-            pltpu.VMEM(out_weight.shape, BF16),
-            pltpu.VMEM(widen.shape, BF16),
-            pltpu.VMEM(narrow.shape, BF16),
-            pltpu.VMEM(by_tile, BF16),
-            pltpu.VMEM(by_tile, BF16),
-            pltpu.VMEM(half, F32),
-            pltpu.VMEM(half, F32),
-            pltpu.SemaphoreType.DMA,
-            pltpu.SemaphoreType.DMA((2, tiles)),
-            pltpu.SemaphoreType.DMA((2, tiles)),
-        ],
-        compiler_params=pltpu.CompilerParams(vmem_limit_bytes=56 << 20),
-    )(segments, lengths, hidden, attended, cotangent, modulation, second_gain, expand_bias, reduce_bias, out_weight, widen, narrow)
-
-
 Z2, Z1, Y, CORE, X = 0, 1, 2, 3, 4
 
 
@@ -485,41 +323,50 @@
 
 def backward_kernel(
     extra_bits, all_bits,
-    segments, lengths, modulation, gate_grads, small_in, condition, table, first_gain, second_gain,
-    narrow_hbm, widen_hbm, out_weight_hbm, activated_hbm, slope_hbm, normed_two_hbm, grad_low_hbm, normal_hbm, spread_hbm,
-    projected_hbm, attended_hbm, cotangent_hbm, queries_hbm, keys_hbm, values_hbm, query_features_hbm, key_features_hbm,
-    normed_hbm, hidden_hbm, weight_hbm,
-    input_grad, sums, mod_out, small_out,
+    segments, lengths, modulation, condition, table, first_gain, second_gain, expand_bias, reduce_bias,
+    narrow_hbm, widen_hbm, out_weight_hbm, attended_hbm, cotangent_hbm, queries_hbm, keys_hbm, values_hbm,
+    query_features_hbm, key_features_hbm, normed_hbm, hidden_hbm, weight_hbm,
+    block_out, input_grad, sums, mod_out, small_out,
     expand_part, reduce_part, output_part,
-    expand_got, reduce_got, one_x, one_z, one_y, one_last, two_z, two_y, two_x, two_last, red_y, red_z, red_w, red_last,
+    expand_got, reduce_got, wide_a, wide_b, wide_z, wide_last, red_a, red_b, red_c, red_last,
     out_a, out_b, out_c, out_d, out_e, tri_a, tri_b, tri_c, tri_d, tri_e,
     queries, keys, values, query_features, key_features,
     grad_middle, grad_attended, delta_features, other_grad, other_delta, other_features, mod_rows,
-    small_acc, small_got, mod_zero, mod_got, mod_one, mod_two, mod_three, mod_four, mod_five,
+    small_acc, small_got, late_acc, late_got, mod_zero, mod_got, mod_one, mod_two, mod_three, mod_four, mod_five,
     cond_zero, cond_got, cond_one, cond_two, cond_three, cond_four, cond_five,
     load_sem, tile_sem, core_send, core_recv, stream_send, stream_recv, swap_send, swap_recv,
-    small_send, small_recv, mod_send, mod_recv,
+    small_send, small_recv, late_send, late_recv, mod_send, mod_recv,
 ):
     tokens, width = input_grad.shape
-    tiles = activated_hbm.shape[0]
+    tiles = narrow_hbm.shape[0] // TILE
     blocks = tokens // BLOCK
     seq = lax.axis_index("seq")
     dp = lax.axis_index("dp")
     bits = [own_bit(axis, extra_bits) for axis in range(5)]
     kit = {"bits": bits, "send": stream_send, "recv": stream_recv, "extra": extra_bits}
     core = bits[CORE]
-    own = {axis: bits[axis] for axis in range(5)}
 
     def others(*axes):
         return {axis: bits[axis] for axis in range(5) if axis not in axes}
 
-    one = [Stream(kit, v, expand_part, 0, 96, {CORE: core, Z2: v}, (X, Z1, Y), (one_x.at[v], one_z.at[v], one_y.at[v])) for v in range(2)]
-    two = [Stream(kit, 2 + v, expand_part, 96, 96, {CORE: core, Z2: v}, (Z1, Y, X), (two_z.at[v], two_y.at[v], two_x.at[v])) for v in range(2)]
-    red = [Stream(kit, 4 + v, reduce_part, 0, 192, {CORE: core, X: v}, (Y, Z1, Z2), (red_y.at[v], red_z.at[v], red_w.at[v])) for v in range(2)]
-    one_merge = Stream(kit, 6, expand_part, 0, 96, others(Z2), (Z2,), (one_last,))
-    two_merge = Stream(kit, 7, expand_part, 96, 96, others(Z2), (Z2,), (two_last,))
-    red_merge = Stream(kit, 8, reduce_part, 0, 192, others(X), (X,), (red_last,))
-    out = Stream(kit, 9, output_part, 0, 48, {}, (CORE, Y, X, Z1, Z2), (out_a, out_b, out_c, out_d, out_e))
+    def chosen(**values):
+        return {CORE: core, **{{"z2": Z2, "z1": Z1, "x": X}[name]: value for name, value in values.items()}}
+
+    wide = [
+        Stream(kit, g, expand_part, 0, 192, chosen(z2=g >> 1, z1=g & 1), (Y, X) if g == 3 else (X, Y), (wide_a.at[g], wide_b.at[g]))
+        for g in range(4)
+    ]
+    red = [
+        Stream(
+            kit, 4 + g, reduce_part, 96 * (g & 1), 96, chosen(x=g >> 1), (Y, Z1, Z2) if g & 1 else (Z1, Y, Z2),
+            (red_a.at[g], red_b.at[g], red_c.at[g]),
+        )
+        for g in range(4)
+    ]
+    wide_merge = [Stream(kit, 8 + v, expand_part, 0, 192, {**others(Z1, Z2), Z2: v}, (Z1,), (wide_z.at[v],)) for v in range(2)]
+    wide_end = Stream(kit, 10, expand_part, 0, 192, others(Z2), (Z2,), (wide_last,))
+    red_end = [Stream(kit, 11 + h, reduce_part, 96 * h, 96, others(X), (X,), (red_last.at[h],)) for h in range(2)]
+    out = Stream(kit, 13, output_part, 0, 48, {}, (CORE, Y, X, Z1, Z2), (out_a, out_b, out_c, out_d, out_e))
 
     greet = [(dp, 1 - seq)] + [(dp ^ (1 << bit), seq) for bit in range(all_bits)]
     barrier = pltpu.get_barrier_semaphore()
@@ -574,46 +421,81 @@
                     index, got = (z2, z1, y, core, tile >> 2, rows), (z2, z1, y, tile >> 2, rows)
                     reduce_part[index] = reduce_part[index] + reduce_got[got]
 
+    def step(stream, stage):
+        stream.add(stage)
+        stream.send(stage + 1)
+
     def mlp_phase(
-        narrow, widen, out_weight, activated, slope, normed_two, grad_low, grad_low_t, normal, spread_row, projected,
-        attended, cotangent, bias_row, grad_normed,
+        narrow, widen, out_weight, attended, hidden, cotangent, normed_two, grad_low, grad_low_t, normal, spread_row,
+        projected, reduced, bias_row, grad_normed,
     ):
         def tile_loads(tile):
             lanes = tile_lanes(tile)
-            pairs = (
-                (narrow_hbm.at[lanes], narrow.at[lanes]), (slope_hbm.at[tile], slope.at[tile]),
-                (widen_hbm.at[:, lanes], widen.at[:, lanes]), (activated_hbm.at[tile], activated.at[tile]),
-            )
+            pairs = ((widen_hbm.at[:, lanes], widen.at[:, lanes]), (narrow_hbm.at[lanes], narrow.at[lanes]))
             return [pltpu.make_async_copy(source, target, tile_sem.at[place, tile]) for place, (source, target) in enumerate(pairs)]
 
         loads = [
             pltpu.make_async_copy(source, target, load_sem.at[5 + number])
             for number, (source, target) in enumerate(
-                ((grad_low_hbm, grad_low), (normed_two_hbm, normed_two), (normal_hbm, normal), (spread_hbm, spread_row),
-                 (projected_hbm, projected), (attended_hbm, attended), (cotangent_hbm, cotangent), (out_weight_hbm, out_weight))
+                ((cotangent_hbm, cotangent), (attended_hbm, attended), (out_weight_hbm, out_weight), (hidden_hbm, hidden))
             )
         ]
-        for load in loads[:2]:
+        for load in loads:
             load.start()
         for tile in range(tiles):
             for load in tile_loads(tile):
                 load.start()
-        for load in loads[2:] + attention_loads:
+        for load in attention_loads:
             load.start()
+        small_acc[0] = jnp.zeros_like(small_acc[0])
         grad_normed[...] = jnp.zeros_like(grad_normed)
+        reduced[...] = jnp.zeros_like(reduced)
         loads[0].wait()
+        bias_sum = jnp.zeros((1, width), F32)
+        for number in range(blocks):
+            rows = pl.ds(number * BLOCK, BLOCK)
+            low = (mod_part(number, 5) * (cotangent[rows, :].astype(F32) * keep[number])).astype(BF16)
+            grad_low[rows, :] = low
+            bias_sum = bias_sum + jnp.sum(low.astype(F32), axis=0, keepdims=True)
+        small_acc[0, pl.ds(REDUCE_BIAS, 1), :] = bias_sum
         grad_low_t[...] = jnp.transpose(grad_low[...])
-        loads[1].wait()
+        for load in loads[1:]:
+            load.wait()
+        for first in range(0, width, 256):
+            lanes = pl.ds(first, 256)
+            projected[:, lanes] = dot(attended[...], out_weight[:, lanes])
+        branch_sum = jnp.zeros((1, width), F32)
+        for number in range(blocks):
+            rows = pl.ds(number * BLOCK, BLOCK)
+            branch = mod_part(number, 2) * projected[rows, :]
+            branch_sum = branch_sum + jnp.sum(keep[number] * branch * branch, axis=0, keepdims=True)
+            value = hidden[rows, :].astype(F32) + branch
+            centered = value - mean_of(value)
+            inverse = lax.rsqrt(mean_of(centered * centered) + 1e-05)
+            normal[rows, :] = centered * inverse
+            spread_row[rows, :] = jnp.broadcast_to(inverse, (BLOCK, 128))
+            line = normal[rows, :] * second_gain[...]
+            normed_two[rows, :] = (line * (1.0 + mod_part(number, 4)) + mod_part(number, 3)).astype(BF16)
         pl.semaphore_wait(barrier, len(greet))
 
-        def back(tile):
+        def through(tile):
             lanes = tile_lanes(tile)
             for load in tile_loads(tile):
                 load.wait()
+            u = dot(normed_two[...], widen[:, lanes]) + expand_bias[:, lanes]
             grad_active = dot_nt(grad_low[...], narrow[lanes, :])
-            grad_wide = (grad_active * slope[tile].astype(F32)).astype(BF16)
+            square = u * u
+            tanh = jnp.tanh(u * (0.7978845608028654 + 0.7978845608028654 * 0.044715 * square))
+            half_sum = 0.5 + 0.5 * tanh
+            active = (u * half_sum).astype(BF16)
+            inner = 0.7978845608028654 + 3.0 * 0.7978845608028654 * 0.044715 * square
+            slope = half_sum + (0.5 * u) * (1.0 - tanh * tanh) * inner
+            grad_wide = (grad_active * slope).astype(BF16)
+            reduced[...] += dot(active, narrow[lanes, :])
+            reduce_t = dot(grad_low_t[...], active).astype(BF16)
+            rows = pl.ds(pl.multiple_of((tile & 3) * 48, 16), 48)
+            reduce_part[:, :, :, :, tile >> 2, rows] = reduce_t.reshape(2, 2, 2, 2, 48, TILE)
             bias_row[pl.ds(0, 1), lanes] = jnp.sum(grad_wide.astype(F32), axis=0, keepdims=True)
-            grad_normed[...] += dot_nt(grad_wide, widen[:, lanes])
             expand_t = dot_tn(grad_wide, normed_two[...]).astype(BF16)
             at = (tile >> 2, (tile >> 1) & 1, tile & 1)
             for group in range(2):
@@ -621,59 +503,92 @@
                     expand_part[at + (group, side)] = expand_t[
                         group * 192 : group * 192 + 192, side * LANES : side * LANES + LANES
                     ]
-            reduce_t = dot(grad_low_t[...], activated[tile]).astype(BF16)
-            rows = pl.ds(pl.multiple_of((tile & 3) * 48, 16), 48)
-            reduce_part[:, :, :, :, tile >> 2, rows] = reduce_t.reshape(2, 2, 2, 2, 48, TILE)
             for copy in core_copies(tile):
                 copy.start()
-
-        def back_two(step, carry):
-            back(2 * step)
-
-            @pl.when(step > 0)
+            grad_normed[...] += dot_nt(grad_wide, widen[:, lanes])
+
+        def begin(g):
+            wide[g].send(0)
+            red[g].send(0)
+
+        def through_two(number, carry):
+            through(2 * number)
+
+            @pl.when(number > 0)
             def _():
-                core_add(2 * step - 1)
-
-            @pl.when(step == 2)
+                core_add(2 * number - 1)
+
+            for g in range(tiles // 2 - 1):
+
+                @pl.when(number == g + 1)
+                def _(g=g):
+                    begin(g)
+
+            through(2 * number + 1)
+            core_add(2 * number)
+
+            @pl.when(number == 2)
             def _():
-                one[0].send(0)
-                two[0].send(0)
-                red[0].send(0)
-
-            back(2 * step + 1)
-            core_add(2 * step)
+                step(wide[0], 0)
+                step(red[0], 0)
+
             return carry
 
-        lax.fori_loop(0, tiles // 2, back_two, 0)
+        lax.fori_loop(0, tiles // 2, through_two, 0)
         core_add(tiles - 1)
-        one[1].send(0)
-        two[1].send(0)
-        red[1].send(0)
-        small_acc[0] = small_in[...]
+        begin(3)
+        step(wide[1], 0)
+        step(red[1], 0)
         for part in range(tiles * TILE // width):
             small_acc[0, pl.ds(EXPAND_BIAS + part, 1), :] = bias_row[pl.ds(0, 1), pl.ds(part * width, width)]
 
-        for load in loads[2:]:
-            load.wait()
         gain_sum = jnp.zeros((1, width), F32)
+        value_sum = jnp.zeros((1, width), F32)
+        mlp_sum = jnp.zeros((1, width), F32)
         for number in range(blocks):
             rows = pl.ds(number * BLOCK, BLOCK)
             here = pl.ds(number, 1)
+            full = reduced[rows, :] + reduce_bias[...]
+            branch = mod_part(number, 5) * full
+            value = hidden[rows, :].astype(F32) + mod_part(number, 2) * projected[rows, :] + branch
+            block_out[rows, :] = value.astype(BF16)
+            value_sum = value_sum + jnp.sum(keep[number] * value * value, axis=0, keepdims=True)
+            mlp_sum = mlp_sum + jnp.sum(keep[number] * branch * branch, axis=0, keepdims=True)
+            grad_out = cotangent[rows, :].astype(F32) * keep[number]
+            mod_rows[here, pl.ds(5 * width, width)] = jnp.sum(grad_out * full, axis=0, keepdims=True)
             grad = grad_normed[rows, :]
             line = normal[rows, :] * second_gain[...]
             mod_rows[here, pl.ds(3 * width, width)] = jnp.sum(grad, axis=0, keepdims=True)
             mod_rows[here, pl.ds(4 * width, width)] = jnp.sum(grad * line, axis=0, keepdims=True)
-            mod_rows[here, pl.ds(5 * width, width)] = gate_grads[here, :]
             grad_line = grad * (1.0 + mod_part(number, 4))
             gain_sum = gain_sum + jnp.sum(grad_line * normal[rows, :], axis=0, keepdims=True)
             grad_normal = grad_line * second_gain[...]
             along = mean_of(grad_normal * normal[rows, :])
             term = (grad_normal - mean_of(grad_normal) - normal[rows, :] * along) * spread_row[rows, :1]
-            total = cotangent[rows, :].astype(F32) * keep[number] + term
+            total = grad_out + term
             grad_middle[rows, :] = total
             mod_rows[here, pl.ds(2 * width, width)] = jnp.sum(total * projected[rows, :], axis=0, keepdims=True)
             grad_low[rows, :] = (mod_part(number, 2) * total).astype(BF16)
+            if number == 2:
+                step(red[2], 0)
         small_acc[0, pl.ds(SECOND_GAIN, 1), :] = gain_sum
+        lane = lane_iota((1, width))
+        counts = jnp.zeros((1, 1), F32)
+        for number in range(blocks):
+            counts = counts + jnp.sum(keep[number], axis=0, keepdims=True)
+        terms = [jnp.sum(term, axis=1, keepdims=True) for term in (value_sum, branch_sum, mlp_sum)] + [counts]
+        stats = jnp.zeros((1, width), F32)
+        for place, term in enumerate(terms):
+            stats = jnp.where(lane == place, term, stats)
+        small_acc[0, pl.ds(STATS, 1), :] = stats
+        for part in range(2, 6):
+            small_acc[0, pl.ds(MOD_BIAS + part, 1), :] = jnp.sum(
+                mod_rows[:, pl.ds(part * width, width)], axis=0, keepdims=True
+            )
+        small_copy(0).start()
+        step(wide[2], 0)
+        wide[0].add(1)
+        step(red[0], 1)
 
         for first in range(0, width, 256):
             grad_attended[:, pl.ds(first, 256)] = dot_nt(
@@ -689,8 +604,8 @@
             delta_features[rows, :] = split_three(dot(upper, chooser) + dot(lower, chooser))
         for load in attention_loads:
             load.wait()
-        for swap in swaps():
-            swap.start()
+        for place in range(HEADS // 2 + 2):
+            swap(place).start()
         for first in range(0, width, TILE):
             output_t = dot_tn(grad_low[:, pl.ds(first, TILE)], attended[...]).astype(BF16)
             for place in range(TILE // 48):
@@ -701,56 +616,59 @@
                         place * 48 : place * 48 + 48, side * LANES : side * LANES + LANES
                     ]
         out.send(0)
-
-    def swaps():
-        partner = (dp, 1 - seq)
-        return [
-            pltpu.make_async_remote_copy(
-                source, target, swap_send.at[number], swap_recv.at[number], device_id=partner, device_id_type=MESH_ID
-            )
-            for number, (source, target) in enumerate(
-                ((grad_attended, other_grad), (delta_features, other_delta), (query_features, other_features))
-            )
-        ]
+        wide[1].add(1)
+        wide_merge[0].send(0)
+        step(red[1], 1)
+
+    def small_copy(number):
+        return pltpu.make_async_remote_copy(
+            small_acc.at[number], small_got.at[number], small_send.at[number], small_recv.at[number],
+            device_id=greet[(1 + number) % len(greet)], device_id_type=MESH_ID,
+        )
+
+    def small_step(number):
+        small_copy(number).wait_recv()
+        small_acc[number + 1] = small_acc[number] + small_got[number]
+        if number + 1 < len(greet):
+            small_copy(number + 1).start()
+
+    def swap(place):
+        if isinstance(place, int) and place < 2:
+            source, target = ((delta_features, other_delta), (query_features, other_features))[place]
+        else:
+            lanes = pl.ds(pl.multiple_of((place - 2) * 128, 128), 128)
+            source, target = grad_attended.at[:, lanes], other_grad.at[:, lanes]
+        return pltpu.make_async_remote_copy(
+            source, target, swap_send.at[place], swap_recv.at[place], device_id=(dp, 1 - seq), device_id_type=MESH_ID
+        )
 
     units = tiles * TILE
+    low_half, wide_half = pltpu.VMEM((tokens, width), BF16), pltpu.VMEM((tokens, width), F32)
     pl.run_scoped(
         mlp_phase,
         pltpu.VMEM((units, width), BF16), pltpu.VMEM((width, units), BF16), pltpu.VMEM((width, width), BF16),
-        pltpu.VMEM((tiles, tokens, TILE), BF16), pltpu.VMEM((tiles, tokens, TILE), BF16),
-        pltpu.VMEM((tokens, width), BF16), pltpu.VMEM((tokens, width), BF16), pltpu.VMEM((width, tokens), BF16),
-        pltpu.VMEM((tokens, width), F32), pltpu.VMEM((tokens, 128), F32), pltpu.VMEM((tokens, width), F32),
-        pltpu.VMEM((tokens, width), BF16), pltpu.VMEM((tokens, width), BF16), pltpu.VMEM((8, units), F32),
-        pltpu.VMEM((tokens, width), F32),
+        low_half, low_half, low_half, low_half, low_half, pltpu.VMEM((width, tokens), BF16),
+        wide_half, pltpu.VMEM((tokens, 128), F32), wide_half, wide_half, pltpu.VMEM((8, units), F32), wide_half,
     )
 
-    def step(stream, stage):
-        stream.add(stage)
-        stream.send(stage + 1)
-
-    def after_all(streams, stage, merge):
-        for stream in streams:
-            stream.add(stage)
-        merge.send(0)
-
     plan = {
-        0: [(step, one[0], 0), (step, two[0], 0)],
-        1: [(step, one[1], 0), (step, two[1], 0)],
-        2: [(step, red[0], 0)],
-        3: [(step, one[0], 1), (step, two[0], 1)],
-        4: [(step, one[1], 1), (step, two[1], 1)],
-        5: [(step, out, 0)],
-        6: [(step, red[1], 0)],
-        7: [(step, red[0], 1)],
-        8: [(after_all, one, 2, one_merge)],
-        9: [(after_all, two, 2, two_merge)],
-        10: [(step, red[1], 1), (step, out, 1)],
-        11: [],
-        12: [(step, out, 2), (after_all, red, 2, red_merge)],
-        13: [(one_merge.add, 0, sums, 0), (two_merge.add, 0, sums, 96)],
-        14: [(step, out, 3)],
+        0: [(step, out, 0)],
+        1: [],
+        2: [(red[0].add, 2), (wide_merge[0].add, 0), (small_step, 0)],
+        3: [(step, red[3], 0)],
+        4: [(step, wide[3], 0), (small_step, 1)],
+        5: [(step, red[2], 1)],
+        6: [(wide[2].add, 1), (small_step, 2)],
+        7: [(red[1].add, 2), (step, out, 1)],
+        8: [(red[2].add, 2), (red_end[0].send, 0), (step, red[3], 1), (small_step, 3)],
+        9: [(wide[3].add, 1), (wide_merge[1].send, 0)],
+        10: [(red[3].add, 2), (red_end[1].send, 0)],
+        11: [(step, out, 2), (small_step, 4)],
+        12: [(wide_merge[1].add, 0), (wide_end.send, 0)],
+        13: [(step, out, 3)],
+        14: [(red_end[0].add, 0, sums, 192), (red_end[1].add, 0, sums, 288)],
         15: [],
-        16: [(red_merge.add, 0, sums, 192)],
+        16: [(wide_end.add, 0, sums, 0)],
         17: [(out.add, 4, sums, 384)],
     }
 
@@ -766,7 +684,7 @@
 
     def attention_phase(normed, hidden, weight, keys_t, grad_query_t, grad_key, grad_value, grad_triple, grad_normed, triple_part):
         loads = [
-            pltpu.make_async_copy(source, target, load_sem.at[13 + number])
+            pltpu.make_async_copy(source, target, load_sem.at[9 + number])
             for number, (source, target) in enumerate(((normed_hbm, normed), (hidden_hbm, hidden), (weight_hbm, weight)))
         ]
         for load in loads:
@@ -809,11 +727,12 @@
             return carry
 
         lax.fori_loop(0, HEADS // 2, own_queries, 0)
-        for swap in swaps():
-            swap.wait_recv()
+        for place in range(2):
+            swap(place).wait_recv()
 
         def other_queries(pair, carry):
             lanes = pl.ds(pl.multiple_of(pair * 128, 128), 128)
+            swap(pair + 2).wait_recv()
             query_pair, grad_pair = queries[1, :, lanes], other_grad[:, lanes]
             pair_lane = lane_iota(query_pair.shape)
             grad_k = grad_key[:, lanes]
@@ -867,7 +786,7 @@
                     ]
         got = (tri_a, tri_b, tri_c, tri_d, tri_e)
         triple = [
-            Stream(kit, 10 + number, triple_part, 48 * number, 48, {}, (CORE,) + order, got, 48 * number)
+            Stream(kit, 14 + number, triple_part, 48 * number, 48, {}, (CORE,) + order, got, 48 * number)
             for number, order in enumerate(((X, Y, Z1, Z2), (Y, Z1, X, Z2), (Z1, X, Y, Z2)))
         ]
         for stream in triple:
@@ -895,25 +814,24 @@
             along = mean_of(grad_normal * normal)
             term = (grad_normal - mean_of(grad_normal) - normal * along) * inverse
             input_grad[rows, :] = (grad_middle[rows, :] + term).astype(BF16)
-        small_acc[0, pl.ds(FIRST_GAIN, 1), :] = gain_sum
-        for part in range(6):
-            small_acc[0, pl.ds(MOD_BIAS + part, 1), :] = jnp.sum(
-                mod_rows[:, pl.ds(part * width, width)], axis=0, keepdims=True
-            )
-
-        def small_copy(number):
+        late_acc[0] = jnp.zeros_like(late_acc[0])
+        late_acc[0, pl.ds(0, 1), :] = gain_sum
+        for part in range(2):
+            late_acc[0, pl.ds(1 + part, 1), :] = jnp.sum(mod_rows[:, pl.ds(part * width, width)], axis=0, keepdims=True)
+
+        def late_copy(number):
             return pltpu.make_async_remote_copy(
-                small_acc.at[number], small_got.at[number], small_send.at[number], small_recv.at[number],
+                late_acc.at[number], late_got.at[number], late_send.at[number], late_recv.at[number],
                 device_id=greet[(1 + number) % len(greet)], device_id_type=MESH_ID,
             )
 
-        def small_step(number):
-            small_copy(number).wait_recv()
-            small_acc[number + 1] = small_acc[number] + small_got[number]
+        def late_step(number):
+            late_copy(number).wait_recv()
+            late_acc[number + 1] = late_acc[number] + late_got[number]
             if number + 1 < len(greet):
-                small_copy(number + 1).start()
-
-        small_copy(0).start()
+                late_copy(number + 1).start()
+
+        late_copy(0).start()
 
         mod_axes = (CORE, Y, Z1, Z2, X)
 
@@ -976,11 +894,11 @@
             copy.start()
 
         for number in range(4):
-            for stream in triple:
-                if number < 3:
+            mod_step(number)
+            late_step(number)
+            if number < 3:
+                for stream in triple:
                     step(stream, number + 1)
-            mod_step(number)
-            small_step(number)
         for number, stream in enumerate(triple):
             stream.add(4, sums, 432 + 48 * number)
         mod_step(4)
@@ -990,9 +908,13 @@
         upper = gathered.astype(BF16)
         lower = (gathered - upper.astype(F32)).astype(BF16)
         mod_out[...] = dot_tn(embedded, upper) + dot_tn(embedded, lower)
+        for number in range(5, len(greet)):
+            small_step(number)
         for number in range(4, len(greet)):
-            small_step(number)
+            late_step(number)
         small_out[...] = small_acc[len(greet)]
+        small_out[pl.ds(FIRST_GAIN, 1), :] = late_acc[len(greet), pl.ds(0, 1), :]
+        small_out[pl.ds(MOD_BIAS, 2), :] = late_acc[len(greet), pl.ds(1, 2), :]
         for stream in triple:
             stream.done()
         for number in range(5):
@@ -1000,6 +922,7 @@
                 copy.wait_send()
         for number in range(len(greet)):
             small_copy(number).wait_send()
+            late_copy(number).wait_send()
 
     pl.run_scoped(
         attention_phase,
@@ -1012,20 +935,20 @@
     for tile in range(tiles):
         for copy in core_copies(tile):
             copy.wait_send()
-    for stream in one + two + red + [one_merge, two_merge, red_merge, out]:
+    for stream in wide + red + wide_merge + red_end + [wide_end, out]:
         stream.done()
-    for swap in swaps():
-        swap.wait_send()
-
-
-def backward(segments, lengths, modulation, gate_grads, small, condition, table, first_gain, second_gain, *arrays):
-    tokens, width = arrays[6].shape
+    for place in range(HEADS // 2 + 2):
+        swap(place).wait_send()
+
+
+def backward(segments, lengths, modulation, condition, table, first_gain, second_gain, expand_bias, reduce_bias, *arrays):
+    tokens, width = arrays[3].shape
     all_bits = lax.axis_size("dp").bit_length() - 1
     extra_bits = all_bits - GROUP_BITS
     steps = all_bits + 1
     smem, vmem = pl.BlockSpec(memory_space=pltpu.SMEM), pl.BlockSpec(memory_space=pltpu.VMEM)
     hbm = pl.BlockSpec(memory_space=pl.ANY)
-    tiles = arrays[3].shape[0]
+    tiles = arrays[0].shape[0] // TILE
 
     def rows_of(count, free, lead=()):
         return pltpu.VMEM(lead + (2,) * free + (count, LANES), BF16)
@@ -1036,7 +959,8 @@
     features = pltpu.VMEM((tokens, 128), BF16)
     both = pltpu.VMEM((2, tokens, width), BF16)
     group_rows = [rows_of(count, free) for count in (48, 144) for free in (4, 3, 2, 1, 0)]
-    halves = [rows_of(count, free, (2,)) if free >= 0 else rows_of(count, 0) for count in (96, 96, 192) for free in (2, 1, 0, -1)]
+    halves = [rows_of(192, 1, (4,)), rows_of(192, 0, (4,)), rows_of(192, 0, (2,)), rows_of(192, 0)]
+    halves += [rows_of(96, 2, (4,)), rows_of(96, 1, (4,)), rows_of(96, 0, (4,)), rows_of(96, 0, (2,))]
     mods = [pltpu.VMEM(shape + (8, LANES), F32) for shape in ((2, 2, 2, 2), (2, 2, 2), (1, 2, 2, 2), (2, 2, 2), (4, 2), (8,), (16,))]
     conds = [pltpu.VMEM(shape + (8, 128), F32) for shape in ((), (), (1,), (2,), (4,), (8,), (16,))]
     dma = pltpu.SemaphoreType.DMA
@@ -1044,12 +968,13 @@
         functools.partial(backward_kernel, extra_bits, all_bits),
         out_shape=(
             jax.ShapeDtypeStruct((tokens, width), BF16),
+            jax.ShapeDtypeStruct((tokens, width), BF16),
             jax.ShapeDtypeStruct((576, LANES), F32),
             jax.ShapeDtypeStruct((128, LANES), F32),
             jax.ShapeDtypeStruct((SMALL_ROWS, width), F32),
         ),
         in_specs=[smem] * 2 + [vmem] * 7 + [hbm] * len(arrays),
-        out_specs=(vmem,) * 4,
+        out_specs=(vmem,) * 5,
         scratch_shapes=[rows_of(192, 5), rows_of(192, 5), rows_of(48, 5), rows_of(192, 4), rows_of(192, 4)]
         + halves
         + group_rows
@@ -1057,14 +982,15 @@
         + [half(F32), half(BF16), features, half(BF16), features, features]
         + [pltpu.VMEM((tokens // BLOCK, 6 * width), F32)]
         + [pltpu.VMEM((steps + 1, SMALL_ROWS, width), F32), pltpu.VMEM((steps, SMALL_ROWS, width), F32)]
+        + [pltpu.VMEM((steps + 1, 8, width), F32), pltpu.VMEM((steps, 8, width), F32)]
         + mods
         + conds
-        + [dma((16,)), dma((4, tiles)), dma((2, tiles)), dma((2, tiles)), dma((13, 5)), dma((13, 5)), dma((3,)), dma((3,))]
-        + [dma((steps,)), dma((steps,)), dma((2, 5)), dma((2, 5))],
+        + [dma((12,)), dma((2, tiles)), dma((2, tiles)), dma((2, tiles)), dma((17, 5)), dma((17, 5)), dma((8,)), dma((8,))]
+        + [dma((steps,)), dma((steps,)), dma((steps,)), dma((steps,)), dma((2, 5)), dma((2, 5))],
         compiler_params=pltpu.CompilerParams(
             collective_id=2, has_side_effects=True, vmem_limit_bytes=63 << 20
         ),
-    )(segments, lengths, modulation, gate_grads, small, condition, table, first_gain, second_gain, *arrays)
+    )(segments, lengths, modulation, condition, table, first_gain, second_gain, expand_bias, reduce_bias, *arrays)
 
 
 def scatter_rest(block, dp_size):
@@ -1100,15 +1026,10 @@
         segment_ids, piece_lengths, time_index, hidden, table, gain_one, modulation_weight,
         modulation_bias[None, :], query_key_value_weight,
     )
-    block_out, grad_low, normed_two, normal, spread_row, projected, gate_grads, small, activated, slope = mlp(
-        segment_ids, piece_lengths, hidden, attended, cot, modulation, gain_two, expand_bias[None, :],
-        reduce_bias[None, :], attention_output_matrix, widen_weight, narrow_weight,
-    )
-    input_grad, block_sum, mod_sum, small_sum = backward(
-        segment_ids, piece_lengths, modulation, gate_grads, small, condition, table, gain_one, gain_two,
-        narrow_weight, widen_weight, attention_output_matrix, activated, slope, normed_two, grad_low, normal,
-        spread_row, projected, attended, cot, queries, keys, values, query_features, key_features, normed, hidden,
-        query_key_value_weight,
+    block_out, input_grad, block_sum, mod_sum, small_sum = backward(
+        segment_ids, piece_lengths, modulation, condition, table, gain_one, gain_two, expand_bias[None, :],
+        reduce_bias[None, :], narrow_weight, widen_weight, attention_output_matrix, attended, cot, queries, keys, values,
+        query_features, key_features, normed, hidden, query_key_value_weight,
     )
     dp_size = lax.axis_size("dp")
     expand_block = scatter_rest(block_sum[:192], dp_size).T

time: 203 us -> 184 us (0.906)
  Pallas kernels: 182 us -> 166 us
  local copies, waits for them, and re-layouts: 17.3 us -> 15.1 us
    pallas_call x1 -> x0, Pallas kernels: 22.9 us -> none  [mlp(): pl.pallas_call(mlp_kernel, out_shape=(jax.ShapeDtypeStruct(half, BF16), j...]
    pallas_call x1, Pallas kernels: 122 us -> 128 us  [backward(): pl.pallas_call(functools.partial(backward_kernel, extra_bits, all_bits),...]
where the time goes in v4:
time: 184 us; the launch traced here: 183 us
  Pallas kernels  166 us (90%)
  local copies, waits for them, and re-layouts  15.1 us (8%)
    pallas_call x1, Pallas kernels, backward(): pl.pallas_call(functools.partial(backward_kernel, extra_bits, all_bits),...  128 us
    pallas_call x1, Pallas kernels, forward(): pl.pallas_call(forward_kernel, out_shape=(half, both, both, both, half, j...  37.5 us

profile of v4, /device:TPU:0, one launch (start us, length us, event | category | flops | bytes accessed | tf_op | source)
XLA Modules:
  0.0 183.4 jit_solution(5655353702011959846)
XLA Ops:
  0.6 1.3 broadcast_in_dim.21.first_gain
  1.9 1.3 broadcast_in_dim.22.mod_bias
  3.3 0.0 copy-start.4
  3.3 0.0 copy-start.5
  3.3 37.5 %shard_map.255 = (bf16[512,768]{1,0:T(8,128)(2,1)}, bf16[2,512,768]{2,1,0:T(8,128)(2,1)}, bf16[2,512,768]{2,1,0:T(8,128)(2,1)}, bf16[2,512,768]{2,1,0:T(8,128)(2...) custom-call(s32[1,1024]{1,0:T(1,128)} %segments.3, ...), custom_call_target="tpu_custom_call" | custom-call | tf_op jit(solution)/shard_map/pallas_call | solution.py:222
  40.7 0.0 copy-done.4
  40.7 0.6 broadcast_in_dim.23.second_gain
  41.3 0.0 copy-done.5
  41.3 0.6 broadcast_in_dim.25.reduce_bias
  41.9 128.3 %shard_map.256 = (bf16[512,768]{1,0:T(8,128)(2,1)}, bf16[512,768]{1,0:T(8,128)(2,1)}, f32[576,384]{1,0:T(8,128)}, f32[128,384]{1,0:T(8,128)}, f32[16,768]{1,0:T(8,128)}) custom-call(s32[1,1024]{1,0:T(1,128)} %segments.3, s32[1,8]{1,0:T(1,128)} %lengths.3, f32[8,4608]{1,0:T(8,128)} %get-tuple-element.27.modulation, f32[8,128]{1,0:T(8,128)} %get-tuple-element.28.condition, ...), custom_call_target="tpu_custom_call" | custom-call | tf_op jit(solution)/shard_map/pallas_call | solution.py:967
  170.2 0.0 copy-start.2
  170.2 0.0 copy-start.3
  170.2 0.0 copy-start.1
  170.2 1.3 slice.52
  172.2 1.2 sqrt_bitcast_fusion
  173.4 1.8 fusion
  175.2 0.0 copy-start
  175.2 0.7 copy.30
  175.9 1.6 slice_bitcast_fusion.1
  177.6 0.0 copy-done.2
  177.6 0.6 constant_dynamic-slice_fusion
  178.2 1.5 slice_bitcast_fusion.2
  179.8 0.0 copy-done.3
  179.8 0.6 reshape.46
  180.4 0.6 reshape.47
  181.0 0.6 slice_reduce_fusion
  181.6 0.0 copy-done.1
  181.6 0.9 copy.33
  182.5 0.0 copy-done
  182.5 0.9 copy.34
  (2 shorter events, 0.0 us)
Async XLA Ops:
  3.3 37.5 %copy-start.4 = (f32[768]{0:T(1024)S(1)}, f32[768]{0:T(1024)}, u32[]{:S(2)}) copy-start(f32[768]{0:T(1024)} %param.25) | copy-start | bytes 9220
  3.3 38.1 %copy-start.5 = (f32[768]{0:T(1024)S(1)}, f32[768]{0:T(1024)}, u32[]{:S(2)}) copy-start(f32[768]{0:T(1024)} %param.29) | copy-start | bytes 9220
  170.2 7.4 %copy-start.2 = (f32[128,384]{1,0:T(8,128)S(1)}, f32[128,384]{1,0:T(8,128)}, u32[]{:S(2)}) copy-start(f32[128,384]{1,0:T(8,128)} %get-tuple-element.39) | copy-start | bytes 589828
  170.2 9.6 %copy-start.3 = (f32[16,768]{1,0:T(8,128)S(1)}, f32[16,768]{1,0:T(8,128)}, u32[]{:S(2)}) copy-start(f32[16,768]{1,0:T(8,128)} %get-tuple-element.38) | copy-start | bytes 147460
  170.2 11.4 %copy-start.1 = (bf16[512,768]{1,0:T(8,128)(2,1)S(1)}, bf16[512,768]{1,0:T(8,128)(2,1)}, u32[]{:S(2)}) copy-start(bf16[512,768]{1,0:T(8,128)(2,1)} %get-tuple-element.36) | copy-start | bytes 2359300
  175.2 7.3 %copy-start = (bf16[512,768]{1,0:T(8,128)(2,1)S(1)}, bf16[512,768]{1,0:T(8,128)(2,1)}, u32[]{:S(2)}) copy-start(bf16[512,768]{1,0:T(8,128)(2,1)} %get-tuple-element.37) | copy-start | bytes 2359300

commit v5 on v4

--- a/solution.py
+++ b/solution.py
@@ -249,6 +249,37 @@
 Z2, Z1, Y, CORE, X = 0, 1, 2, 3, 4
 
 
+WIDE_ORDERS = ((Y, X), (X, Y), (X, Y), (X, Y))
+REDUCE_ORDERS = ((Z1, Y, Z2), (Y, Z1, Z2), (Y, Z2, Z1), (Z2, Y, Z1))
+OUTPUT_ORDER = (CORE, X, Y, Z1, Z2)
+TRIPLE_ORDERS = ((CORE, Y, X, Z1, Z2), (CORE, Z1, Y, X, Z2), (CORE, X, Y, Z1, Z2))
+PLAN = (
+    (("T", 6), (("r", 0), ("w", 0),)),
+    (("T", 7), (("w", 1),)),
+    (("N", 0), (("r", 1),)),
+    (("N", 4), (("w", 2),)),
+    (("D", 0), (("s", 0), ("r", 2),)),
+    (("D", 1), (("r", 0), ("w", 0),)),
+    (("A", 1), (("w", 1), ("o", 0),)),
+    (("A", 3), (("w", 2), ("w", 3),)),
+    (("A", 4), (("r", 3), ("s", 0),)),
+    (("A", 6), (("r", 1),)),
+    (("A", 7), (("w", 3),)),
+    (("A", 9), (("r", 3),)),
+    (("A", 10), (("r", 2),)),
+    (("E", 0), (("r", 0),)),
+    (("B", 0), (("s", 0), ("wm", 0),)),
+    (("B", 3), (("r", 1),)),
+    (("B", 5), (("wm", 1),)),
+    (("C", 0), (("r", 3), ("o", 0),)),
+    (("C", 1), (("s", 0), ("r", 2),)),
+    (("C", 4), (("q", 0),)),
+    (("C", 5), (("q", 1),)),
+    (("C", 6), (("re", 1), ("s", 0),)),
+    (("F", 0), (("q", 2), ("o", 0), ("we", 0), ("re", 0), ("m", 0), ("q", 0), ("q", 1), ("m", 0), ("o", 0), ("q", 2), ("m", 0), ("q", 1), ("o", 0), ("q", 0), ("q", 2), ("q", 1), ("m", 0), ("q", 0), ("q", 2), ("m", 0), ("q", 1), ("q", 0), ("q", 2),)),
+)
+
+
 def exchange_partner(axis, extra_bits):
     dp, seq = lax.axis_index("dp"), lax.axis_index("seq")
     if axis == X:
@@ -263,9 +294,10 @@
 
 
 class Stream:
-    def __init__(self, kit, number, part, first, count, fixed, order, got, got_first=0):
+    def __init__(self, kit, number, part, first, count, fixed, order, got, got_first=0, total_first=None):
         self.kit, self.number, self.part, self.first, self.count = kit, number, part, first, count
         self.fixed, self.order, self.got, self.got_first = fixed, order, got, got_first
+        self.total_first = total_first
 
     def free(self, stage):
         return [axis for axis in range(5) if axis not in self.fixed and axis not in self.order[: stage + 1]]
@@ -291,8 +323,9 @@
     def send(self, stage):
         self.copy(stage).start()
 
-    def add(self, stage, total=None, total_first=0):
+    def add(self, stage):
         self.copy(stage).wait_recv()
+        last = stage == len(self.order) - 1 and self.total_first is not None
         bits, free = self.kit["bits"], self.free(stage)
         rows, got_rows = pl.ds(self.first, self.count), pl.ds(self.got_first, self.count)
 
@@ -305,10 +338,11 @@
                 index[axis] = (step >> (len(free) - 1 - order)) & 1
                 place.append(index[axis])
             mine, theirs = self.part[tuple(index) + (rows,)], self.got[stage][tuple(place) + (got_rows,)]
-            if total is None:
+            if last:
+                total = mine.astype(F32) + theirs.astype(F32)
+                self.kit["sums"][pl.ds(self.total_first, self.count), :] = total
+            else:
                 self.part[tuple(index) + (rows,)] = mine + theirs
-            else:
-                total[pl.ds(total_first, self.count), :] = mine.astype(F32) + theirs.astype(F32)
             return carry
 
         if free:
@@ -332,7 +366,7 @@
     out_a, out_b, out_c, out_d, out_e, tri_a, tri_b, tri_c, tri_d, tri_e,
     queries, keys, values, query_features, key_features,
     grad_middle, grad_attended, delta_features, other_grad, other_delta, other_features, mod_rows,
-    small_acc, small_got, late_acc, late_got, mod_zero, mod_got, mod_one, mod_two, mod_three, mod_four, mod_five,
+    small_acc, small_got, late_acc, late_got, mod_got, mod_two, mod_three, mod_four, mod_five,
     cond_zero, cond_got, cond_one, cond_two, cond_three, cond_four, cond_five,
     load_sem, tile_sem, core_send, core_recv, stream_send, stream_recv, swap_send, swap_recv,
     small_send, small_recv, late_send, late_recv, mod_send, mod_recv,
@@ -343,7 +377,7 @@
     seq = lax.axis_index("seq")
     dp = lax.axis_index("dp")
     bits = [own_bit(axis, extra_bits) for axis in range(5)]
-    kit = {"bits": bits, "send": stream_send, "recv": stream_recv, "extra": extra_bits}
+    kit = {"bits": bits, "send": stream_send, "recv": stream_recv, "extra": extra_bits, "sums": sums}
     core = bits[CORE]
 
     def others(*axes):
@@ -352,21 +386,64 @@
     def chosen(**values):
         return {CORE: core, **{{"z2": Z2, "z1": Z1, "x": X}[name]: value for name, value in values.items()}}
 
-    wide = [
-        Stream(kit, g, expand_part, 0, 192, chosen(z2=g >> 1, z1=g & 1), (Y, X) if g == 3 else (X, Y), (wide_a.at[g], wide_b.at[g]))
-        for g in range(4)
-    ]
-    red = [
-        Stream(
-            kit, 4 + g, reduce_part, 96 * (g & 1), 96, chosen(x=g >> 1), (Y, Z1, Z2) if g & 1 else (Z1, Y, Z2),
+    streams = {}
+    for g in range(4):
+        streams["w", g] = Stream(
+            kit, g, expand_part, 0, 192, chosen(z2=g >> 1, z1=g & 1), WIDE_ORDERS[g], (wide_a.at[g], wide_b.at[g])
+        )
+        streams["r", g] = Stream(
+            kit, 4 + g, reduce_part, 96 * (g & 1), 96, chosen(x=g >> 1), REDUCE_ORDERS[g],
             (red_a.at[g], red_b.at[g], red_c.at[g]),
         )
-        for g in range(4)
-    ]
-    wide_merge = [Stream(kit, 8 + v, expand_part, 0, 192, {**others(Z1, Z2), Z2: v}, (Z1,), (wide_z.at[v],)) for v in range(2)]
-    wide_end = Stream(kit, 10, expand_part, 0, 192, others(Z2), (Z2,), (wide_last,))
-    red_end = [Stream(kit, 11 + h, reduce_part, 96 * h, 96, others(X), (X,), (red_last.at[h],)) for h in range(2)]
-    out = Stream(kit, 13, output_part, 0, 48, {}, (CORE, Y, X, Z1, Z2), (out_a, out_b, out_c, out_d, out_e))
+    for v in range(2):
+        streams["wm", v] = Stream(
+            kit, 8 + v, expand_part, 0, 192, {**others(Z1, Z2), Z2: v}, (Z1,), (wide_z.at[v],)
+        )
+        streams["re", v] = Stream(
+            kit, 11 + v, reduce_part, 96 * v, 96, others(X), (X,), (red_last.at[v],), total_first=192 + 96 * v
+        )
+    streams["we", 0] = Stream(kit, 10, expand_part, 0, 192, others(Z2), (Z2,), (wide_last,), total_first=0)
+    streams["o", 0] = Stream(
+        kit, 13, output_part, 0, 48, {}, OUTPUT_ORDER, (out_a, out_b, out_c, out_d, out_e), total_first=384
+    )
+    merges = {
+        ("wm", 0): (("w", 0), ("w", 1)), ("wm", 1): (("w", 2), ("w", 3)), ("we", 0): (("wm", 0), ("wm", 1)),
+        ("re", 0): (("r", 0), ("r", 2)), ("re", 1): (("r", 1), ("r", 3)),
+    }
+    work, stages, finished = {}, {}, set()
+    for slot, names in PLAN:
+        todo = work.setdefault(slot, [])
+        for name in names:
+            stage = stages.get(name, 0)
+            stages[name] = stage + 1
+            todo.append((True, name, stage))
+            if name[0] in ("m", "s"):
+                continue
+            if stage + 1 < (len(streams[name].order) if name in streams else 5):
+                todo.append((False, name, stage + 1))
+                continue
+            finished.add(name)
+            for merged, parts in merges.items():
+                if name in parts and finished.issuperset(parts):
+                    todo.append((False, merged, 0))
+
+    def perform(slot):
+        for is_add, name, stage in work.get(slot, ()):
+            if name[0] == "s":
+                small_step(stage)
+            elif is_add:
+                streams[name].add(stage)
+            else:
+                streams[name].send(stage)
+
+    def perform_at(letter, first, stride, count, index):
+        for place in range(count):
+            slot = (letter, first + stride * place)
+            if work.get(slot):
+
+                @pl.when(index == place)
+                def _(slot=slot):
+                    perform(slot)
 
     greet = [(dp, 1 - seq)] + [(dp ^ (1 << bit), seq) for bit in range(all_bits)]
     barrier = pltpu.get_barrier_semaphore()
@@ -421,13 +498,9 @@
                     index, got = (z2, z1, y, core, tile >> 2, rows), (z2, z1, y, tile >> 2, rows)
                     reduce_part[index] = reduce_part[index] + reduce_got[got]
 
-    def step(stream, stage):
-        stream.add(stage)
-        stream.send(stage + 1)
-
     def mlp_phase(
-        narrow, widen, out_weight, attended, hidden, cotangent, normed_two, grad_low, grad_low_t, normal, spread_row,
-        projected, reduced, bias_row, grad_normed,
+        narrow, widen, out_weight, attended, hidden, cotangent, normed_two, grad_low, grad_low_t,
+        projected, reduced, grad_normed,
     ):
         def tile_loads(tile):
             lanes = tile_lanes(tile)
@@ -472,9 +545,7 @@
             value = hidden[rows, :].astype(F32) + branch
             centered = value - mean_of(value)
             inverse = lax.rsqrt(mean_of(centered * centered) + 1e-05)
-            normal[rows, :] = centered * inverse
-            spread_row[rows, :] = jnp.broadcast_to(inverse, (BLOCK, 128))
-            line = normal[rows, :] * second_gain[...]
+            line = centered * inverse * second_gain[...]
             normed_two[rows, :] = (line * (1.0 + mod_part(number, 4)) + mod_part(number, 3)).astype(BF16)
         pl.semaphore_wait(barrier, len(greet))
 
@@ -495,7 +566,10 @@
             reduce_t = dot(grad_low_t[...], active).astype(BF16)
             rows = pl.ds(pl.multiple_of((tile & 3) * 48, 16), 48)
             reduce_part[:, :, :, :, tile >> 2, rows] = reduce_t.reshape(2, 2, 2, 2, 48, TILE)
-            bias_row[pl.ds(0, 1), lanes] = jnp.sum(grad_wide.astype(F32), axis=0, keepdims=True)
+            bias_lanes = pl.ds(pl.multiple_of((tile & 1) * TILE, TILE), TILE)
+            small_acc[0, pl.ds(EXPAND_BIAS + (tile >> 1), 1), bias_lanes] = jnp.sum(
+                grad_wide.astype(F32), axis=0, keepdims=True
+            )
             expand_t = dot_tn(grad_wide, normed_two[...]).astype(BF16)
             at = (tile >> 2, (tile >> 1) & 1, tile & 1)
             for group in range(2):
@@ -508,8 +582,8 @@
             grad_normed[...] += dot_nt(grad_wide, widen[:, lanes])
 
         def begin(g):
-            wide[g].send(0)
-            red[g].send(0)
+            streams["w", g].send(0)
+            streams["r", g].send(0)
 
         def through_two(number, carry):
             through(2 * number)
@@ -524,53 +598,47 @@
                 def _(g=g):
                     begin(g)
 
+            perform_at("T", 0, 2, tiles // 2, number)
             through(2 * number + 1)
             core_add(2 * number)
-
-            @pl.when(number == 2)
-            def _():
-                step(wide[0], 0)
-                step(red[0], 0)
-
+            perform_at("T", 1, 2, tiles // 2, number)
             return carry
 
         lax.fori_loop(0, tiles // 2, through_two, 0)
         core_add(tiles - 1)
         begin(3)
-        step(wide[1], 0)
-        step(red[1], 0)
-        for part in range(tiles * TILE // width):
-            small_acc[0, pl.ds(EXPAND_BIAS + part, 1), :] = bias_row[pl.ds(0, 1), pl.ds(part * width, width)]
-
         gain_sum = jnp.zeros((1, width), F32)
         value_sum = jnp.zeros((1, width), F32)
         mlp_sum = jnp.zeros((1, width), F32)
         for number in range(blocks):
+            perform(("N", number))
             rows = pl.ds(number * BLOCK, BLOCK)
             here = pl.ds(number, 1)
             full = reduced[rows, :] + reduce_bias[...]
             branch = mod_part(number, 5) * full
-            value = hidden[rows, :].astype(F32) + mod_part(number, 2) * projected[rows, :] + branch
+            before = hidden[rows, :].astype(F32) + mod_part(number, 2) * projected[rows, :]
+            centered = before - mean_of(before)
+            inverse = lax.rsqrt(mean_of(centered * centered) + 1e-05)
+            normal = centered * inverse
+            value = before + branch
             block_out[rows, :] = value.astype(BF16)
             value_sum = value_sum + jnp.sum(keep[number] * value * value, axis=0, keepdims=True)
             mlp_sum = mlp_sum + jnp.sum(keep[number] * branch * branch, axis=0, keepdims=True)
             grad_out = cotangent[rows, :].astype(F32) * keep[number]
             mod_rows[here, pl.ds(5 * width, width)] = jnp.sum(grad_out * full, axis=0, keepdims=True)
             grad = grad_normed[rows, :]
-            line = normal[rows, :] * second_gain[...]
+            line = normal * second_gain[...]
             mod_rows[here, pl.ds(3 * width, width)] = jnp.sum(grad, axis=0, keepdims=True)
             mod_rows[here, pl.ds(4 * width, width)] = jnp.sum(grad * line, axis=0, keepdims=True)
             grad_line = grad * (1.0 + mod_part(number, 4))
-            gain_sum = gain_sum + jnp.sum(grad_line * normal[rows, :], axis=0, keepdims=True)
+            gain_sum = gain_sum + jnp.sum(grad_line * normal, axis=0, keepdims=True)
             grad_normal = grad_line * second_gain[...]
-            along = mean_of(grad_normal * normal[rows, :])
-            term = (grad_normal - mean_of(grad_normal) - normal[rows, :] * along) * spread_row[rows, :1]
+            along = mean_of(grad_normal * normal)
+            term = (grad_normal - mean_of(grad_normal) - normal * along) * inverse
             total = grad_out + term
             grad_middle[rows, :] = total
             mod_rows[here, pl.ds(2 * width, width)] = jnp.sum(total * projected[rows, :], axis=0, keepdims=True)
             grad_low[rows, :] = (mod_part(number, 2) * total).astype(BF16)
-            if number == 2:
-                step(red[2], 0)
         small_acc[0, pl.ds(SECOND_GAIN, 1), :] = gain_sum
         lane = lane_iota((1, width))
         counts = jnp.zeros((1, 1), F32)
@@ -586,9 +654,7 @@
                 mod_rows[:, pl.ds(part * width, width)], axis=0, keepdims=True
             )
         small_copy(0).start()
-        step(wide[2], 0)
-        wide[0].add(1)
-        step(red[0], 1)
+        perform(("N", blocks))
 
         for first in range(0, width, 256):
             grad_attended[:, pl.ds(first, 256)] = dot_nt(
@@ -606,6 +672,7 @@
             load.wait()
         for place in range(HEADS // 2 + 2):
             swap(place).start()
+        perform(("D", 0))
         for first in range(0, width, TILE):
             output_t = dot_tn(grad_low[:, pl.ds(first, TILE)], attended[...]).astype(BF16)
             for place in range(TILE // 48):
@@ -615,10 +682,8 @@
                     output_part[at + (side,)] = output_t[
                         place * 48 : place * 48 + 48, side * LANES : side * LANES + LANES
                     ]
-        out.send(0)
-        wide[1].add(1)
-        wide_merge[0].send(0)
-        step(red[1], 1)
+        streams["o", 0].send(0)
+        perform(("D", 1))
 
     def small_copy(number):
         return pltpu.make_async_remote_copy(
@@ -648,41 +713,10 @@
         mlp_phase,
         pltpu.VMEM((units, width), BF16), pltpu.VMEM((width, units), BF16), pltpu.VMEM((width, width), BF16),
         low_half, low_half, low_half, low_half, low_half, pltpu.VMEM((width, tokens), BF16),
-        wide_half, pltpu.VMEM((tokens, 128), F32), wide_half, wide_half, pltpu.VMEM((8, units), F32), wide_half,
+        wide_half, wide_half, wide_half,
     )
 
-    plan = {
-        0: [(step, out, 0)],
-        1: [],
-        2: [(red[0].add, 2), (wide_merge[0].add, 0), (small_step, 0)],
-        3: [(step, red[3], 0)],
-        4: [(step, wide[3], 0), (small_step, 1)],
-        5: [(step, red[2], 1)],
-        6: [(wide[2].add, 1), (small_step, 2)],
-        7: [(red[1].add, 2), (step, out, 1)],
-        8: [(red[2].add, 2), (red_end[0].send, 0), (step, red[3], 1), (small_step, 3)],
-        9: [(wide[3].add, 1), (wide_merge[1].send, 0)],
-        10: [(red[3].add, 2), (red_end[1].send, 0)],
-        11: [(step, out, 2), (small_step, 4)],
-        12: [(wide_merge[1].add, 0), (wide_end.send, 0)],
-        13: [(step, out, 3)],
-        14: [(red_end[0].add, 0, sums, 192), (red_end[1].add, 0, sums, 288)],
-        15: [],
-        16: [(wide_end.add, 0, sums, 0)],
-        17: [(out.add, 4, sums, 384)],
-    }
-
-    def run_plan(pair, first, stride, count):
-        for place in range(count):
-            actions = plan[first + stride * place]
-            if actions:
-
-                @pl.when(pair == place)
-                def _(actions=actions):
-                    for action in actions:
-                        action[0](*action[1:])
-
-    def attention_phase(normed, hidden, weight, keys_t, grad_query_t, grad_key, grad_value, grad_triple, grad_normed, triple_part):
+    def attention_phase(normed, hidden, weight, keys_t, grad_query_t, grad_key, grad_value, grad_triple, grad_normed, triple_part, mod_zero, mod_one):
         loads = [
             pltpu.make_async_copy(source, target, load_sem.at[9 + number])
             for number, (source, target) in enumerate(((normed_hbm, normed), (hidden_hbm, hidden), (weight_hbm, weight)))
@@ -723,10 +757,36 @@
                             grad_key[:, lanes] += grad_k
                     grad_q = grad_q + dot(keys_t[part, head_rows, :], grad_scores)
                 grad_query_t[head_rows, :] = grad_q
-                run_plan(pair, half, 2, HEADS // 2)
+                perform_at("A", half, 2, HEADS // 2, pair)
             return carry
 
         lax.fori_loop(0, HEADS // 2, own_queries, 0)
+        for load in loads:
+            load.wait()
+        turns = []
+        grad_normed[...] = jnp.transpose(grad_query_t[...])
+        for number in range(blocks):
+            rows = pl.ds(number * BLOCK, BLOCK)
+            before = block_place(segments, lengths, seq * blocks + number)[1]
+            cosine, sine = rotary_block(table, before)
+            turns.append((cosine, -sine))
+            for pair in range(HEADS // 2):
+                lanes = pl.ds(pair * 128, 128)
+                grad_triple[rows, lanes] = (turn(grad_normed[rows, lanes], cosine, -sine) * 0.125).astype(BF16)
+
+        def third(part):
+            triple_t = dot_tn(grad_triple[:, pl.ds(part * width, width)], normed[...]).astype(BF16)
+            for place in range(width // 48):
+                group, piece = divmod(part * (width // 48) + place, 3)
+                at = (group >> 3, (group >> 2) & 1, (group >> 1) & 1, group & 1)
+                for side in range(2):
+                    triple_part[at + (side, pl.ds(48 * piece, 48))] = triple_t[
+                        place * 48 : place * 48 + 48, side * LANES : side * LANES + LANES
+                    ]
+
+        third(0)
+        grad_normed[...] = dot_nt(grad_triple[:, pl.ds(0, width)], weight[:, pl.ds(0, width)])
+        perform(("E", 0))
         for place in range(2):
             swap(place).wait_recv()
 
@@ -758,45 +818,34 @@
                 grad_k = grad_k + dot(grad_scores, query)
             grad_key[:, lanes] = grad_k
             grad_value[:, lanes] = grad_v
-            run_plan(pair, 12, 1, HEADS // 2)
+            perform_at("B", 0, 1, HEADS // 2, pair)
             return carry
 
         lax.fori_loop(0, HEADS // 2, other_queries, 0)
 
-        grad_normed[...] = jnp.transpose(grad_query_t[...])
         for number in range(blocks):
             rows = pl.ds(number * BLOCK, BLOCK)
-            before = block_place(segments, lengths, seq * blocks + number)[1]
-            cosine, sine = rotary_block(table, before)
             for pair in range(HEADS // 2):
                 lanes = pl.ds(pair * 128, 128)
-                grad_triple[rows, lanes] = (turn(grad_normed[rows, lanes], cosine, -sine) * 0.125).astype(BF16)
-                grad_triple[rows, pl.ds(width + pair * 128, 128)] = turn(grad_key[rows, lanes], cosine, -sine).astype(BF16)
+                grad_triple[rows, pl.ds(width + pair * 128, 128)] = turn(grad_key[rows, lanes], *turns[number]).astype(BF16)
             grad_triple[rows, pl.ds(2 * width, width)] = grad_value[rows, :].astype(BF16)
-
-        for load in loads:
-            load.wait()
-        for part in range(2):
-            triple_t = dot_tn(grad_triple[:, pl.ds(part * 1152, 1152)], normed[...]).astype(BF16)
-            for place in range(8):
-                at = (part, place >> 2, (place >> 1) & 1, place & 1)
-                for side in range(2):
-                    triple_part[at + (side,)] = triple_t[
-                        place * 144 : place * 144 + 144, side * LANES : side * LANES + LANES
-                    ]
-        got = (tri_a, tri_b, tri_c, tri_d, tri_e)
+        third(1)
+        third(2)
         triple = [
-            Stream(kit, 14 + number, triple_part, 48 * number, 48, {}, (CORE,) + order, got, 48 * number)
-            for number, order in enumerate(((X, Y, Z1, Z2), (Y, Z1, X, Z2), (Z1, X, Y, Z2)))
+            Stream(
+                kit, 14 + number, triple_part, 48 * number, 48, {}, order, (tri_a, tri_b, tri_c, tri_d, tri_e),
+                48 * number, 432 + 48 * number,
+            )
+            for number, order in enumerate(TRIPLE_ORDERS)
         ]
-        for stream in triple:
+        for number, stream in enumerate(triple):
+            streams["q", number] = stream
             stream.send(0)
-        grad_normed[...] = jnp.zeros_like(grad_normed)
-        for first in range(0, 3 * width, width):
-            lanes = pl.ds(first, width)
+        perform(("C", 0))
+        for part in range(1, 3):
+            lanes = pl.ds(part * width, width)
             grad_normed[...] += dot_nt(grad_triple[:, lanes], weight[:, lanes])
-        for stream in triple:
-            step(stream, 0)
+            perform(("C", part))
 
         gain_sum = jnp.zeros((1, width), F32)
         for number in range(blocks):
@@ -814,6 +863,7 @@
             along = mean_of(grad_normal * normal)
             term = (grad_normal - mean_of(grad_normal) - normal * along) * inverse
             input_grad[rows, :] = (grad_middle[rows, :] + term).astype(BF16)
+            perform(("C", 3 + number))
         late_acc[0] = jnp.zeros_like(late_acc[0])
         late_acc[0, pl.ds(0, 1), :] = gain_sum
         for part in range(2):
@@ -893,15 +943,16 @@
         for copy in mod_copies(0):
             copy.start()
 
-        for number in range(4):
-            mod_step(number)
-            late_step(number)
-            if number < 3:
-                for stream in triple:
-                    step(stream, number + 1)
-        for number, stream in enumerate(triple):
-            stream.add(4, sums, 432 + 48 * number)
-        mod_step(4)
+        for is_add, name, stage in work[("F", 0)]:
+            if name[0] == "m":
+                mod_step(stage)
+                late_step(stage)
+            elif name[0] == "s":
+                small_step(stage)
+            elif is_add:
+                streams[name].add(stage)
+            else:
+                streams[name].send(stage)
         chunk_rows = mod_five.shape[0] * mod_five.shape[1]
         gathered = mod_five[...].reshape(chunk_rows, LANES)
         embedded = cond_five[...].reshape(chunk_rows, 128).astype(BF16)
@@ -910,7 +961,7 @@
         mod_out[...] = dot_tn(embedded, upper) + dot_tn(embedded, lower)
         for number in range(5, len(greet)):
             small_step(number)
-        for number in range(4, len(greet)):
+        for number in range(5, len(greet)):
             late_step(number)
         small_out[...] = small_acc[len(greet)]
         small_out[pl.ds(FIRST_GAIN, 1), :] = late_acc[len(greet), pl.ds(0, 1), :]
@@ -930,13 +981,15 @@
         pltpu.VMEM((2, width, tokens), BF16), pltpu.VMEM((width, tokens), F32), pltpu.VMEM((tokens, width), F32),
         pltpu.VMEM((tokens, width), F32), pltpu.VMEM((tokens, 3 * width), BF16), pltpu.VMEM((tokens, width), F32),
         pltpu.VMEM((2, 2, 2, 2, 2, 144, LANES), BF16),
+        pltpu.VMEM((2, 2, 2, 2, 8, LANES), F32), pltpu.VMEM((1, 2, 2, 2, 8, LANES), F32),
     )
 
     for tile in range(tiles):
         for copy in core_copies(tile):
             copy.wait_send()
-    for stream in wide + red + wide_merge + red_end + [wide_end, out]:
-        stream.done()
+    for name, stream in streams.items():
+        if name[0] != "q":
+            stream.done()
     for place in range(HEADS // 2 + 2):
         swap(place).wait_send()
 
@@ -961,7 +1014,7 @@
     group_rows = [rows_of(count, free) for count in (48, 144) for free in (4, 3, 2, 1, 0)]
     halves = [rows_of(192, 1, (4,)), rows_of(192, 0, (4,)), rows_of(192, 0, (2,)), rows_of(192, 0)]
     halves += [rows_of(96, 2, (4,)), rows_of(96, 1, (4,)), rows_of(96, 0, (4,)), rows_of(96, 0, (2,))]
-    mods = [pltpu.VMEM(shape + (8, LANES), F32) for shape in ((2, 2, 2, 2), (2, 2, 2), (1, 2, 2, 2), (2, 2, 2), (4, 2), (8,), (16,))]
+    mods = [pltpu.VMEM(shape + (8, LANES), F32) for shape in ((2, 2, 2), (2, 2, 2), (4, 2), (8,), (16,))]
     conds = [pltpu.VMEM(shape + (8, 128), F32) for shape in ((), (), (1,), (2,), (4,), (8,), (16,))]
     dma = pltpu.SemaphoreType.DMA
     return pl.pallas_call(

time: 184 us -> 163 us (0.89)
  Pallas kernels: 166 us -> 143 us
    pallas_call x1, Pallas kernels: 128 us -> 106 us  [backward(): pl.pallas_call(functools.partial(backward_kernel, extra_bits, all_bits),...]
where the time goes in v5:
time: 163 us; the launch traced here: 161 us
  Pallas kernels  143 us (88%)
  local copies, waits for them, and re-layouts  15.1 us (9%)
    pallas_call x1, Pallas kernels, backward(): pl.pallas_call(functools.partial(backward_kernel, extra_bits, all_bits),...  106 us
    pallas_call x1, Pallas kernels, forward(): pl.pallas_call(forward_kernel, out_shape=(half, both, both, both, half, j...  37.5 us

profile of v5, /device:TPU:0, one launch (start us, length us, event | category | flops | bytes accessed | tf_op | source)
XLA Modules:
  0.0 160.9 jit_solution(5472221307005184813)
XLA Ops:
  0.6 1.3 broadcast_in_dim.21.first_gain
  1.9 1.3 broadcast_in_dim.22.mod_bias
  3.3 0.0 copy-start.4
  3.3 0.0 copy-start.5
  3.3 37.5 %shard_map.255 = (bf16[512,768]{1,0:T(8,128)(2,1)}, bf16[2,512,768]{2,1,0:T(8,128)(2,1)}, bf16[2,512,768]{2,1,0:T(8,128)(2,1)}, bf16[2,512,768]{2,1,0:T(8,128)(2...) custom-call(s32[1,1024]{1,0:T(1,128)} %segments.3, ...), custom_call_target="tpu_custom_call" | custom-call | tf_op jit(solution)/shard_map/pallas_call | solution.py:222
  40.7 0.0 copy-done.4
  40.7 0.6 broadcast_in_dim.23.second_gain
  41.3 0.0 copy-done.5
  41.3 0.6 broadcast_in_dim.25.reduce_bias
  41.9 105.8 %shard_map.256 = (bf16[512,768]{1,0:T(8,128)(2,1)}, bf16[512,768]{1,0:T(8,128)(2,1)}, f32[576,384]{1,0:T(8,128)}, f32[128,384]{1,0:T(8,128)}, f32[16,768]{1,0:T(8,128)}) custom-call(s32[1,1024]{1,0:T(1,128)} %segments.3, s32[1,8]{1,0:T(1,128)} %lengths.3, f32[8,4608]{1,0:T(8,128)} %get-tuple-element.27.modulation, f32[8,128]{1,0:T(8,128)} %get-tuple-element.28.condition, ...), custom_call_target="tpu_custom_call" | custom-call | tf_op jit(solution)/shard_map/pallas_call | solution.py:1020
  147.7 0.0 copy-start.2
  147.7 0.0 copy-start.3
  147.7 0.0 copy-start.1
  147.7 1.3 slice.52
  149.7 1.2 sqrt_bitcast_fusion
  150.9 1.8 %fusion = (f32[192,384]{1,0:T(8,128)S(1)}, f32[384,192]{0,1:T(8,128)}) fusion(f32[576,384]{1,0:T(8,128)} %get-tuple-element.40), kind=kLoop, calls=%fused_computation.8 | loop fusion | bytes 1179648 | tf_op jit(solution)/shard_map/slice | solution.py:1089
  152.7 0.0 copy-start
  152.7 0.7 copy.30
  153.5 1.6 %slice_bitcast_fusion.1 = f32[384,144]{0,1:T(8,128)} fusion(f32[576,384]{1,0:T(8,128)} %get-tuple-element.40), kind=kLoop, calls=%fused_computation.1 | loop fusion | bytes 442368 | tf_op jit(solution)/shard_map/transpose | solution.py:1092
  155.1 0.0 copy-done.2
  155.1 0.6 constant_dynamic-slice_fusion
  155.8 1.5 slice_bitcast_fusion.2
  157.3 0.0 copy-done.3
  157.3 0.6 reshape.46
  157.9 0.6 reshape.47
  158.5 0.6 slice_reduce_fusion
  159.1 0.0 copy-done.1
  159.1 0.9 copy.33
  160.0 0.0 copy-done
  160.0 0.9 copy.34
  (2 shorter events, 0.0 us)
Async XLA Ops:
  3.3 37.5 %copy-start.4 = (f32[768]{0:T(1024)S(1)}, f32[768]{0:T(1024)}, u32[]{:S(2)}) copy-start(f32[768]{0:T(1024)} %param.25) | copy-start | bytes 9220
  3.3 38.1 %copy-start.5 = (f32[768]{0:T(1024)S(1)}, f32[768]{0:T(1024)}, u32[]{:S(2)}) copy-start(f32[768]{0:T(1024)} %param.29) | copy-start | bytes 9220
  147.7 7.4 %copy-start.2 = (f32[128,384]{1,0:T(8,128)S(1)}, f32[128,384]{1,0:T(8,128)}, u32[]{:S(2)}) copy-start(f32[128,384]{1,0:T(8,128)} %get-tuple-element.39) | copy-start | bytes 589828
  147.7 9.6 %copy-start.3 = (f32[16,768]{1,0:T(8,128)S(1)}, f32[16,768]{1,0:T(8,128)}, u32[]{:S(2)}) copy-start(f32[16,768]{1,0:T(8,128)} %get-tuple-element.38) | copy-start | bytes 147460
  147.7 11.4 %copy-start.1 = (bf16[512,768]{1,0:T(8,128)(2,1)S(1)}, bf16[512,768]{1,0:T(8,128)(2,1)}, u32[]{:S(2)}) copy-start(bf16[512,768]{1,0:T(8,128)(2,1)} %get-tuple-element.36) | copy-start | bytes 2359300
  152.7 7.3 %copy-start = (bf16[512,768]{1,0:T(8,128)(2,1)S(1)}, bf16[512,768]{1,0:T(8,128)(2,1)}, u32[]{:S(2)}) copy-start(bf16[512,768]{1,0:T(8,128)(2,1)} %get-tuple-element.37) | copy-start | bytes 2359300

commit v6 on v5

--- a/solution.py
+++ b/solution.py
@@ -51,6 +51,10 @@
     return lax.dot_general(left, right, (((0,), (0,)), ((), ())), preferred_element_type=F32)
 
 
+def as_row(vector):
+    return vector[...].reshape(1, -1)
+
+
 def lane_iota(shape):
     return lax.broadcasted_iota(jnp.int32, shape, len(shape) - 1)
 
@@ -110,10 +114,15 @@
     barrier = pltpu.get_barrier_semaphore()
     pl.semaphore_signal(barrier, inc=1, device_id=partner, device_id_type=MESH_ID)
     pl.semaphore_wait(barrier, 1)
-    exchange = pltpu.make_async_remote_copy(
-        hidden, other_hidden, send_sem, recv_sem, device_id=partner, device_id_type=MESH_ID
-    )
-    exchange.start()
+    exchanges = [
+        pltpu.make_async_remote_copy(
+            hidden.at[pl.ds(place * tokens // 2, tokens // 2)], other_hidden.at[pl.ds(place * tokens // 2, tokens // 2)],
+            send_sem.at[place], recv_sem.at[place], device_id=partner, device_id_type=MESH_ID,
+        )
+        for place in range(2)
+    ]
+    for exchange in exchanges:
+        exchange.start()
 
     places = []
     for number in range(2 * blocks):
@@ -127,17 +136,20 @@
         sine = sin_high * cos_low + cos_high * sin_low
         row = jnp.where(lane_iota(cosine.shape) < 64, cosine, sine)
         condition[pl.ds(number, 1), :] = row.astype(BF16).astype(F32)
-    modulation[...] = dot(condition[...].astype(BF16), mod_weight[...]) + mod_bias[...]
+    modulation[...] = dot(condition[...].astype(BF16), mod_weight[...]) + as_row(mod_bias)
 
     lane = lane_iota((BLOCK, 128))
     row = row_iota((BLOCK, 128))
 
-    for part in range(2):
+    half_blocks = blocks // 2
+    sections = ((0, 0, blocks), (1, 0, half_blocks), (1, half_blocks, half_blocks))
+    for section, (part, first_block, count) in enumerate(sections):
         source = hidden if part == 0 else other_hidden
         if part == 1:
-            exchange.wait_recv()
+            exchanges[section - 1].wait_recv()
+        section_rows = pl.ds(first_block * BLOCK, count * BLOCK)
         turns = []
-        for number in range(blocks):
+        for number in range(first_block, first_block + count):
             rows = pl.ds(number * BLOCK, BLOCK)
             segment, before, valid_count = places[part * blocks + number]
             turns.append(rotary_block(table, before))
@@ -152,7 +164,7 @@
             value = source[rows, :].astype(F32)
             centered = value - mean_of(value)
             spread = mean_of(centered * centered)
-            line = centered * lax.rsqrt(spread + 1e-05) * first_gain[...]
+            line = centered * lax.rsqrt(spread + 1e-05) * as_row(first_gain)
             result = (line * (1.0 + scale) + shift).astype(BF16)
             if part == 0:
                 normed[rows, :] = result
@@ -161,44 +173,50 @@
         normed_source = normed if part == 0 else other_hidden
         for tile in range(3 * width // LANES):
             which, first = divmod(tile * LANES, width)
-            product = dot(normed_source[...], weight[:, pl.ds(tile * LANES, LANES)])
+            product = dot(normed_source[section_rows, :], weight[:, pl.ds(tile * LANES, LANES)])
             target = (queries, keys, values)[which]
-            for number in range(blocks):
-                cosine, sine = turns[number]
+            for place in range(count):
+                cosine, sine = turns[place]
                 for pair in range(LANES // 128):
-                    piece = product[number * BLOCK : (number + 1) * BLOCK, pair * 128 : (pair + 1) * 128]
+                    piece = product[place * BLOCK : (place + 1) * BLOCK, pair * 128 : (pair + 1) * 128]
                     if which < 2:
                         piece = turn(piece, cosine, sine)
                     if which == 0:
                         piece = piece.astype(BF16).astype(F32) * 0.125
-                    target[part, pl.ds(number * BLOCK, BLOCK), pl.ds(first + pair * 128, 128)] = piece.astype(BF16)
-        turned_values[...] = jnp.transpose(values[part])
+                    rows = pl.ds((first_block + place) * BLOCK, BLOCK)
+                    target[part, rows, pl.ds(first + pair * 128, 128)] = piece.astype(BF16)
+        turned_rows = pl.ds(0, count * BLOCK)
+        turned_values[:, turned_rows] = jnp.transpose(values[part, section_rows, :])
 
         def attend(pair, carry):
             lanes = pl.ds(pl.multiple_of(pair * 128, 128), 128)
-            query_pair, key_pair = queries[0, :, lanes], keys[part, :, lanes]
-            left = jnp.concatenate([key_pair, key_features[part]], axis=1)
+            query_pair, key_pair = queries[0, :, lanes], keys[part, section_rows, lanes]
+            left = jnp.concatenate([key_pair, key_features[part, section_rows, :]], axis=1)
             pair_lane = lane_iota(query_pair.shape)
+            both = []
             for half in range(2):
+                query = jnp.where((pair_lane < 64) == (half == 0), query_pair, jnp.zeros_like(query_pair))
+                both.append(dot_nt(left, jnp.concatenate([query, query_features[...]], axis=1)))
+            for half, scores in enumerate(both):
                 head = pair * 2 + half
                 head_rows = pl.ds(pl.multiple_of(head * 64, 64), 64)
                 one_row = pl.ds(head, 1)
-                query = jnp.where((pair_lane < 64) == (half == 0), query_pair, jnp.zeros_like(query_pair))
-                scores = dot_nt(left, jnp.concatenate([query, query_features[...]], axis=1))
                 top = jnp.max(scores, axis=0, keepdims=True)
-                if part == 1:
+                if section > 0:
                     top = jnp.maximum(top, peak[one_row, :])
                 weights = jnp.exp(scores - top)
                 summed = jnp.sum(weights, axis=0, keepdims=True)
-                mixed = dot(turned_values[head_rows, :], weights.astype(BF16))
-                if part == 0:
+                mixed = dot(turned_values[head_rows, turned_rows], weights.astype(BF16))
+                if section > 0:
+                    rescale = jnp.exp(peak[one_row, :] - top)
+                    summed = summed + rescale * total[one_row, :]
+                    mixed = mixed + out_t[head_rows, :] * rescale
+                if section < len(sections) - 1:
                     out_t[head_rows, :] = mixed
                     total[one_row, :] = summed
                     peak[one_row, :] = top
                 else:
-                    rescale = jnp.exp(peak[one_row, :] - top)
-                    summed = summed + rescale * total[one_row, :]
-                    out_t[head_rows, :] = (out_t[head_rows, :] * rescale + mixed) * (1.0 / summed)
+                    out_t[head_rows, :] = mixed * (1.0 / summed)
                     peak[one_row, :] = top + jnp.log(summed)
             return carry
 
@@ -210,7 +228,8 @@
         + [jnp.zeros((128 - 3 * HEADS, tokens), F32)], axis=0,
     )
     query_features[...] = query_features[...] + split_three(jnp.transpose(log_rows))
-    exchange.wait_send()
+    for exchange in exchanges:
+        exchange.wait_send()
 
 
 def forward(segments, lengths, times, hidden, table, first_gain, mod_weight, mod_bias, weight):
@@ -236,8 +255,8 @@
             pltpu.VMEM((width, tokens), F32),
             pltpu.VMEM((16, tokens), F32),
             pltpu.VMEM((16, tokens), F32),
-            pltpu.SemaphoreType.DMA,
-            pltpu.SemaphoreType.DMA,
+            pltpu.SemaphoreType.DMA((2,)),
+            pltpu.SemaphoreType.DMA((2,)),
         ],
         compiler_params=pltpu.CompilerParams(
             collective_id=1, has_side_effects=True, vmem_limit_bytes=56 << 20
@@ -545,7 +564,7 @@
             value = hidden[rows, :].astype(F32) + branch
             centered = value - mean_of(value)
             inverse = lax.rsqrt(mean_of(centered * centered) + 1e-05)
-            line = centered * inverse * second_gain[...]
+            line = centered * inverse * as_row(second_gain)
             normed_two[rows, :] = (line * (1.0 + mod_part(number, 4)) + mod_part(number, 3)).astype(BF16)
         pl.semaphore_wait(barrier, len(greet))
 
@@ -553,7 +572,7 @@
             lanes = tile_lanes(tile)
             for load in tile_loads(tile):
                 load.wait()
-            u = dot(normed_two[...], widen[:, lanes]) + expand_bias[:, lanes]
+            u = dot(normed_two[...], widen[:, lanes]) + expand_bias[lanes].reshape(1, TILE)
             grad_active = dot_nt(grad_low[...], narrow[lanes, :])
             square = u * u
             tanh = jnp.tanh(u * (0.7978845608028654 + 0.7978845608028654 * 0.044715 * square))
@@ -614,7 +633,7 @@
             perform(("N", number))
             rows = pl.ds(number * BLOCK, BLOCK)
             here = pl.ds(number, 1)
-            full = reduced[rows, :] + reduce_bias[...]
+            full = reduced[rows, :] + as_row(reduce_bias)
             branch = mod_part(number, 5) * full
             before = hidden[rows, :].astype(F32) + mod_part(number, 2) * projected[rows, :]
             centered = before - mean_of(before)
@@ -627,12 +646,12 @@
             grad_out = cotangent[rows, :].astype(F32) * keep[number]
             mod_rows[here, pl.ds(5 * width, width)] = jnp.sum(grad_out * full, axis=0, keepdims=True)
             grad = grad_normed[rows, :]
-            line = normal * second_gain[...]
+            line = normal * as_row(second_gain)
             mod_rows[here, pl.ds(3 * width, width)] = jnp.sum(grad, axis=0, keepdims=True)
             mod_rows[here, pl.ds(4 * width, width)] = jnp.sum(grad * line, axis=0, keepdims=True)
             grad_line = grad * (1.0 + mod_part(number, 4))
             gain_sum = gain_sum + jnp.sum(grad_line * normal, axis=0, keepdims=True)
-            grad_normal = grad_line * second_gain[...]
+            grad_normal = grad_line * as_row(second_gain)
             along = mean_of(grad_normal * normal)
             term = (grad_normal - mean_of(grad_normal) - normal * along) * inverse
             total = grad_out + term
@@ -856,10 +875,10 @@
             normal = centered * inverse
             grad = grad_normed[rows, :]
             mod_rows[here, pl.ds(0, width)] = jnp.sum(grad, axis=0, keepdims=True)
-            mod_rows[here, pl.ds(width, width)] = jnp.sum(grad * (normal * first_gain[...]), axis=0, keepdims=True)
+            mod_rows[here, pl.ds(width, width)] = jnp.sum(grad * (normal * as_row(first_gain)), axis=0, keepdims=True)
             grad_line = grad * (1.0 + mod_part(number, 1))
             gain_sum = gain_sum + jnp.sum(grad_line * normal, axis=0, keepdims=True)
-            grad_normal = grad_line * first_gain[...]
+            grad_normal = grad_line * as_row(first_gain)
             along = mean_of(grad_normal * normal)
             term = (grad_normal - mean_of(grad_normal) - normal * along) * inverse
             input_grad[rows, :] = (grad_middle[rows, :] + term).astype(BF16)
@@ -1054,6 +1073,54 @@
     return lax.psum_scatter(block, "dp", scatter_dimension=0, axis_index_groups=groups, tiled=True)
 
 
+def finish_kernel(
+    block_in, grad_in, sums, mod_sum, small,
+    block_out, input_grad, first_gain, mod_block, mod_bias, triple_block, output_block, second_gain, expand_block,
+    expand_bias, reduce_block, reduce_bias, masked_rms,
+):
+    width = first_gain.shape[0]
+    block_out[...] = block_in[...]
+    input_grad[...] = grad_in[...]
+    expand_block[...] = sums[pl.ds(0, 192), :]
+    for chunk in range(4):
+        reduce_block[:, pl.ds(chunk * LANES, LANES)] = sums[pl.ds(192 + 48 * chunk, 48), :]
+    output_block[...] = sums[pl.ds(384, 48), :]
+    triple_block[...] = sums[pl.ds(432, 144), :]
+    half = mod_sum.shape[0] // 2
+    first_row = pl.multiple_of(lax.axis_index("seq") * half, half)
+    mod_block[...] = mod_sum[pl.ds(first_row, half), pl.ds(0, mod_block.shape[1])]
+    for target, first in (
+        (first_gain, FIRST_GAIN), (mod_bias, MOD_BIAS), (second_gain, SECOND_GAIN), (expand_bias, EXPAND_BIAS),
+        (reduce_bias, REDUCE_BIAS),
+    ):
+        for part in range(target.shape[0] // width):
+            target[pl.ds(part * width, width)] = small[first + part, :]
+    count = jnp.sum(jnp.where(lane_iota((1, width)) == 3, small[pl.ds(STATS, 1), :], 0.0))
+    masked_rms[...] = jnp.sqrt(small[pl.ds(STATS, 1), pl.ds(0, 128)] / (count * width))
+
+
+def finish(block_out, input_grad, sums, mod_sum, small):
+    width = small.shape[1]
+    vmem = pl.BlockSpec(memory_space=pltpu.VMEM)
+    shapes = (
+        (width,), (mod_sum.shape[0] // 2, 6 * width // 16), (6 * width,), (144, LANES), (48, LANES), (width,), (192, LANES),
+        (4 * width,), (48, 4 * LANES), (width,), (1, 128),
+    )
+    block_out, input_grad, *rest = pl.pallas_call(
+        finish_kernel,
+        out_shape=(
+            jax.ShapeDtypeStruct(block_out.shape, block_out.dtype),
+            jax.ShapeDtypeStruct(input_grad.shape, input_grad.dtype),
+        )
+        + tuple(jax.ShapeDtypeStruct(shape, F32) for shape in shapes),
+        in_specs=[vmem] * 5,
+        out_specs=(vmem,) * (2 + len(shapes)),
+    )(block_out, input_grad, sums, mod_sum, small)
+    for place in (3, 4, 6, 8):
+        rest[place] = rest[place].T
+    return (block_out, input_grad, *rest[:-1], rest[-1][0, :3])
+
+
 def local(
     hidden_in,
     segment_ids,
@@ -1074,17 +1141,20 @@
     slot_count, own_rows, width = hidden_in.shape
     hidden, cot = hidden_in[0], cotangent[0]
     table = jnp.asarray(angle_table())
-    gain_one, gain_two = first_gain[None, :], second_gain[None, :]
+    gain_one, gain_two = first_gain, second_gain
     normed, queries, keys, values, attended, query_features, key_features, modulation, condition = forward(
         segment_ids, piece_lengths, time_index, hidden, table, gain_one, modulation_weight,
-        modulation_bias[None, :], query_key_value_weight,
+        modulation_bias, query_key_value_weight,
     )
     block_out, input_grad, block_sum, mod_sum, small_sum = backward(
-        segment_ids, piece_lengths, modulation, condition, table, gain_one, gain_two, expand_bias[None, :],
-        reduce_bias[None, :], narrow_weight, widen_weight, attention_output_matrix, attended, cot, queries, keys, values,
+        segment_ids, piece_lengths, modulation, condition, table, gain_one, gain_two, expand_bias,
+        reduce_bias, narrow_weight, widen_weight, attention_output_matrix, attended, cot, queries, keys, values,
         query_features, key_features, normed, hidden, query_key_value_weight,
     )
     dp_size = lax.axis_size("dp")
+    if dp_size == 2**GROUP_BITS:
+        block_out, input_grad, *rest = finish(block_out, input_grad, block_sum, mod_sum, small_sum)
+        return (block_out[None], input_grad[None], *rest)
     expand_block = scatter_rest(block_sum[:192], dp_size).T
     reduce_block = block_sum[192:384].reshape(4, -1, LANES).transpose(1, 0, 2).reshape(-1, 4 * LANES)
     reduce_block = scatter_rest(reduce_block, dp_size).T

time: 163 us -> 146 us (0.90)
  local copies, waits for them, and re-layouts: 15.1 us -> 1.12 us
    pallas_call x1, Pallas kernels: 37.5 us -> 32.4 us  [forward(): pl.pallas_call(forward_kernel, out_shape=(half, both, both, both, half, j...]
    slice x6 -> x0, local copies, waits for them, and re-layouts: 4.42 us -> none  [the longest x1 1.8 us: local(): block_sum[192:384].reshape(4, -1, LANES).transpose(1, 0, 2)]
    broadcast_in_dim x4 -> x0, local copies, waits for them, and re-layouts: 3.77 us -> none  [the longest x2 1.85 us: local(): gain_one, gain_two = (first_gain[None, :], second_gain[None, :])]
    pallas_call x0 -> x1, Pallas kernels: none -> 3.34 us  [finish(): pl.pallas_call(finish_kernel, out_shape=(jax.ShapeDtypeStruct(block_out.s...]
    transpose x2 -> x0, local copies, waits for them, and re-layouts: 3.15 us -> none  [the longest x1 1.63 us: local(): triple_block = scatter_rest(block_sum[432:576], dp_size).T]
    reshape x3 -> x0, local copies, waits for them, and re-layouts: 1.96 us -> none  [the longest x1 0.73 us: local(): block_sum[192:384].reshape(4, -1, LANES).transpose(1, 0, 2)]
    unnamed x14 -> x0, local copies, waits for them, and re-layouts: 1.78 us -> none
where the time goes in v6:
time: 146 us; the launch traced here: 143 us
  Pallas kernels  142 us (97%)
    pallas_call x1, Pallas kernels, backward(): pl.pallas_call(functools.partial(backward_kernel, extra_bits, all_bits),...  106 us
    pallas_call x1, Pallas kernels, forward(): pl.pallas_call(forward_kernel, out_shape=(half, both, both, both, half, j...  32.4 us
    pallas_call x1, Pallas kernels, finish(): pl.pallas_call(finish_kernel, out_shape=(jax.ShapeDtypeStruct(block_out.s...  3.34 us

profile of v6, /device:TPU:0, one launch (start us, length us, event | category | flops | bytes accessed | tf_op | source)
XLA Modules:
  0.0 143.4 jit_solution(907115593714545265)
XLA Ops:
  0.6 32.4 %shard_map.255 = (bf16[512,768]{1,0:T(8,128)(2,1)}, bf16[2,512,768]{2,1,0:T(8,128)(2,1)}, bf16[2,512,768]{2,1,0:T(8,128)(2,1)}, bf16[2,512,768]{2,1,0:T(8,128)(2...) custom-call(s32[1,1024]{1,0:T(1,128)} %segments.3, ...), custom_call_target="tpu_custom_call" | custom-call | tf_op jit(solution)/shard_map/pallas_call | solution.py:241
  33.1 105.9 %shard_map.256 = (bf16[512,768]{1,0:T(8,128)(2,1)}, bf16[512,768]{1,0:T(8,128)(2,1)}, f32[576,384]{1,0:T(8,128)}, f32[128,384]{1,0:T(8,128)}, f32[16,768]{1,0:T(8,128)}) custom-call(s32[1,1024]{1,0:T(1,128)} %segments.3, s32[1,8]{1,0:T(1,128)} %lengths.3, f32[8,4608]{1,0:T(8,128)} %get-tuple-element.40.modulation, f32[8,128]{1,0:T(8,128)} %get-tuple-element.41.condition, ...), custom_call_target="tpu_custom_call" | custom-call | tf_op jit(solution)/shard_map/pallas_call | solution.py:1039
  139.0 3.3 %shard_map.257 = (bf16[512,768]{1,0:T(8,128)(2,1)}, bf16[512,768]{1,0:T(8,128)(2,1)}, f32[768]{0:T(1024)}, f32[64,288]{1,0:T(8,128)}, f32[4608]{0:T(1024)}, /*in...) custom-call(bf16[512,768]{1,0:T(8,128)(2,1)} %get-tuple-element.49.b, ...), custom_call_target="tpu_custom_call" | custom-call | tf_op jit(solution)/shard_map/pallas_call | solution.py:1109
  142.3 1.1 slice_bitcast_fusion

commit v7 on v6

--- a/solution.py
+++ b/solution.py
@@ -268,34 +268,36 @@
 Z2, Z1, Y, CORE, X = 0, 1, 2, 3, 4
 
 
-WIDE_ORDERS = ((Y, X), (X, Y), (X, Y), (X, Y))
-REDUCE_ORDERS = ((Z1, Y, Z2), (Y, Z1, Z2), (Y, Z2, Z1), (Z2, Y, Z1))
-OUTPUT_ORDER = (CORE, X, Y, Z1, Z2)
-TRIPLE_ORDERS = ((CORE, Y, X, Z1, Z2), (CORE, Z1, Y, X, Z2), (CORE, X, Y, Z1, Z2))
+WIDE_ORDERS = ((X, Y), (Y, X), (X, Y), (Y, X))
+REDUCE_ORDERS = ((Z1, Z2, Y), (Z1, Y, Z2), (Y, Z1, Z2), (Z1, Y, Z2))
+OUTPUT_ORDER = (CORE, Z1, Y, X, Z2)
+TRIPLE_ORDERS = ((Y, X, Z1, Z2), (Z1, X, Y, Z2), (X, Y, Z1, Z2))
 PLAN = (
     (("T", 6), (("r", 0), ("w", 0),)),
-    (("T", 7), (("w", 1),)),
-    (("N", 0), (("r", 1),)),
-    (("N", 4), (("w", 2),)),
-    (("D", 0), (("s", 0), ("r", 2),)),
-    (("D", 1), (("r", 0), ("w", 0),)),
-    (("A", 1), (("w", 1), ("o", 0),)),
-    (("A", 3), (("w", 2), ("w", 3),)),
-    (("A", 4), (("r", 3), ("s", 0),)),
-    (("A", 6), (("r", 1),)),
-    (("A", 7), (("w", 3),)),
-    (("A", 9), (("r", 3),)),
-    (("A", 10), (("r", 2),)),
-    (("E", 0), (("r", 0),)),
-    (("B", 0), (("s", 0), ("wm", 0),)),
-    (("B", 3), (("r", 1),)),
-    (("B", 5), (("wm", 1),)),
-    (("C", 0), (("r", 3), ("o", 0),)),
-    (("C", 1), (("s", 0), ("r", 2),)),
-    (("C", 4), (("q", 0),)),
-    (("C", 5), (("q", 1),)),
-    (("C", 6), (("re", 1), ("s", 0),)),
-    (("F", 0), (("q", 2), ("o", 0), ("we", 0), ("re", 0), ("m", 0), ("q", 0), ("q", 1), ("m", 0), ("o", 0), ("q", 2), ("m", 0), ("q", 1), ("o", 0), ("q", 0), ("q", 2), ("q", 1), ("m", 0), ("q", 0), ("q", 2), ("m", 0), ("q", 1), ("q", 0), ("q", 2),)),
+    (("N", 0), (("w", 1), ("r", 1),)),
+    (("D", 1), (("w", 2),)),
+    (("D", 2), (("r", 2),)),
+    (("A", 0), (("s", 0), ("r", 0),)),
+    (("A", 1), (("w", 1), ("w", 0),)),
+    (("A", 2), (("o", 0),)),
+    (("A", 4), (("r", 3),)),
+    (("A", 5), (("w", 3),)),
+    (("A", 6), (("r", 2),)),
+    (("A", 8), (("r", 1), ("wm", 0),)),
+    (("A", 10), (("w", 2),)),
+    (("A", 11), (("s", 0),)),
+    (("E", 0), (("o", 0), ("r", 0),)),
+    (("B", 0), (("r", 3),)),
+    (("B", 2), (("r", 2),)),
+    (("B", 4), (("o", 0), ("w", 3),)),
+    (("B", 5), (("s", 0), ("r", 1),)),
+    (("C", 0), (("o", 0), ("r", 3),)),
+    (("C", 1), (("re", 0),)),
+    (("C", 2), (("wm", 1),)),
+    (("C", 3), (("s", 0),)),
+    (("C", 4), (("re", 1),)),
+    (("C", 5), (("o", 0),)),
+    (("F", 0), (("m", 0), ("we", 0), ("q", 0), ("q", 2), ("s", 0), ("m", 0), ("q", 1), ("q", 0), ("q", 2), ("m", 0), ("q", 0), ("q", 1), ("q", 2), ("q", 1), ("m", 0), ("q", 0), ("q", 2), ("q", 1), ("m", 0),)),
 )
 
 
@@ -388,7 +390,7 @@
     small_acc, small_got, late_acc, late_got, mod_got, mod_two, mod_three, mod_four, mod_five,
     cond_zero, cond_got, cond_one, cond_two, cond_three, cond_four, cond_five,
     load_sem, tile_sem, core_send, core_recv, stream_send, stream_recv, swap_send, swap_recv,
-    small_send, small_recv, late_send, late_recv, mod_send, mod_recv,
+    small_send, small_recv, late_send, late_recv, mod_send, mod_recv, triple_send, triple_recv,
 ):
     tokens, width = input_grad.shape
     tiles = narrow_hbm.shape[0] // TILE
@@ -438,7 +440,7 @@
             todo.append((True, name, stage))
             if name[0] in ("m", "s"):
                 continue
-            if stage + 1 < (len(streams[name].order) if name in streams else 5):
+            if stage + 1 < (len(streams[name].order) if name in streams else 4):
                 todo.append((False, name, stage + 1))
                 continue
             finished.add(name)
@@ -627,24 +629,14 @@
         core_add(tiles - 1)
         begin(3)
         gain_sum = jnp.zeros((1, width), F32)
-        value_sum = jnp.zeros((1, width), F32)
-        mlp_sum = jnp.zeros((1, width), F32)
         for number in range(blocks):
             perform(("N", number))
             rows = pl.ds(number * BLOCK, BLOCK)
             here = pl.ds(number, 1)
-            full = reduced[rows, :] + as_row(reduce_bias)
-            branch = mod_part(number, 5) * full
             before = hidden[rows, :].astype(F32) + mod_part(number, 2) * projected[rows, :]
             centered = before - mean_of(before)
             inverse = lax.rsqrt(mean_of(centered * centered) + 1e-05)
             normal = centered * inverse
-            value = before + branch
-            block_out[rows, :] = value.astype(BF16)
-            value_sum = value_sum + jnp.sum(keep[number] * value * value, axis=0, keepdims=True)
-            mlp_sum = mlp_sum + jnp.sum(keep[number] * branch * branch, axis=0, keepdims=True)
-            grad_out = cotangent[rows, :].astype(F32) * keep[number]
-            mod_rows[here, pl.ds(5 * width, width)] = jnp.sum(grad_out * full, axis=0, keepdims=True)
             grad = grad_normed[rows, :]
             line = normal * as_row(second_gain)
             mod_rows[here, pl.ds(3 * width, width)] = jnp.sum(grad, axis=0, keepdims=True)
@@ -654,25 +646,10 @@
             grad_normal = grad_line * as_row(second_gain)
             along = mean_of(grad_normal * normal)
             term = (grad_normal - mean_of(grad_normal) - normal * along) * inverse
-            total = grad_out + term
+            total = cotangent[rows, :].astype(F32) * keep[number] + term
             grad_middle[rows, :] = total
-            mod_rows[here, pl.ds(2 * width, width)] = jnp.sum(total * projected[rows, :], axis=0, keepdims=True)
             grad_low[rows, :] = (mod_part(number, 2) * total).astype(BF16)
         small_acc[0, pl.ds(SECOND_GAIN, 1), :] = gain_sum
-        lane = lane_iota((1, width))
-        counts = jnp.zeros((1, 1), F32)
-        for number in range(blocks):
-            counts = counts + jnp.sum(keep[number], axis=0, keepdims=True)
-        terms = [jnp.sum(term, axis=1, keepdims=True) for term in (value_sum, branch_sum, mlp_sum)] + [counts]
-        stats = jnp.zeros((1, width), F32)
-        for place, term in enumerate(terms):
-            stats = jnp.where(lane == place, term, stats)
-        small_acc[0, pl.ds(STATS, 1), :] = stats
-        for part in range(2, 6):
-            small_acc[0, pl.ds(MOD_BIAS + part, 1), :] = jnp.sum(
-                mod_rows[:, pl.ds(part * width, width)], axis=0, keepdims=True
-            )
-        small_copy(0).start()
         perform(("N", blocks))
 
         for first in range(0, width, 256):
@@ -692,6 +669,37 @@
         for place in range(HEADS // 2 + 2):
             swap(place).start()
         perform(("D", 0))
+        value_sum = jnp.zeros((1, width), F32)
+        mlp_sum = jnp.zeros((1, width), F32)
+        for number in range(blocks):
+            rows = pl.ds(number * BLOCK, BLOCK)
+            here = pl.ds(number, 1)
+            full = reduced[rows, :] + as_row(reduce_bias)
+            branch = mod_part(number, 5) * full
+            value = hidden[rows, :].astype(F32) + mod_part(number, 2) * projected[rows, :] + branch
+            block_out[rows, :] = value.astype(BF16)
+            value_sum = value_sum + jnp.sum(keep[number] * value * value, axis=0, keepdims=True)
+            mlp_sum = mlp_sum + jnp.sum(keep[number] * branch * branch, axis=0, keepdims=True)
+            grad_out = cotangent[rows, :].astype(F32) * keep[number]
+            mod_rows[here, pl.ds(5 * width, width)] = jnp.sum(grad_out * full, axis=0, keepdims=True)
+            mod_rows[here, pl.ds(2 * width, width)] = jnp.sum(
+                grad_middle[rows, :] * projected[rows, :], axis=0, keepdims=True
+            )
+        lane = lane_iota((1, width))
+        counts = jnp.zeros((1, 1), F32)
+        for number in range(blocks):
+            counts = counts + jnp.sum(keep[number], axis=0, keepdims=True)
+        terms = [jnp.sum(term, axis=1, keepdims=True) for term in (value_sum, branch_sum, mlp_sum)] + [counts]
+        stats = jnp.zeros((1, width), F32)
+        for place, term in enumerate(terms):
+            stats = jnp.where(lane == place, term, stats)
+        small_acc[0, pl.ds(STATS, 1), :] = stats
+        for part in range(2, 6):
+            small_acc[0, pl.ds(MOD_BIAS + part, 1), :] = jnp.sum(
+                mod_rows[:, pl.ds(part * width, width)], axis=0, keepdims=True
+            )
+        small_copy(0).start()
+        perform(("D", 1))
         for first in range(0, width, TILE):
             output_t = dot_tn(grad_low[:, pl.ds(first, TILE)], attended[...]).astype(BF16)
             for place in range(TILE // 48):
@@ -702,7 +710,7 @@
                         place * 48 : place * 48 + 48, side * LANES : side * LANES + LANES
                     ]
         streams["o", 0].send(0)
-        perform(("D", 1))
+        perform(("D", 2))
 
     def small_copy(number):
         return pltpu.make_async_remote_copy(
@@ -803,7 +811,25 @@
                         place * 48 : place * 48 + 48, side * LANES : side * LANES + LANES
                     ]
 
+        def triple_core(number):
+            index = ((0, 0), (0, 1), (1,))[number]
+            full = (slice(None),) * (3 - len(index))
+            return pltpu.make_async_remote_copy(
+                triple_part.at[index + full + (1 - core,)], tri_a.at[index],
+                triple_send.at[number], triple_recv.at[number],
+                device_id=exchange_partner(CORE, extra_bits), device_id_type=MESH_ID,
+            )
+
+        def triple_add(number):
+            triple_core(number).wait_recv()
+            for z1 in (number,) if number < 2 else range(2):
+                for y in range(2):
+                    for side in range(2):
+                        got = (number // 2, z1, y)
+                        triple_part[got + (core, side)] = triple_part[got + (core, side)] + tri_a[got + (side,)]
+
         third(0)
+        triple_core(0).start()
         grad_normed[...] = dot_nt(grad_triple[:, pl.ds(0, width)], weight[:, pl.ds(0, width)])
         perform(("E", 0))
         for place in range(2):
@@ -849,22 +875,27 @@
                 grad_triple[rows, pl.ds(width + pair * 128, 128)] = turn(grad_key[rows, lanes], *turns[number]).astype(BF16)
             grad_triple[rows, pl.ds(2 * width, width)] = grad_value[rows, :].astype(BF16)
         third(1)
+        triple_core(1).start()
+        triple_add(0)
         third(2)
+        triple_core(2).start()
+        triple_add(1)
         triple = [
             Stream(
-                kit, 14 + number, triple_part, 48 * number, 48, {}, order, (tri_a, tri_b, tri_c, tri_d, tri_e),
+                kit, 14 + number, triple_part, 48 * number, 48, {CORE: core}, order, (tri_b, tri_c, tri_d, tri_e),
                 48 * number, 432 + 48 * number,
             )
             for number, order in enumerate(TRIPLE_ORDERS)
         ]
-        for number, stream in enumerate(triple):
-            streams["q", number] = stream
-            stream.send(0)
         perform(("C", 0))
         for part in range(1, 3):
             lanes = pl.ds(part * width, width)
             grad_normed[...] += dot_nt(grad_triple[:, lanes], weight[:, lanes])
             perform(("C", part))
+        triple_add(2)
+        for number, stream in enumerate(triple):
+            streams["q", number] = stream
+            stream.send(0)
 
         gain_sum = jnp.zeros((1, width), F32)
         for number in range(blocks):
@@ -987,6 +1018,8 @@
         small_out[pl.ds(MOD_BIAS, 2), :] = late_acc[len(greet), pl.ds(1, 2), :]
         for stream in triple:
             stream.done()
+        for number in range(3):
+            triple_core(number).wait_send()
         for number in range(5):
             for copy in mod_copies(number):
                 copy.wait_send()
@@ -1058,7 +1091,7 @@
         + mods
         + conds
         + [dma((12,)), dma((2, tiles)), dma((2, tiles)), dma((2, tiles)), dma((17, 5)), dma((17, 5)), dma((8,)), dma((8,))]
-        + [dma((steps,)), dma((steps,)), dma((steps,)), dma((steps,)), dma((2, 5)), dma((2, 5))],
+        + [dma((steps,)), dma((steps,)), dma((steps,)), dma((steps,)), dma((2, 5)), dma((2, 5)), dma((3,)), dma((3,))],
         compiler_params=pltpu.CompilerParams(
             collective_id=2, has_side_effects=True, vmem_limit_bytes=63 << 20
         ),
@@ -1096,7 +1129,7 @@
         for part in range(target.shape[0] // width):
             target[pl.ds(part * width, width)] = small[first + part, :]
     count = jnp.sum(jnp.where(lane_iota((1, width)) == 3, small[pl.ds(STATS, 1), :], 0.0))
-    masked_rms[...] = jnp.sqrt(small[pl.ds(STATS, 1), pl.ds(0, 128)] / (count * width))
+    masked_rms[...] = jnp.sqrt(small[STATS, pl.ds(0, 128)] / (count * width))[:3]
 
 
 def finish(block_out, input_grad, sums, mod_sum, small):
@@ -1104,7 +1137,7 @@
     vmem = pl.BlockSpec(memory_space=pltpu.VMEM)
     shapes = (
         (width,), (mod_sum.shape[0] // 2, 6 * width // 16), (6 * width,), (144, LANES), (48, LANES), (width,), (192, LANES),
-        (4 * width,), (48, 4 * LANES), (width,), (1, 128),
+        (4 * width,), (48, 4 * LANES), (width,), (3,),
     )
     block_out, input_grad, *rest = pl.pallas_call(
         finish_kernel,
@@ -1118,7 +1151,7 @@
     )(block_out, input_grad, sums, mod_sum, small)
     for place in (3, 4, 6, 8):
         rest[place] = rest[place].T
-    return (block_out, input_grad, *rest[:-1], rest[-1][0, :3])
+    return (block_out, input_grad, *rest)
 
 
 def local(

time: 146 us -> 139 us (0.952); the launches traced: 143 us -> 139 us
  Pallas kernels: 142 us -> 139 us
    pallas_call x1, Pallas kernels: 106 us -> 103 us  [backward(): pl.pallas_call(functools.partial(backward_kernel, extra_bits, all_bits),...]
where the time goes in v7:
time: 139 us
  Pallas kernels  139 us (100%)
    pallas_call x1, Pallas kernels, backward(): pl.pallas_call(functools.partial(backward_kernel, extra_bits, all_bits),...  103 us
    pallas_call x1, Pallas kernels, forward(): pl.pallas_call(forward_kernel, out_shape=(half, both, both, both, half, j...  32.3 us
    pallas_call x1, Pallas kernels, finish(): pl.pallas_call(finish_kernel, out_shape=(jax.ShapeDtypeStruct(block_out.s...  3.34 us

profile of v7, /device:TPU:0, one launch (start us, length us, event | category | flops | bytes accessed | tf_op | source)
XLA Modules:
  0.0 139.3 jit_solution(7196776239547979387)
XLA Ops:
  0.6 32.3 %shard_map.255 = (bf16[512,768]{1,0:T(8,128)(2,1)}, bf16[2,512,768]{2,1,0:T(8,128)(2,1)}, bf16[2,512,768]{2,1,0:T(8,128)(2,1)}, bf16[2,512,768]{2,1,0:T(8,128)(2...) custom-call(s32[1,1024]{1,0:T(1,128)} %segments.3, ...), custom_call_target="tpu_custom_call" | custom-call | tf_op jit(solution)/shard_map/pallas_call | solution.py:241
  32.9 103.0 %shard_map.256 = (bf16[512,768]{1,0:T(8,128)(2,1)}, bf16[512,768]{1,0:T(8,128)(2,1)}, f32[576,384]{1,0:T(8,128)}, f32[128,384]{1,0:T(8,128)}, f32[16,768]{1,0:T(8,128)}) custom-call(s32[1,1024]{1,0:T(1,128)} %segments.3, s32[1,8]{1,0:T(1,128)} %lengths.3, f32[8,4608]{1,0:T(8,128)} %get-tuple-element.40.modulation, f32[8,128]{1,0:T(8,128)} %get-tuple-element.41.condition, ...), custom_call_target="tpu_custom_call" | custom-call | tf_op jit(solution)/shard_map/pallas_call | solution.py:1072
  136.0 3.3 %shard_map.257 = (bf16[512,768]{1,0:T(8,128)(2,1)}, bf16[512,768]{1,0:T(8,128)(2,1)}, f32[768]{0:T(1024)}, f32[64,288]{1,0:T(8,128)}, f32[4608]{0:T(1024)}, /*in...) custom-call(bf16[512,768]{1,0:T(8,128)(2,1)} %get-tuple-element.49.b, ...), custom_call_target="tpu_custom_call" | custom-call | tf_op jit(solution)/shard_map/pallas_call | solution.py:1142

commit v8 on v7

--- a/solution.py
+++ b/solution.py
@@ -103,14 +103,20 @@
 
 
 def forward_kernel(
-    segments, lengths, times, hidden, table, first_gain, mod_weight, mod_bias, weight,
-    normed, queries, keys, values, attended, query_features, key_features, modulation, condition,
-    other_hidden, turned_values, out_t, peak, total, send_sem, recv_sem,
+    segments, lengths, times, hidden, table, first_gain, mod_weight_hbm, mod_bias, weight_hbm,
+    normed_hbm, queries_hbm, keys_hbm, values_hbm, attended, query_features, key_features, modulation, condition,
+    mod_weight, weight, normed, queries, keys, values,
+    other_hidden, turned_values, out_t, peak, total, send_sem, recv_sem, load_sem, store_sem,
 ):
     tokens, width = hidden.shape
     blocks = tokens // BLOCK
     seq = lax.axis_index("seq")
     partner = (lax.axis_index("dp"), 1 - seq)
+    mod_load = pltpu.make_async_copy(mod_weight_hbm, mod_weight, load_sem.at[0])
+    weight_load = pltpu.make_async_copy(weight_hbm, weight, load_sem.at[1])
+    mod_load.start()
+    weight_load.start()
+    stores = []
     barrier = pltpu.get_barrier_semaphore()
     pl.semaphore_signal(barrier, inc=1, device_id=partner, device_id_type=MESH_ID)
     pl.semaphore_wait(barrier, 1)
@@ -136,6 +142,7 @@
         sine = sin_high * cos_low + cos_high * sin_low
         row = jnp.where(lane_iota(cosine.shape) < 64, cosine, sine)
         condition[pl.ds(number, 1), :] = row.astype(BF16).astype(F32)
+    mod_load.wait()
     modulation[...] = dot(condition[...].astype(BF16), mod_weight[...]) + as_row(mod_bias)
 
     lane = lane_iota((BLOCK, 128))
@@ -171,6 +178,10 @@
             else:
                 other_hidden[rows, :] = result
         normed_source = normed if part == 0 else other_hidden
+        if section == 0:
+            weight_load.wait()
+            stores.append(pltpu.make_async_copy(normed, normed_hbm, store_sem.at[3, 0]))
+            stores[-1].start()
         for tile in range(3 * width // LANES):
             which, first = divmod(tile * LANES, width)
             product = dot(normed_source[section_rows, :], weight[:, pl.ds(tile * LANES, LANES)])
@@ -185,6 +196,12 @@
                         piece = piece.astype(BF16).astype(F32) * 0.125
                     rows = pl.ds((first_block + place) * BLOCK, BLOCK)
                     target[part, rows, pl.ds(first + pair * 128, 128)] = piece.astype(BF16)
+        for place, (source, target) in enumerate(((queries, queries_hbm), (keys, keys_hbm), (values, values_hbm))):
+            copy = pltpu.make_async_copy(
+                source.at[part, section_rows], target.at[part, section_rows], store_sem.at[place, section]
+            )
+            copy.start()
+            stores.append(copy)
         turned_rows = pl.ds(0, count * BLOCK)
         turned_values[:, turned_rows] = jnp.transpose(values[part, section_rows, :])
 
@@ -228,6 +245,8 @@
         + [jnp.zeros((128 - 3 * HEADS, tokens), F32)], axis=0,
     )
     query_features[...] = query_features[...] + split_three(jnp.transpose(log_rows))
+    for copy in stores:
+        copy.wait()
     for exchange in exchanges:
         exchange.wait_send()
 
@@ -238,6 +257,7 @@
     half = jax.ShapeDtypeStruct((tokens, width), BF16)
     both = jax.ShapeDtypeStruct((2, tokens, width), BF16)
     smem, vmem = pl.BlockSpec(memory_space=pltpu.SMEM), pl.BlockSpec(memory_space=pltpu.VMEM)
+    hbm = pl.BlockSpec(memory_space=pl.ANY)
     return pl.pallas_call(
         forward_kernel,
         out_shape=(
@@ -247,9 +267,15 @@
             jax.ShapeDtypeStruct((blocks, 6 * width), F32),
             jax.ShapeDtypeStruct((blocks, 128), F32),
         ),
-        in_specs=[smem] * 3 + [vmem] * 6,
-        out_specs=(vmem,) * 9,
+        in_specs=[smem] * 3 + [vmem] * 3 + [hbm, vmem, hbm],
+        out_specs=(hbm,) * 4 + (vmem,) * 5,
         scratch_shapes=[
+            pltpu.VMEM(mod_weight.shape, BF16),
+            pltpu.VMEM(weight.shape, BF16),
+            pltpu.VMEM((tokens, width), BF16),
+            pltpu.VMEM((2, tokens, width), BF16),
+            pltpu.VMEM((2, tokens, width), BF16),
+            pltpu.VMEM((2, tokens, width), BF16),
             pltpu.VMEM((tokens, width), BF16),
             pltpu.VMEM((width, tokens), BF16),
             pltpu.VMEM((width, tokens), F32),
@@ -257,6 +283,8 @@
             pltpu.VMEM((16, tokens), F32),
             pltpu.SemaphoreType.DMA((2,)),
             pltpu.SemaphoreType.DMA((2,)),
+            pltpu.SemaphoreType.DMA((2,)),
+            pltpu.SemaphoreType.DMA((4, 3)),
         ],
         compiler_params=pltpu.CompilerParams(
             collective_id=1, has_side_effects=True, vmem_limit_bytes=56 << 20

time: 139 us -> 136 us (0.978)
  Pallas kernels: 139 us -> 136 us
    pallas_call x1, Pallas kernels: 32.3 us -> 29.3 us  [forward(): pl.pallas_call(forward_kernel, out_shape=(half, both, both, both, half, j...]
where the time goes in v8:
time: 136 us
  Pallas kernels  136 us (100%)
    pallas_call x1, Pallas kernels, backward(): pl.pallas_call(functools.partial(backward_kernel, extra_bits, all_bits),...  103 us
    pallas_call x1, Pallas kernels, forward(): pl.pallas_call(forward_kernel, out_shape=(half, both, both, both, half, j...  29.3 us
    pallas_call x1, Pallas kernels, finish(): pl.pallas_call(finish_kernel, out_shape=(jax.ShapeDtypeStruct(block_out.s...  3.34 us

profile of v8, /device:TPU:0, one launch (start us, length us, event | category | flops | bytes accessed | tf_op | source)
XLA Modules:
  0.0 136.3 jit_solution(644422259638801329)
XLA Ops:
  0.6 29.3 %shard_map.255 = (bf16[512,768]{1,0:T(8,128)(2,1)}, bf16[2,512,768]{2,1,0:T(8,128)(2,1)}, bf16[2,512,768]{2,1,0:T(8,128)(2,1)}, bf16[2,512,768]{2,1,0:T(8,128)(2...) custom-call(s32[1,1024]{1,0:T(1,128)} %segments.3, ...), custom_call_target="tpu_custom_call" | custom-call | tf_op jit(solution)/shard_map/pallas_call | solution.py:261
  29.9 103.0 %shard_map.256 = (bf16[512,768]{1,0:T(8,128)(2,1)}, bf16[512,768]{1,0:T(8,128)(2,1)}, f32[576,384]{1,0:T(8,128)}, f32[128,384]{1,0:T(8,128)}, f32[16,768]{1,0:T(8,128)}) custom-call(s32[1,1024]{1,0:T(1,128)} %segments.3, s32[1,8]{1,0:T(1,128)} %lengths.3, f32[8,4608]{1,0:T(8,128)} %get-tuple-element.40.modulation, f32[8,128]{1,0:T(8,128)} %get-tuple-element.41.condition, ...), custom_call_target="tpu_custom_call" | custom-call | tf_op jit(solution)/shard_map/pallas_call | solution.py:1100
  132.9 3.3 %shard_map.257 = (bf16[512,768]{1,0:T(8,128)(2,1)}, bf16[512,768]{1,0:T(8,128)(2,1)}, f32[768]{0:T(1024)}, f32[64,288]{1,0:T(8,128)}, f32[4608]{0:T(1024)}, /*in...) custom-call(bf16[512,768]{1,0:T(8,128)(2,1)} %get-tuple-element.49.b, ...), custom_call_target="tpu_custom_call" | custom-call | tf_op jit(solution)/shard_map/pallas_call | solution.py:1170
